TPU v7x, 256 devices: a whole 4x4x8 slice. The times are simulated.
256 devices in a mesh: seq: 16 (over y, x), chan: 16 (over z, core).
Axes of the slice: x: 4, y: 4, z: 8, core: 2. Of those that a mesh axis runs over, the one named last changes fastest.
Arguments:
- tokens: bfloat16 [57344, 2048], P('seq', 'chan'), may hold values from -6 to 6
- w_query: bfloat16 [2048, 256], replicated, may hold values from -0.125 to 0.125
- w_key: bfloat16 [2048, 256], replicated, may hold values from -0.125 to 0.125
- w_value: bfloat16 [2048, 2048], P(None, 'chan'), may hold values from -0.125 to 0.125
- w_out: bfloat16 [2048, 2048], replicated, may hold values from -0.125 to 0.125
- gain: float32 [2048], replicated, may hold values from 0.1 to 1.9
Outputs:
- mixed: bfloat16 [57344, 2048], P('seq', 'chan')
All inputs are finite; a program needn't handle non-finite values.
Results may differ from a plain program's by a relative error of at most 0.019.
Values may be sent and summed in bfloat16 or wider, within the bound.
A program may use at most 128 MiB of HBM per device.

v0:
```python
import jax
import jax.numpy as jnp
from jax import lax
from jax.sharding import PartitionSpec as P

HEADS = 16
FEAT = 16
HEAD_DIM = 128
BLOCK = 896


def feature_parts(rows):
    linear = rows * FEAT ** (-0.25)
    square = (rows[..., :, None] * rows[..., None, :]).reshape(rows.shape[:-1] + (FEAT * FEAT,)) * (
        2.0 * FEAT
    ) ** (-0.5)
    return (linear, square)


def per_device(tokens, w_query, w_key, w_value, w_out, gain):
    highest = lax.Precision.HIGHEST
    groups = lax.axis_size("chan")
    per_group = HEADS // groups
    my_group = lax.axis_index("chan")
    my_slab = lax.axis_index("seq")
    tok_rows = tokens.shape[0]
    query_cols = per_group * FEAT
    value_cols = per_group * HEAD_DIM
    query_mine = lax.dynamic_slice_in_dim(w_query, my_group * query_cols, query_cols, 1)
    key_mine = lax.dynamic_slice_in_dim(w_key, my_group * query_cols, query_cols, 1)
    initial = (
        jnp.zeros((tok_rows, query_cols), jnp.float32),
        jnp.zeros((tok_rows, query_cols), jnp.float32),
        jnp.zeros((tok_rows, value_cols), jnp.float32),
    )
    piece = lax.all_gather(tokens, "chan", axis=1, tiled=True)
    query_sum, key_sum, value_sum = tuple(
        (
            jnp.dot(piece, weight, preferred_element_type=jnp.float32)
            for weight in (query_mine, key_mine, w_value)
        )
    )
    query_rows = query_sum.astype(jnp.bfloat16)
    key_rows = key_sum.astype(jnp.bfloat16)
    value_rows = value_sum.astype(jnp.bfloat16)
    blocks = tok_rows // BLOCK
    query_blocks = query_rows.reshape(blocks, BLOCK, per_group, FEAT)
    key_blocks = key_rows.reshape(blocks, BLOCK, per_group, FEAT)
    value_blocks = value_rows.reshape(blocks, BLOCK, per_group, HEAD_DIM)
    value_f32 = value_blocks.astype(jnp.float32)
    key_linear, key_square = feature_parts(key_blocks.astype(jnp.float32))
    own_zero = jnp.sum(value_f32, axis=1)
    own_one = jnp.einsum("bthf,bthe->bhfe", key_linear, value_f32, precision=highest)
    own_two = jnp.einsum("bthf,bthe->bhfe", key_square, value_f32, precision=highest)
    own = (own_zero, own_one, own_two)
    slab_total = tuple((jnp.sum(member, axis=0) for member in own))
    initial = tuple((jnp.zeros_like(member) for member in slab_total))
    pieces = (
        lax.all_gather(slab_total[0][None].astype(jnp.bfloat16), "seq", axis=0, tiled=True).astype(
            jnp.float32
        ),
        lax.all_gather(slab_total[1][None].astype(jnp.bfloat16), "seq", axis=0, tiled=True).astype(
            jnp.float32
        ),
        lax.all_gather(slab_total[2][None].astype(jnp.bfloat16), "seq", axis=0, tiled=True).astype(
            jnp.float32
        ),
    )
    count = pieces[0].shape[0]
    order = jnp.arange(count, dtype=jnp.int32)
    earlier_mask = order < my_slab
    prefix = tuple(
        (
            total
            + jnp.sum(
                jnp.where(earlier_mask.reshape((count,) + (1,) * (piece.ndim - 1)), piece, 0.0),
                axis=0,
            )
            for total, piece in zip(initial, pieces)
        )
    )
    earlier = tuple(
        (
            jnp.concatenate([jnp.zeros_like(member[:1]), jnp.cumsum(member, axis=0)[:-1]], axis=0)
            + base[None]
            for member, base in zip(own, prefix)
        )
    )
    query_linear, query_square = feature_parts(query_blocks.astype(jnp.float32))
    inter = earlier[0][:, None] + jnp.einsum(
        "bthf,bhfe->bthe", query_linear, earlier[1], precision=highest
    )
    inter = inter + jnp.einsum("bthf,bhfe->bthe", query_square, earlier[2], precision=highest)
    scores = jnp.einsum(
        "bthf,bshf->bhts", query_blocks, key_blocks, preferred_element_type=jnp.float32
    ) * FEAT ** (-0.5)
    kernel = 1.0 + scores + 0.5 * scores * scores
    causal = jnp.arange(BLOCK)[:, None] >= jnp.arange(BLOCK)[None, :]
    weights = jnp.where(causal, kernel, 0.0).astype(jnp.bfloat16)
    intra = jnp.einsum("bhts,bshe->bthe", weights, value_blocks, preferred_element_type=jnp.float32)
    numerator = (intra + inter).reshape(tok_rows, per_group, HEAD_DIM)
    gain_mine = lax.dynamic_slice_in_dim(gain, my_group * value_cols, value_cols, 0).reshape(
        per_group, HEAD_DIM
    )
    mean_square = jnp.mean(numerator * numerator, axis=-1, keepdims=True)
    hidden = (
        (numerator * lax.rsqrt(mean_square + 1e-05) * gain_mine)
        .astype(jnp.bfloat16)
        .reshape(tok_rows, value_cols)
    )
    out_mine = lax.dynamic_slice_in_dim(w_out, my_group * value_cols, value_cols, 0)
    partial_value = jnp.dot(hidden, out_mine, preferred_element_type=jnp.float32)
    partial_value = lax.optimization_barrier(partial_value.astype(jnp.bfloat16)).astype(jnp.float32)
    mixed = lax.psum_scatter(
        partial_value.astype(jnp.bfloat16), "chan", scatter_dimension=1, tiled=True
    )
    return mixed


def solution(mesh):
    return jax.shard_map(
        per_device,
        mesh=mesh,
        in_specs=(P("seq", "chan"), P(), P(), P(None, "chan"), P(), P()),
        out_specs=P("seq", "chan"),
        check_vma=False,
    )
```

profile of v0, /device:TPU:1, one launch (start us, length us, event | category | flops | bytes accessed | tf_op | source)
XLA Modules:
  0.0 357.3 jit_solution(1797674125439511556)
XLA Ops:
  6.5 0.0 copy-start
  6.5 0.0 all-gather.7.cloned.1.call-start
  6.5 0.7 all-gather.7.cloned.1.call-update
  7.3 0.0 all-gather.9.cloned.1.call-start
  7.3 0.8 dynamic_slice.14
  8.1 0.2 iota_compare_fusion
  8.3 98.0 %all-gather.7.cloned.1.call-done = bf16[3584,2048]{1,0:T(8,128)(2,1)} async-done(((bf16[3584,128]{1,0:T(8,128)(2,1)}), bf16[3584,2048]{1,0:T(8,128)(2,1)}) %all-gather.7.cloned.1.call-update) | async-done | bytes 14680080 | tf_op jit(solution)/shard_map/all_gather | solution.py:36
  106.3 9.2 %fusion.51 = (bf16[128]{0:T(256)(128)(2,1)S(1)}, bf16[3584,128]{1,0:T(8,128)(2,1)S(1)}) fusion(bf16[3584,2048]{1,0:T(8,128)(2,1)} %all-gather.7.cloned.1.call-done, bf16[2048,128]{1,0:T(8,128)(2,1)} %param.9), kind=kOutput, calls=%fused_computation.68 | convolution fusion | flops 1879965568 | bytes 16122112 | tf_op jit(solution)/shard_map/dot_general | solution.py:39
  115.5 0.1 convert_reduce_fusion
  115.7 0.0 copy-done
  115.7 9.4 %convolution_convert_fusion.2 = bf16[16,3584]{1,0:T(8,128)(2,1)S(1)} fusion(bf16[3584,2048]{1,0:T(8,128)(2,1)} %all-gather.7.cloned.1.call-done, bf16[2048,256]{1,0:T(8,128)(2,1)S(1)} %copy-done, s32[]{:T(128)S(6)} %select_n.25), kind=kOutput, calls=%fused_computation.3 | convolution fusion | flops 234938368 | bytes 15319044 | tf_op jit(solution)/shard_map/dot_general | solution.py:39
  125.1 0.5 fusion.50
  125.7 16.0 %all-gather.3 = bf16[16,1,128]{2,1,0:T(2,128)(2,1)S(1)} all-gather(bf16[1,1,128]{2,1,0:T(2,128)(2,1)S(1)} %bitcast.100), channel_id=2, replica_groups=mesh['seq'=16,'chan'=16] {'seq'}, dimensions={0}, use_global_device_ids=true | all-gather | bytes 4352 | tf_op jit(solution)/shard_map/all_gather | solution.py:59
  141.6 0.1 fusion.32
  141.7 0.0 copy-start.3
  141.7 16.8 %all-gather.1 = bf16[256,128]{1,0:T(8,128)(2,1)S(1)} all-gather(bf16[16,128]{1,0:T(8,128)(2,1)S(1)} %get-tuple-element.7), channel_id=3, replica_groups=mesh['seq'=16,'chan'=16] {'seq'}, dimensions={0}, use_global_device_ids=true | all-gather | bytes 69632 | tf_op jit(solution)/shard_map/all_gather | solution.py:62
  158.5 0.4 multiply_multiply_fusion.1
  158.9 2.5 fusion.49
  161.4 0.0 copy-done.3
  161.4 0.0 all-gather.9.cloned.1.call-update
  161.4 0.0 reduce-scatter.4.cloned.1.call-start
  161.4 0.4 fusion.8
  161.8 0.0 copy-start.2
  161.9 0.1 fusion.20
  162.0 0.1 fusion.37
  162.1 0.0 slice-start.1
  162.1 9.6 %convolution_convert_fusion.3 = bf16[16,3584]{1,0:T(8,128)(2,1)S(1)} fusion(bf16[3584,2048]{1,0:T(8,128)(2,1)} %all-gather.7.cloned.1.call-done, bf16[2048,256]{1,0:T(8,128)(2,1)} %param.7, s32[]{:T(128)S(6)} %select_n.25), kind=kOutput, calls=%fused_computation.4 | convolution fusion | flops 234938368 | bytes 15319044 | tf_op jit(solution)/shard_map/dot_general | solution.py:39
  171.7 0.0 copy-done.2
  171.8 0.0 slice-done.1
  171.8 0.0 slice-start
  171.8 2.9 fusion.16
  174.7 2.2 multiply_multiply_fusion
  176.8 36.9 %all-gather.9.cloned.1.call-done = bf16[4096,128]{1,0:T(8,128)(2,1)} async-done(((bf16[256,128]{1,0:T(8,128)(2,1)}), bf16[4096,128]{1,0:T(8,128)(2,1)}) %all-gather.9.cloned.1.call-update) | async-done | bytes 1048592 | tf_op jit(solution)/shard_map/all_gather | solution.py:65
  213.8 1.5 fusion
  215.3 0.0 slice-done
  215.3 5.6 %fusion.6 = f32[4,128,896]{2,1,0:T(8,128)} fusion(f32[4,896,256]{1,2,0:T(8,128)} %bitcast.84, f32[3,1,256,128]{3,2,0,1:T(8,128)S(1)} %slice-done, f32[256,128]{1,0:T(8,128)S(1)} %fusion), kind=kOutput, calls=%fused_computation.20 | convolution fusion | flops 1409417216 | bytes 6029312 | tf_op jit(solution)/shard_map/bthf,bhfe->bthe/dot_general | solution.py:93
  220.9 8.5 %multiply_reduce_fusion = (f32[4,896]{1,0:T(4,128)S(1)}, f32[4,896,1,128]{1,3,0,2:T(8,128)}) fusion(f32[4,128,896]{2,1,0:T(8,128)} %fusion.6, f32[4,128,896]{2,1,0:T(8,128)} %fusion.16, f32[4,128]{1,0:T(4,128)S(1)} %add_bitcast_fusion, bf16[4,896,128]{2,1,0:T(8,128)(2,1)S(1)} %bitcast.88, pred[896,896]{1,0:T(8,128)(4,1)S(1)} %iota_compare_fusion, ...), kind=kOutput, calls=%fused_computation.18 | convolution fusion | flops 949613056 | bytes 7471104 | tf_op jit(solution)/shard_map/bhts,bshe->bthe/dot_general | solution.py:100
  229.4 1.8 copy.41
  231.2 0.5 fusion.3
  231.7 8.3 %convolution_convert_fusion = bf16[3584,2048]{1,0:T(8,128)(2,1)} fusion(bf16[3584,128]{1,0:T(8,128)(2,1)S(1)} %fusion.3, bf16[2048,2048]{1,0:T(8,128)(2,1)} %param.10, s32[]{:T(128)S(6)} %select_n.30), kind=kOutput, calls=%fused_computation | convolution fusion | flops 1886388224 | bytes 16121860 | tf_op jit(solution)/shard_map/dot_general | solution.py:112
  240.0 18.8 %copy.45 = bf16[3584,2048]{0,1:T(8,128)(2,1)} copy(bf16[3584,2048]{1,0:T(8,128)(2,1)} %convolution_convert_fusion) | data formatting | bytes 29360128
  258.8 0.0 reduce-scatter.4.cloned.1.call-update
  258.9 0.0 copy-start.1
  258.9 89.7 %reduce-scatter.4.cloned.1.call-done = bf16[128,3584]{1,0:T(8,128)(2,1)} async-done(((bf16[2048,3584]{1,0:T(8,128)(2,1)}), bf16[128,3584]{1,0:T(8,128)(2,1)}) %reduce-scatter.4.cloned.1.call-update) | async-done | bytes 917520
  348.6 2.2 copy.46
  350.8 0.0 copy-done.1
  (7 shorter events, 0.1 us)
Async XLA Ops:
  6.5 109.1 %copy-start = (bf16[2048,256]{1,0:T(8,128)(2,1)S(1)}, bf16[2048,256]{1,0:T(8,128)(2,1)}, u32[]{:S(2)}) copy-start(bf16[2048,256]{1,0:T(8,128)(2,1)} %param.8) | copy-start | bytes 3145732
  6.5 99.8 %all-gather.7.cloned.1.call-start = ((), (), s32[]{:S(2)}) async-start(), calls=%async_computation.1 | async-start | bytes 15597568 | tf_op jit(solution)/shard_map/all_gather | solution.py:36
  7.3 206.5 %all-gather.9.cloned.1.call-start = ((), (), s32[]{:S(2)}) async-start(), calls=%async_computation.2 | async-start | bytes 1114112 | tf_op jit(solution)/shard_map/all_gather | solution.py:65
  141.7 19.6 %copy-start.3 = (f32[4,1,16,128]{3,2,0,1:T(8,128)}, f32[4,1,16,128]{3,2,0,1:T(8,128)S(1)}, u32[]{:S(2)}) copy-start(f32[4,1,16,128]{3,2,0,1:T(8,128)S(1)} %fusion.32) | copy-start | bytes 98308
  161.4 187.2 %reduce-scatter.4.cloned.1.call-start = ((), (), s32[]{:S(2)}) async-start(), calls=%async_computation.3 | async-start | bytes 15597568
  161.8 9.9 %copy-start.2 = (f32[4,1,256,128]{3,2,0,1:T(8,128)}, f32[4,1,256,128]{3,2,0,1:T(8,128)S(1)}, u32[]{:S(2)}) copy-start(f32[4,1,256,128]{3,2,0,1:T(8,128)S(1)} %fusion.8) | copy-start | bytes 1572868
  162.1 9.6 %slice-start.1 = ((f32[4,1,16,128]{3,2,0,1:T(8,128)}), f32[3,1,16,128]{3,2,0,1:T(8,128)S(1)}, s32[]{:S(2)}) async-start(f32[4,1,16,128]{3,2,0,1:T(8,128)} %copy-done.3), calls=%async_computation.5 | async-start | bytes 49152 | tf_op jit(solution)/shard_map/slice | solution.py:84
  171.8 43.5 %slice-start = ((f32[4,1,256,128]{3,2,0,1:T(8,128)}), f32[3,1,256,128]{3,2,0,1:T(8,128)S(1)}, s32[]{:S(2)}) async-start(f32[4,1,256,128]{3,2,0,1:T(8,128)} %copy-done.2), calls=%async_computation.4 | async-start | bytes 786432 | tf_op jit(solution)/shard_map/slice | solution.py:84
  258.9 91.9 %copy-start.1 = (bf16[2048,256]{1,0:T(8,128)(2,1)S(1)}, bf16[2048,256]{1,0:T(8,128)(2,1)}, u32[]{:S(2)}) copy-start(bf16[2048,256]{1,0:T(8,128)(2,1)} %param.8) | copy-start | bytes 3145732
Sparse Core Ops, SparseCore 0:
  9.1 97.1 all-gather.6
  161.5 52.2 all-gather.8
  259.0 89.5 reduce-scatter.3
where the time goes:
time: 358 us; the launch traced here: 357 us
  waiting for transfers between devices  225 us (63%)
  matrix products  56.5 us (16%)
  blocking collectives  32.8 us (9%)
  local copies, waits for them, and re-layouts  23.6 us (7%)
  between operations  13.3 us (4%)
  other arithmetic  5.75 us (2%)
    all_gather x1, waiting for transfers between devices, per_device(): piece = lax.all_gather(tokens, 'chan', axis=1, tiled=True)  98 us
    unnamed x4, waiting for transfers between devices  90.4 us
    all_gather x1, waiting for transfers between devices, per_device(): lax.all_gather(slab_total[2][None].astype(jnp.bfloat16), 'seq', axis=0, t...  36.9 us
    dot_general x3, matrix products, per_device(): jnp.dot(piece, weight, preferred_element_type=jnp.float32)  28.2 us
    unnamed x10, local copies, waits for them, and re-layouts  21 us
    all_gather x1, blocking collectives, per_device(): lax.all_gather(slab_total[1][None].astype(jnp.bfloat16), 'seq', axis=0, t...  16.8 us
    all_gather x1, blocking collectives, per_device(): lax.all_gather(slab_total[0][None].astype(jnp.bfloat16), 'seq', axis=0, t...  16 us
    dot_general x1, matrix products, per_device(): jnp.einsum('bhts,bshe->bthe', weights, value_blocks, preferred_element_ty...  8.46 us
  transfers between devices with their start and end apart: 3, of which 3 were waited for; matrix products, arithmetic and copies ran while one was open for 5% of the time, Pallas kernels for 0%

commit v1 on v0

v1 whole, which is shorter than its diff:
```python
import jax
import jax.numpy as jnp
from jax import lax
from jax.sharding import PartitionSpec as P

HEADS = 16
FEAT = 16
HEAD_DIM = 128
BLOCK = 896


def feature_parts(rows):
    linear = rows * FEAT ** (-0.25)
    square = (rows[..., :, None] * rows[..., None, :]).reshape(rows.shape[:-1] + (FEAT * FEAT,)) * (
        2.0 * FEAT
    ) ** (-0.5)
    return (linear, square)


def attend(query_rows, key_rows, value_rows, gain_mine, my_slab):
    highest = lax.Precision.HIGHEST
    tok_rows, per_group, _ = value_rows.shape
    blocks = tok_rows // BLOCK
    query_blocks = query_rows.reshape(blocks, BLOCK, per_group, FEAT)
    key_blocks = key_rows.reshape(blocks, BLOCK, per_group, FEAT)
    value_blocks = value_rows.reshape(blocks, BLOCK, per_group, HEAD_DIM)
    value_f32 = value_blocks.astype(jnp.float32)
    key_linear, key_square = feature_parts(key_blocks.astype(jnp.float32))
    own_zero = jnp.sum(value_f32, axis=1)[:, :, None, :]
    own_one = jnp.einsum("bthf,bthe->bhfe", key_linear, value_f32, precision=highest)
    own_two = jnp.einsum("bthf,bthe->bhfe", key_square, value_f32, precision=highest)
    own = jnp.concatenate([own_zero, own_one, own_two], axis=2)
    slab_total = jnp.sum(own, axis=0)
    pieces = lax.all_gather(
        slab_total[None].astype(jnp.bfloat16), "seq", axis=0, tiled=True
    ).astype(jnp.float32)
    count = pieces.shape[0]
    earlier_mask = jnp.arange(count, dtype=jnp.int32) < my_slab
    prefix = jnp.sum(jnp.where(earlier_mask[:, None, None, None], pieces, 0.0), axis=0)
    earlier = jnp.concatenate([jnp.zeros_like(own[:1]), jnp.cumsum(own, axis=0)[:-1]], axis=0) + prefix[None]
    query_linear, query_square = feature_parts(query_blocks.astype(jnp.float32))
    inter = earlier[:, :, 0][:, None] + jnp.einsum(
        "bthf,bhfe->bthe", query_linear, earlier[:, :, 1 : 1 + FEAT], precision=highest
    )
    inter = inter + jnp.einsum(
        "bthf,bhfe->bthe", query_square, earlier[:, :, 1 + FEAT :], precision=highest
    )
    scores = jnp.einsum(
        "bthf,bshf->bhts", query_blocks, key_blocks, preferred_element_type=jnp.float32
    ) * FEAT ** (-0.5)
    kernel = 1.0 + scores + 0.5 * scores * scores
    causal = jnp.arange(BLOCK)[:, None] >= jnp.arange(BLOCK)[None, :]
    weights = jnp.where(causal, kernel, 0.0).astype(jnp.bfloat16)
    intra = jnp.einsum("bhts,bshe->bthe", weights, value_blocks, preferred_element_type=jnp.float32)
    numerator = (intra + inter).reshape(tok_rows, per_group, HEAD_DIM)
    mean_square = jnp.mean(numerator * numerator, axis=-1, keepdims=True)
    hidden = (numerator * lax.rsqrt(mean_square + 1e-05) * gain_mine).astype(jnp.bfloat16)
    return hidden.reshape(tok_rows, per_group * HEAD_DIM)


def per_device(tokens, w_query, w_key, w_value, w_out, gain):
    groups = lax.axis_size("chan")
    per_group = HEADS // groups
    my_group = lax.axis_index("chan")
    my_slab = lax.axis_index("seq")
    value_full = lax.all_gather(w_value, "chan", axis=1, tiled=True)
    rows = lax.all_to_all(tokens, "chan", 0, 1, tiled=True)
    chunk = rows.shape[0]
    weight = jnp.concatenate([w_query, w_key, value_full], axis=1)
    proj = jnp.dot(rows, weight, preferred_element_type=jnp.float32).astype(jnp.bfloat16)
    qk_cols = HEADS * FEAT
    query = proj[:, :qk_cols].reshape(chunk, groups, per_group * FEAT)
    key = proj[:, qk_cols : 2 * qk_cols].reshape(chunk, groups, per_group * FEAT)
    value = proj[:, 2 * qk_cols :].reshape(chunk, groups, per_group * HEAD_DIM)
    packed = jnp.concatenate([query, key, value], axis=2)
    mine = lax.all_to_all(packed, "chan", 1, 0, tiled=True)
    tok_rows = mine.shape[0]
    qf = per_group * FEAT
    query_rows = mine[:, 0, :qf].reshape(tok_rows, per_group, FEAT)
    key_rows = mine[:, 0, qf : 2 * qf].reshape(tok_rows, per_group, FEAT)
    value_rows = mine[:, 0, 2 * qf :].reshape(tok_rows, per_group, HEAD_DIM)
    value_cols = per_group * HEAD_DIM
    gain_mine = lax.dynamic_slice_in_dim(gain, my_group * value_cols, value_cols, 0).reshape(
        per_group, HEAD_DIM
    )
    hidden = attend(query_rows, key_rows, value_rows, gain_mine, my_slab)
    hidden_rows = lax.all_to_all(hidden, "chan", 0, 1, tiled=True)
    mixed_rows = jnp.dot(hidden_rows, w_out, preferred_element_type=jnp.float32).astype(jnp.bfloat16)
    return lax.all_to_all(mixed_rows, "chan", 1, 0, tiled=True)


def solution(mesh):
    return jax.shard_map(
        per_device,
        mesh=mesh,
        in_specs=(P("seq", "chan"), P(), P(), P(None, "chan"), P(), P()),
        out_specs=P("seq", "chan"),
        check_vma=False,
    )
```

time: 358 us -> 283 us (0.79)
  waiting for transfers between devices: 225 us -> 81.7 us
  blocking collectives: 32.8 us -> 144 us
  matrix products: 56.5 us -> 27.2 us
  local copies, waits for them, and re-layouts: 23.6 us -> 8.45 us
    all_to_all x0 -> x4, blocking collectives: none -> 144 us  [the longest x1 41.4 us: per_device(): rows = lax.all_to_all(tokens, 'chan', 0, 1, tiled=True)]
    unnamed x4 -> x2, waiting for transfers between devices: 90.4 us -> 0.73 us
    all_gather x2, waiting for transfers between devices: 135 us -> 81 us  [the longest x1 41.9 us: per_device(): value_full = lax.all_gather(w_value, 'chan', axis=1, tiled=True)]
    all_gather x2 -> x0, blocking collectives: 32.8 us -> none  [the longest x1 16.8 us: per_device(): lax.all_gather(slab_total[1][None].astype(jnp.bfloat16), 'seq', axis=0, t...]
    dot_general x9 -> x7, matrix products: 56.5 us -> 27.2 us  [the longest x1 8.15 us: attend(): jnp.einsum('bhts,bshe->bthe', weights, value_blocks, preferred_element_ty...]
    unnamed x10 -> x3, local copies, waits for them, and re-layouts: 21 us -> 0.93 us
  transfers between devices with their start and end apart: 3 -> 2, of which waited for: 3 -> 2; matrix products, arithmetic and copies ran while one was open for 5% -> 1% of each run, Pallas kernels for 0% -> 0%
where the time goes in v1:
time: 283 us; the launch traced here: 282 us
  blocking collectives  144 us (51%)
  waiting for transfers between devices  81.7 us (29%)
  matrix products  27.2 us (10%)
  between operations  13.6 us (5%)
  local copies, waits for them, and re-layouts  8.45 us (3%)
  other arithmetic  7.13 us (3%)
    all_gather x1, waiting for transfers between devices, per_device(): value_full = lax.all_gather(w_value, 'chan', axis=1, tiled=True)  41.9 us
    all_to_all x1, blocking collectives, per_device(): rows = lax.all_to_all(tokens, 'chan', 0, 1, tiled=True)  41.4 us
    all_to_all x1, blocking collectives, per_device(): mine = lax.all_to_all(packed, 'chan', 1, 0, tiled=True)  39.7 us
    all_gather x1, waiting for transfers between devices, attend(): lax.all_gather(slab_total[None].astype(jnp.bfloat16), 'seq', axis=0, tile...  39.1 us
    all_to_all x1, blocking collectives, per_device(): hidden_rows = lax.all_to_all(hidden, 'chan', 0, 1, tiled=True)  34.7 us
    all_to_all x1, blocking collectives, per_device(): return lax.all_to_all(mixed_rows, 'chan', 1, 0, tiled=True)  28.4 us
    dot_general x1, matrix products, attend(): jnp.einsum('bhts,bshe->bthe', weights, value_blocks, preferred_element_ty...  8.15 us
    dot_general x1, matrix products, per_device(): jnp.dot(rows, weight, preferred_element_type=jnp.float32)  5.98 us
  transfers between devices with their start and end apart: 2, of which 2 were waited for; matrix products, arithmetic and copies ran while one was open for 1% of the time, Pallas kernels for 0%

profile of v1, /device:TPU:1, one launch (start us, length us, event | category | flops | bytes accessed | tf_op | source)
XLA Modules:
  0.0 282.4 jit_solution(14427101673856947613)
XLA Ops:
  6.5 0.0 all-gather.5.cloned.1.call-start
  6.5 0.7 all-gather.5.cloned.1.call-update
  7.3 0.0 all-gather.7.cloned.1.call-start
  7.3 41.4 %all_to_all.72 = bf16[16,224,128]{2,1,0:T(8,128)(2,1)S(1)} all-to-all(bf16[16,224,128]{2,1,0:T(8,128)(2,1)} %bitcast.94), channel_id=1, replica_groups=mesh['seq'=16,'chan'=16] {'chan'}, dimensions={0} | all-to-all | bytes 1835008 | tf_op jit(solution)/shard_map/all_to_all | solution.py:67
  48.7 41.9 %all-gather.5.cloned.1.call-done = bf16[2048,2048]{1,0:T(8,128)(2,1)} async-done(((bf16[2048,128]{1,0:T(8,128)(2,1)}), bf16[2048,2048]{1,0:T(8,128)(2,1)}) %all-gather.5.cloned.1.call-update) | async-done | bytes 8388624 | tf_op jit(solution)/shard_map/all_gather | solution.py:66
  90.5 6.0 %fusion.9 = bf16[224,2560]{1,0:T(8,128)(2,1)S(1)} fusion(bf16[2048,2048]{1,0:T(8,128)(2,1)} %all-gather.5.cloned.1.call-done, bf16[2048,256]{1,0:T(8,128)(2,1)} %param.8, bf16[2048,256]{1,0:T(8,128)(2,1)} %param.7, bf16[16,224,128]{2,1,0:T(8,128)(2,1)S(1)} %all_to_all.72), kind=kOutput, calls=%fused_computation.10 | convolution fusion | flops 2380840960 | bytes 12550144 | tf_op jit(solution)/shard_map/dot_general | solution.py:70
  96.6 0.1 slice.42
  96.7 0.1 copy.34
  96.8 0.1 copy.35
  96.9 0.5 copy.52
  97.4 0.2 pad_maximum_fusion
  97.7 39.7 %all_to_all.73 = bf16[224,16,160]{0,2,1:T(8,128)(2,1)S(1)} all-to-all(bf16[224,16,160]{0,2,1:T(8,128)(2,1)S(1)} %pad_maximum_fusion), channel_id=1, replica_groups=mesh['seq'=16,'chan'=16] {'chan'}, dimensions={1} | all-to-all | bytes 2293760 | tf_op jit(solution)/shard_map/all_to_all | solution.py:76
  137.4 0.7 copy.37
  138.1 2.2 all_to_all.60
  140.3 0.1 slice.43
  140.5 0.8 copy.38
  141.3 0.5 convolution_bitcast_fusion.1
  141.8 0.1 convert_reduce_fusion
  141.9 0.4 multiply_multiply_fusion.1
  142.3 1.8 convolution_bitcast_fusion
  144.1 0.7 fusion.22
  144.8 0.0 all-gather.7.cloned.1.call-update
  144.8 0.8 dynamic_slice.3
  145.6 1.1 iota_compare_fusion
  146.7 0.1 fusion.23
  146.9 2.2 multiply_multiply_fusion
  149.0 39.1 %all-gather.7.cloned.1.call-done = bf16[16,273,128]{2,1,0:T(8,128)(2,1)} async-done(((bf16[1,273,128]{2,1,0:T(8,128)(2,1)}), bf16[16,273,128]{2,1,0:T(8,128)(2,1)}) %all-gather.7.cloned.1.call-update) | async-done | bytes 1118224 | tf_op jit(solution)/shard_map/all_gather | solution.py:34
  188.2 0.0 copy-start
  188.2 1.7 fusion.12
  189.9 1.6 fusion.24
  191.6 0.0 copy-done
  191.6 3.5 %fusion.21 = f32[4,128,896]{2,1,0:T(8,128)} fusion(f32[4,896,256]{1,2,0:T(8,128)S(1)} %bitcast.88, f32[4,1,273,128]{3,2,0,1:T(8,128)S(1)} %pad_add_fusion), kind=kOutput, calls=%fused_computation.35 | convolution fusion | flops 1409286144 | bytes 6029312 | tf_op jit(solution)/shard_map/bthf,bhfe->bthe/dot_general | solution.py:45
  195.1 8.1 %multiply_reduce_fusion = (f32[4,896]{1,0:T(4,128)S(1)}, f32[4,896,1,128]{1,3,0,2:T(8,128)}) fusion(f32[4,128,896]{2,1,0:T(8,128)} %fusion.21, f32[4,128,896]{2,1,0:T(8,128)S(1)} %fusion.24, f32[4,128]{1,0:T(4,128)S(1)} %bitcast.100, bf16[4,896,128]{2,1,0:T(8,128)(2,1)S(1)} %bitcast.86, pred[896,896]{1,0:T(8,128)(4,1)} %iota_compare_fusion, ...), kind=kOutput, calls=%fused_computation.21 | convolution fusion | flops 949613056 | bytes 7471104 | tf_op jit(solution)/shard_map/bhts,bshe->bthe/dot_general | solution.py:54
  203.3 1.8 copy.46
  205.1 0.1 rsqrt.12
  205.2 0.5 multiply_convert_fusion
  205.7 34.7 %all_to_all.74 = bf16[16,224,128]{2,1,0:T(8,128)(2,1)S(1)} all-to-all(bf16[16,224,128]{2,1,0:T(8,128)(2,1)S(1)} %multiply_convert_fusion), channel_id=1, replica_groups=mesh['seq'=16,'chan'=16] {'chan'}, dimensions={0} | all-to-all | bytes 1835008 | tf_op jit(solution)/shard_map/all_to_all | solution.py:87
  240.5 5.6 %fusion.16 = bf16[28,16,8,128]{3,2,1,0:T(8,128)(2,1)S(1)} fusion(bf16[2048,2048]{1,0:T(8,128)(2,1)} %param.10, bf16[16,224,128]{2,1,0:T(8,128)(2,1)S(1)} %all_to_all.74), kind=kOutput, calls=%fused_computation.23 | convolution fusion | flops 1879506944 | bytes 10223616 | tf_op jit(solution)/shard_map/dot_general | solution.py:88
  246.1 0.2 copy.83
  246.2 28.4 %all_to_all.75 = bf16[224,16,128]{2,0,1:T(8,128)(2,1)S(1)} all-to-all(bf16[224,16,128]{2,0,1:T(8,128)(2,1)S(1)} %bitcast.92), channel_id=1, replica_groups=mesh['seq'=16,'chan'=16] {'chan'}, dimensions={1} | all-to-all | bytes 1835008 | tf_op jit(solution)/shard_map/all_to_all | solution.py:89
  274.7 0.9 copy.85
  (11 shorter events, 0.2 us)
Async XLA Ops:
  6.5 84.0 %all-gather.5.cloned.1.call-start = ((), (), s32[]{:S(2)}) async-start(), calls=%async_computation.4 | async-start | bytes 8912896 | tf_op jit(solution)/shard_map/all_gather | solution.py:66
  7.3 180.9 %all-gather.7.cloned.1.call-start = ((), (), s32[]{:S(2)}) async-start(), calls=%async_computation.5 | async-start | bytes 1218560 | tf_op jit(solution)/shard_map/all_gather | solution.py:34
  188.2 3.4 %copy-start = (f32[4,896,16,16]{1,3,2,0:T(8,128)S(1)}, f32[4,896,16,16]{1,3,2,0:T(8,128)}, u32[]{:S(2)}) copy-start(f32[4,896,16,16]{1,3,2,0:T(8,128)} %multiply_multiply_fusion) | copy-start | bytes 11010052
Sparse Core Ops, SparseCore 0:
  9.1 81.3 all-gather.4
  144.9 43.1 all-gather.6

commit v2 on v1

--- a/solution.py
+++ b/solution.py
@@ -1,7 +1,11 @@
 import jax
 import jax.numpy as jnp
 from jax import lax
+from jax.experimental import pallas as pl
+from jax.experimental.pallas import tpu as pltpu
 from jax.sharding import PartitionSpec as P
+
+MESH = pl.DeviceIdType.MESH
 
 HEADS = 16
 FEAT = 16
@@ -15,6 +19,75 @@
         2.0 * FEAT
     ) ** (-0.5)
     return (linear, square)
+
+
+def exchange_kernel(x_ref, y_ref, buf, send_sem, recv_sem, own_sem):
+    n = x_ref.shape[0]
+    me = lax.axis_index("chan")
+    slab = lax.axis_index("seq")
+    barrier = pltpu.get_barrier_semaphore()
+    for step in range(1, n):
+        peer = lax.rem(me + step, n)
+        pl.semaphore_signal(barrier, inc=1, device_id=(slab, peer), device_id_type=MESH)
+    pl.semaphore_wait(barrier, n - 1)
+    own = pltpu.make_async_copy(x_ref.at[me], buf.at[me], own_sem)
+    own.start()
+    sends = []
+    for step in range(1, n):
+        peer = lax.rem(me + step, n)
+        copy = pltpu.make_async_remote_copy(
+            src_ref=x_ref.at[peer],
+            dst_ref=buf.at[me],
+            send_sem=send_sem.at[peer],
+            recv_sem=recv_sem.at[me],
+            device_id=(slab, peer),
+            device_id_type=MESH,
+        )
+        copy.start()
+        sends.append(copy)
+    for step in range(1, n):
+        source = lax.rem(me + n - step, n)
+        pltpu.make_async_remote_copy(
+            src_ref=x_ref.at[source],
+            dst_ref=buf.at[source],
+            send_sem=send_sem.at[source],
+            recv_sem=recv_sem.at[source],
+            device_id=(slab, source),
+            device_id_type=MESH,
+        ).wait_recv()
+    for copy in sends:
+        copy.wait_send()
+    own.wait()
+    y_ref[...] = buf[...]
+
+
+def exchange(x, collective_id):
+    n = x.shape[0]
+    return pl.pallas_call(
+        exchange_kernel,
+        out_shape=jax.ShapeDtypeStruct(x.shape, x.dtype),
+        in_specs=[pl.BlockSpec(memory_space=pltpu.VMEM)],
+        out_specs=pl.BlockSpec(memory_space=pltpu.VMEM),
+        scratch_shapes=[
+            pltpu.VMEM(x.shape, x.dtype),
+            pltpu.SemaphoreType.DMA((n,)),
+            pltpu.SemaphoreType.DMA((n,)),
+            pltpu.SemaphoreType.DMA(()),
+        ],
+        compiler_params=pltpu.CompilerParams(collective_id=collective_id, has_side_effects=True),
+    )(x)
+
+
+def split_rows(x, groups, collective_id):
+    rows, cols = x.shape
+    got = exchange(x.reshape(groups, rows // groups, cols), collective_id)
+    return got.transpose(1, 0, 2).reshape(rows // groups, groups * cols)
+
+
+def split_cols(x, groups, collective_id):
+    rows, _, cols = x.shape
+    got = exchange(x.transpose(1, 0, 2), collective_id)
+    return got.reshape(groups * rows, cols)
 
 
 def attend(query_rows, key_rows, value_rows, gain_mine, my_slab):
@@ -64,7 +137,7 @@
     my_group = lax.axis_index("chan")
     my_slab = lax.axis_index("seq")
     value_full = lax.all_gather(w_value, "chan", axis=1, tiled=True)
-    rows = lax.all_to_all(tokens, "chan", 0, 1, tiled=True)
+    rows = split_rows(tokens, groups, 1)
     chunk = rows.shape[0]
     weight = jnp.concatenate([w_query, w_key, value_full], axis=1)
     proj = jnp.dot(rows, weight, preferred_element_type=jnp.float32).astype(jnp.bfloat16)
@@ -73,7 +146,7 @@
     key = proj[:, qk_cols : 2 * qk_cols].reshape(chunk, groups, per_group * FEAT)
     value = proj[:, 2 * qk_cols :].reshape(chunk, groups, per_group * HEAD_DIM)
     packed = jnp.concatenate([query, key, value], axis=2)
-    mine = lax.all_to_all(packed, "chan", 1, 0, tiled=True)
+    mine = split_cols(packed, groups, 2)[:, None]
     tok_rows = mine.shape[0]
     qf = per_group * FEAT
     query_rows = mine[:, 0, :qf].reshape(tok_rows, per_group, FEAT)
@@ -84,9 +157,9 @@
         per_group, HEAD_DIM
     )
     hidden = attend(query_rows, key_rows, value_rows, gain_mine, my_slab)
-    hidden_rows = lax.all_to_all(hidden, "chan", 0, 1, tiled=True)
+    hidden_rows = split_rows(hidden, groups, 3)
     mixed_rows = jnp.dot(hidden_rows, w_out, preferred_element_type=jnp.float32).astype(jnp.bfloat16)
-    return lax.all_to_all(mixed_rows, "chan", 1, 0, tiled=True)
+    return split_cols(mixed_rows.reshape(chunk, groups, -1), groups, 4)
 
 
 def solution(mesh):

time: 283 us -> 295 us (1.042)
  Pallas kernels: 0 us -> 144 us
  blocking collectives: 144 us -> 0 us
  waiting for transfers between devices: 81.7 us -> 85.3 us
  other arithmetic: 7.13 us -> 10.7 us
    all_to_all x4 -> x0, blocking collectives: 144 us -> none  [the longest x1 41.4 us: per_device(): rows = lax.all_to_all(tokens, 'chan', 0, 1, tiled=True)]
    pallas_call x0 -> x4, Pallas kernels: none -> 144 us  [exchange(): pl.pallas_call(exchange_kernel, out_shape=jax.ShapeDtypeStruct(x.shape, x...]
    all_to_all x3 -> x0, local copies, waits for them, and re-layouts: 3.08 us -> none  [the longest x2 2.92 us: per_device(): mine = lax.all_to_all(packed, 'chan', 1, 0, tiled=True)]
  transfers between devices with their start and end apart: 2 -> 2, of which waited for: 2 -> 2; matrix products, arithmetic and copies ran while one was open for 1% -> 2% of each run, Pallas kernels for 0% -> 13%
where the time goes in v2:
time: 295 us
  Pallas kernels  144 us (49%)
  waiting for transfers between devices  85.3 us (29%)
  matrix products  30 us (10%)
  between operations  13.6 us (5%)
  local copies, waits for them, and re-layouts  11.3 us (4%)
  other arithmetic  10.7 us (4%)
    pallas_call x4, Pallas kernels, exchange(): pl.pallas_call(exchange_kernel, out_shape=jax.ShapeDtypeStruct(x.shape, x...  144 us
    all_gather x1, waiting for transfers between devices, per_device(): value_full = lax.all_gather(w_value, 'chan', axis=1, tiled=True)  43.3 us
    all_gather x1, waiting for transfers between devices, attend(): lax.all_gather(slab_total[None].astype(jnp.bfloat16), 'seq', axis=0, tile...  41.3 us
    dot_general x1, matrix products, attend(): jnp.einsum('bhts,bshe->bthe', weights, value_blocks, preferred_element_ty...  9.12 us
    dot_general x1, matrix products, per_device(): jnp.dot(rows, weight, preferred_element_type=jnp.float32)  6.4 us
  transfers between devices with their start and end apart: 2, of which 2 were waited for; matrix products, arithmetic and copies ran while one was open for 2% of the time, Pallas kernels for 13%

profile of v2, /device:TPU:1, one launch (start us, length us, event | category | flops | bytes accessed | tf_op | source)
XLA Modules:
  0.0 294.7 jit_solution(533261183470288064)
XLA Ops:
  6.5 0.0 all-gather.5.cloned.1.call-start
  6.5 0.7 all-gather.5.cloned.1.call-update
  7.3 0.0 all-gather.7.cloned.1.call-start
  7.3 38.1 %shard_map.64 = bf16[16,224,128]{2,1,0:T(8,128)(2,1)} custom-call(bf16[16,224,128]{2,1,0:T(8,128)(2,1)} %bitcast.99), custom_call_target="tpu_custom_call" | custom-call | tf_op jit(solution)/shard_map/pallas_call | solution.py:66
  45.4 43.3 %all-gather.5.cloned.1.call-done = bf16[2048,2048]{1,0:T(8,128)(2,1)} async-done(((bf16[2048,128]{1,0:T(8,128)(2,1)}), bf16[2048,2048]{1,0:T(8,128)(2,1)}) %all-gather.5.cloned.1.call-update) | async-done | bytes 8388624 | tf_op jit(solution)/shard_map/all_gather | solution.py:139
  88.8 6.4 %fusion.9 = bf16[224,2560]{1,0:T(8,128)(2,1)S(1)} fusion(bf16[2048,2048]{1,0:T(8,128)(2,1)} %all-gather.5.cloned.1.call-done, bf16[2048,256]{1,0:T(8,128)(2,1)} %param.8, bf16[2048,256]{1,0:T(8,128)(2,1)} %param.7, bf16[16,224,128]{2,1,0:T(8,128)(2,1)} %shard_map.64), kind=kOutput, calls=%fused_computation.10 | convolution fusion | flops 2380840960 | bytes 12550144 | tf_op jit(solution)/shard_map/dot_general | solution.py:143
  95.2 0.2 copy_bitcast_fusion
  95.3 0.1 copy.35
  95.5 0.4 copy.37
  95.9 0.1 copy.36
  96.0 0.4 copy.38
  96.4 2.9 maximum_bitcast_fusion.x_ref
  99.3 47.3 %shard_map.65 = bf16[16,224,160]{2,1,0:T(8,128)(2,1)} custom-call(bf16[16,224,160]{2,1,0:T(8,128)(2,1)} %maximum_bitcast_fusion.x_ref), custom_call_target="tpu_custom_call" | custom-call | tf_op jit(solution)/shard_map/pallas_call | solution.py:66
  146.5 0.0 copy-start.1
  146.5 1.9 fusion.39
  148.5 0.1 copy-done.1
  148.6 0.3 slice.43
  148.9 0.3 copy.43
  149.3 0.5 convolution_bitcast_fusion.1
  149.8 0.1 convert_reduce_fusion
  149.9 0.4 multiply_multiply_fusion.1
  150.3 1.8 convolution_bitcast_fusion
  152.1 0.7 fusion.22
  152.8 0.0 all-gather.7.cloned.1.call-update
  152.8 1.3 dynamic_slice.3
  154.2 1.1 iota_compare_fusion
  155.3 0.1 fusion.23
  155.4 0.3 copy.42
  155.7 2.2 multiply_multiply_fusion
  157.9 41.3 %all-gather.7.cloned.1.call-done = bf16[16,273,128]{2,1,0:T(8,128)(2,1)} async-done(((bf16[1,273,128]{2,1,0:T(8,128)(2,1)}), bf16[16,273,128]{2,1,0:T(8,128)(2,1)}) %all-gather.7.cloned.1.call-update) | async-done | bytes 1118224 | tf_op jit(solution)/shard_map/all_gather | solution.py:107
  199.2 0.0 copy-start
  199.2 1.7 fusion.12
  200.9 2.9 fusion.24
  203.8 0.0 copy-start.2
  203.8 0.6 slice.47
  204.4 0.0 copy-done
  204.4 3.5 %fusion.21 = f32[4,128,896]{2,1,0:T(8,128)} fusion(f32[4,896,256]{1,2,0:T(8,128)S(1)} %bitcast.89, f32[4,1,273,128]{3,2,0,1:T(8,128)S(1)} %pad_add_fusion), kind=kOutput, calls=%fused_computation.37 | convolution fusion | flops 1409286144 | bytes 6029312 | tf_op jit(solution)/shard_map/bthf,bhfe->bthe/dot_general | solution.py:118
  208.0 0.0 copy-done.2
  208.0 9.1 %multiply_reduce_fusion = (f32[4,896]{1,0:T(4,128)}, f32[4,896,1,128]{1,3,0,2:T(8,128)}) fusion(f32[4,128,896]{2,1,0:T(8,128)} %fusion.21, f32[4,128,896]{2,1,0:T(8,128)} %fusion.24, f32[4,128]{1,0:T(4,128)} %bitcast.105, bf16[4,896,128]{2,1,0:T(8,128)(2,1)S(1)} %bitcast.87, bf16[4,896,16]{2,1,0:T(8,128)(2,1)S(1)} %bitcast.96, ...), kind=kOutput, calls=%fused_computation.22 | convolution fusion | flops 949613056 | bytes 7471104 | tf_op jit(solution)/shard_map/bhts,bshe->bthe/dot_general | solution.py:127
  217.1 0.0 copy-start.3
  217.1 0.0 copy-start.4
  217.1 1.8 copy.49
  218.9 0.0 copy-done.3
  218.9 0.1 rsqrt.12
  219.0 0.0 copy-done.4
  219.0 1.5 multiply_convert_fusion.x_ref
  220.5 31.2 %shard_map.66 = bf16[16,224,128]{2,1,0:T(8,128)(2,1)} custom-call(bf16[16,224,128]{2,1,0:T(8,128)(2,1)} %multiply_convert_fusion.x_ref), custom_call_target="tpu_custom_call" | custom-call | tf_op jit(solution)/shard_map/pallas_call | solution.py:66
  251.6 5.7 %fusion.16 = bf16[28,16,8,128]{3,2,1,0:T(8,128)(2,1)S(1)} fusion(bf16[2048,2048]{1,0:T(8,128)(2,1)} %param.10, bf16[16,224,128]{2,1,0:T(8,128)(2,1)} %shard_map.66), kind=kOutput, calls=%fused_computation.24 | convolution fusion | flops 1879506944 | bytes 10223616 | tf_op jit(solution)/shard_map/dot_general | solution.py:161
  257.4 1.1 copy.75
  258.5 27.2 %shard_map.67 = bf16[16,224,128]{2,1,0:T(8,128)(2,1)} custom-call(bf16[16,224,128]{2,1,0:T(8,128)(2,1)} %bitcast.97), custom_call_target="tpu_custom_call" | custom-call | tf_op jit(solution)/shard_map/pallas_call | solution.py:66
  285.7 2.2 copy.77
  (7 shorter events, 0.2 us)
Async XLA Ops:
  6.5 82.2 %all-gather.5.cloned.1.call-start = ((), (), s32[]{:S(2)}) async-start(), calls=%async_computation | async-start | bytes 8912896 | tf_op jit(solution)/shard_map/all_gather | solution.py:139
  7.3 191.9 %all-gather.7.cloned.1.call-start = ((), (), s32[]{:S(2)}) async-start(), calls=%async_computation.1 | async-start | bytes 1218560 | tf_op jit(solution)/shard_map/all_gather | solution.py:107
  146.5 2.1 copy-start.1
  199.2 5.3 %copy-start = (f32[4,896,16,16]{1,3,2,0:T(8,128)S(1)}, f32[4,896,16,16]{1,3,2,0:T(8,128)}, u32[]{:S(2)}) copy-start(f32[4,896,16,16]{1,3,2,0:T(8,128)} %multiply_multiply_fusion) | copy-start | bytes 11010052
  203.8 4.1 %copy-start.2 = (pred[896,896]{1,0:T(8,128)(4,1)S(1)}, pred[896,896]{1,0:T(8,128)(4,1)}, u32[]{:S(2)}) copy-start(pred[896,896]{1,0:T(8,128)(4,1)} %iota_compare_fusion) | copy-start | bytes 2408452
  217.1 1.8 copy-start.3
  217.1 1.9 copy-start.4
Sparse Core Ops, SparseCore 0:
  9.1 79.5 all-gather.4
  152.9 46.1 all-gather.6

commit v3 on v2

--- a/solution.py
+++ b/solution.py
@@ -6,6 +6,16 @@
 from jax.sharding import PartitionSpec as P
 
 MESH = pl.DeviceIdType.MESH
+CHAN = ("z", "core")
+
+
+def chan_index():
+    return lax.axis_index("z") * lax.axis_size("core") + lax.axis_index("core")
+
+
+def chan_device(slab, peer):
+    cores = lax.axis_size("core")
+    return (slab, peer // cores, peer % cores)
 
 HEADS = 16
 FEAT = 16
@@ -23,12 +33,12 @@
 
 def exchange_kernel(x_ref, y_ref, buf, send_sem, recv_sem, own_sem):
     n = x_ref.shape[0]
-    me = lax.axis_index("chan")
+    me = chan_index()
     slab = lax.axis_index("seq")
     barrier = pltpu.get_barrier_semaphore()
     for step in range(1, n):
         peer = lax.rem(me + step, n)
-        pl.semaphore_signal(barrier, inc=1, device_id=(slab, peer), device_id_type=MESH)
+        pl.semaphore_signal(barrier, inc=1, device_id=chan_device(slab, peer), device_id_type=MESH)
     pl.semaphore_wait(barrier, n - 1)
     own = pltpu.make_async_copy(x_ref.at[me], buf.at[me], own_sem)
     own.start()
@@ -40,7 +50,7 @@
             dst_ref=buf.at[me],
             send_sem=send_sem.at[peer],
             recv_sem=recv_sem.at[me],
-            device_id=(slab, peer),
+            device_id=chan_device(slab, peer),
             device_id_type=MESH,
         )
         copy.start()
@@ -52,7 +62,7 @@
             dst_ref=buf.at[source],
             send_sem=send_sem.at[source],
             recv_sem=recv_sem.at[source],
-            device_id=(slab, source),
+            device_id=chan_device(slab, source),
             device_id_type=MESH,
         ).wait_recv()
     for copy in sends:
@@ -78,6 +88,63 @@
     )(x)
 
 
+def gather_kernel(x_ref, y_ref, buf, send_sem, recv_sem, own_sem):
+    n = buf.shape[0]
+    me = lax.axis_index("seq")
+    here = (lax.axis_index("z"), lax.axis_index("core"))
+    barrier = pltpu.get_barrier_semaphore()
+    for step in range(1, n):
+        peer = lax.rem(me + step, n)
+        pl.semaphore_signal(barrier, inc=1, device_id=(peer,) + here, device_id_type=MESH)
+    pl.semaphore_wait(barrier, n - 1)
+    own = pltpu.make_async_copy(x_ref, buf.at[me], own_sem)
+    own.start()
+    sends = []
+    for step in range(1, n):
+        peer = lax.rem(me + step, n)
+        copy = pltpu.make_async_remote_copy(
+            src_ref=x_ref,
+            dst_ref=buf.at[me],
+            send_sem=send_sem.at[peer],
+            recv_sem=recv_sem.at[me],
+            device_id=(peer,) + here,
+            device_id_type=MESH,
+        )
+        copy.start()
+        sends.append(copy)
+    for step in range(1, n):
+        source = lax.rem(me + n - step, n)
+        pltpu.make_async_remote_copy(
+            src_ref=x_ref,
+            dst_ref=buf.at[source],
+            send_sem=send_sem.at[source],
+            recv_sem=recv_sem.at[source],
+            device_id=(source,) + here,
+            device_id_type=MESH,
+        ).wait_recv()
+    for copy in sends:
+        copy.wait_send()
+    own.wait()
+    y_ref[...] = buf[...]
+
+
+def gather_seq(x, slabs, collective_id):
+    shape = (slabs,) + x.shape
+    return pl.pallas_call(
+        gather_kernel,
+        out_shape=jax.ShapeDtypeStruct(shape, x.dtype),
+        in_specs=[pl.BlockSpec(memory_space=pltpu.VMEM)],
+        out_specs=pl.BlockSpec(memory_space=pltpu.VMEM),
+        scratch_shapes=[
+            pltpu.VMEM(shape, x.dtype),
+            pltpu.SemaphoreType.DMA((slabs,)),
+            pltpu.SemaphoreType.DMA((slabs,)),
+            pltpu.SemaphoreType.DMA(()),
+        ],
+        compiler_params=pltpu.CompilerParams(collective_id=collective_id, has_side_effects=True),
+    )(x)
+
+
 def split_rows(x, groups, collective_id):
     rows, cols = x.shape
     got = exchange(x.reshape(groups, rows // groups, cols), collective_id)
@@ -104,9 +171,10 @@
     own_two = jnp.einsum("bthf,bthe->bhfe", key_square, value_f32, precision=highest)
     own = jnp.concatenate([own_zero, own_one, own_two], axis=2)
     slab_total = jnp.sum(own, axis=0)
-    pieces = lax.all_gather(
-        slab_total[None].astype(jnp.bfloat16), "seq", axis=0, tiled=True
-    ).astype(jnp.float32)
+    state_rows = slab_total.shape[0] * slab_total.shape[1]
+    pieces = gather_seq(
+        slab_total.astype(jnp.bfloat16).reshape(state_rows, HEAD_DIM), lax.axis_size("seq"), 5
+    ).astype(jnp.float32).reshape((-1,) + slab_total.shape)
     count = pieces.shape[0]
     earlier_mask = jnp.arange(count, dtype=jnp.int32) < my_slab
     prefix = jnp.sum(jnp.where(earlier_mask[:, None, None, None], pieces, 0.0), axis=0)
@@ -132,21 +200,25 @@
 
 
 def per_device(tokens, w_query, w_key, w_value, w_out, gain):
-    groups = lax.axis_size("chan")
+    groups = lax.axis_size(CHAN)
     per_group = HEADS // groups
-    my_group = lax.axis_index("chan")
+    my_group = chan_index()
     my_slab = lax.axis_index("seq")
-    value_full = lax.all_gather(w_value, "chan", axis=1, tiled=True)
+    value_z = lax.all_gather(w_value, "z", axis=0)
+    value_all = lax.all_gather(value_z, "core", axis=0)
     rows = split_rows(tokens, groups, 1)
     chunk = rows.shape[0]
-    weight = jnp.concatenate([w_query, w_key, value_full], axis=1)
-    proj = jnp.dot(rows, weight, preferred_element_type=jnp.float32).astype(jnp.bfloat16)
-    qk_cols = HEADS * FEAT
-    query = proj[:, :qk_cols].reshape(chunk, groups, per_group * FEAT)
-    key = proj[:, qk_cols : 2 * qk_cols].reshape(chunk, groups, per_group * FEAT)
-    value = proj[:, 2 * qk_cols :].reshape(chunk, groups, per_group * HEAD_DIM)
+    query = jnp.dot(rows, w_query, preferred_element_type=jnp.float32).astype(jnp.bfloat16)
+    key = jnp.dot(rows, w_key, preferred_element_type=jnp.float32).astype(jnp.bfloat16)
+    value = jnp.einsum("tf,czfe->tzce", rows, value_all, preferred_element_type=jnp.float32)
+    value = value.astype(jnp.bfloat16).reshape(chunk, groups, per_group * HEAD_DIM)
+    query = query.reshape(chunk, groups, per_group * FEAT)
+    key = key.reshape(chunk, groups, per_group * FEAT)
     packed = jnp.concatenate([query, key, value], axis=2)
-    mine = split_cols(packed, groups, 2)[:, None]
+    width = packed.shape[2]
+    lanes = chunk * width // HEAD_DIM
+    sent = exchange(packed.transpose(1, 0, 2).reshape(groups, lanes, HEAD_DIM), 2)
+    mine = sent.reshape(groups * chunk, 1, width)
     tok_rows = mine.shape[0]
     qf = per_group * FEAT
     query_rows = mine[:, 0, :qf].reshape(tok_rows, per_group, FEAT)
@@ -163,10 +235,13 @@
 
 
 def solution(mesh):
+    seq, chan = mesh.devices.shape
+    cores = 2 if chan % 2 == 0 else 1
+    split = jax.sharding.Mesh(mesh.devices.reshape(seq, chan // cores, cores), ("seq", "z", "core"))
     return jax.shard_map(
         per_device,
-        mesh=mesh,
-        in_specs=(P("seq", "chan"), P(), P(), P(None, "chan"), P(), P()),
-        out_specs=P("seq", "chan"),
+        mesh=split,
+        in_specs=(P("seq", CHAN), P(), P(), P(None, CHAN), P(), P()),
+        out_specs=P("seq", CHAN),
         check_vma=False,
     )

time: 295 us -> 284 us (0.963)
  waiting for transfers between devices: 85.3 us -> 61.2 us
  local copies, waits for them, and re-layouts: 11.3 us -> 26.1 us
    pallas_call x4, Pallas kernels: 144 us -> 118 us  [exchange(): pl.pallas_call(exchange_kernel, out_shape=jax.ShapeDtypeStruct(x.shape, x...]
    pallas_call x0 -> x1, Pallas kernels: none -> 24.6 us  [gather_seq(): pl.pallas_call(gather_kernel, out_shape=jax.ShapeDtypeStruct(shape, x.dty...]
    all_gather x2, waiting for transfers between devices: 84.6 us -> 60.5 us  [the longest x1 60.5 us: per_device(): value_z = lax.all_gather(w_value, 'z', axis=0)]
    reshape x4 -> x6, local copies, waits for them, and re-layouts: 1.27 us -> 12.1 us  [the longest x1 3.83 us: per_device(): packed.transpose(1, 0, 2).reshape(groups, lanes, HEAD_DIM)]
    dot_general x1 -> x3, matrix products: 6.4 us -> 7.6 us  [the longest x1 5.57 us: per_device(): jnp.einsum('tf,czfe->tzce', rows, value_all, preferred_element_type=jnp.f...]
  transfers between devices with their start and end apart: 2 -> 2, of which waited for: 2 -> 1; matrix products, arithmetic and copies ran while one was open for 2% -> 3% of each run, Pallas kernels for 13% -> 10%
where the time goes in v3:
time: 284 us; the launch traced here: 283 us
  Pallas kernels  143 us (50%)
  waiting for transfers between devices  61.2 us (22%)
  matrix products  30.9 us (11%)
  local copies, waits for them, and re-layouts  26.1 us (9%)
  between operations  13.7 us (5%)
  other arithmetic  8.46 us (3%)
    pallas_call x4, Pallas kernels, exchange(): pl.pallas_call(exchange_kernel, out_shape=jax.ShapeDtypeStruct(x.shape, x...  118 us
    all_gather x1, waiting for transfers between devices, per_device(): value_z = lax.all_gather(w_value, 'z', axis=0)  60.5 us
    pallas_call x1, Pallas kernels, gather_seq(): pl.pallas_call(gather_kernel, out_shape=jax.ShapeDtypeStruct(shape, x.dty...  24.6 us
    dot_general x1, matrix products, attend(): jnp.einsum('bhts,bshe->bthe', weights, value_blocks, preferred_element_ty...  8.84 us
    dot_general x1, matrix products, per_device(): jnp.dot(hidden_rows, w_out, preferred_element_type=jnp.float32)  5.75 us
  transfers between devices with their start and end apart: 2, of which 1 were waited for; matrix products, arithmetic and copies ran while one was open for 3% of the time, Pallas kernels for 10%

profile of v3, /device:TPU:1, one launch (start us, length us, event | category | flops | bytes accessed | tf_op | source)
XLA Modules:
  0.0 283.5 jit_solution(5953769940399015256)
XLA Ops:
  6.5 0.0 copy-start
  6.5 0.0 all-gather.5.cloned.1.call-start
  6.5 0.7 all-gather.5.cloned.1.call-update
  7.3 0.0 all-gather.7.cloned.1.call-start
  7.3 60.5 %all-gather.5.cloned.1.call-done = bf16[16384,128]{1,0:T(8,128)(2,1)} async-done(((bf16[2048,128]{1,0:T(8,128)(2,1)}), bf16[16384,128]{1,0:T(8,128)(2,1)}) %all-gather.5.cloned.1.call-update) | async-done | bytes 4194320 | tf_op jit(solution)/shard_map/all_gather | solution.py:207
  67.8 0.0 all-gather.7.cloned.1.call-update
  67.8 27.9 %shard_map.64 = bf16[16,224,128]{2,1,0:T(8,128)(2,1)} custom-call(bf16[16,224,128]{2,1,0:T(8,128)(2,1)} %bitcast.102), custom_call_target="tpu_custom_call" | custom-call | tf_op jit(solution)/shard_map/pallas_call | solution.py:76
  95.7 0.0 copy-start.4
  95.7 1.6 copy.36
  97.4 1.3 reshape.242
  98.7 0.0 copy-done
  98.7 0.0 copy-done.4
  98.7 0.0 copy-start.8
  98.7 0.4 convolution_convert_fusion.2
  99.1 0.1 copy.38
  99.2 1.3 copy.41
  100.5 1.6 convolution_convert_fusion.3
  102.1 0.1 copy.37
  102.2 1.3 copy.40
  103.5 0.8 dynamic_slice.3
  104.3 1.1 iota_compare_fusion
  105.4 0.0 all-gather.7.cloned.1.call-done
  105.4 0.0 copy-done.8
  105.4 0.0 copy-start.5
  105.4 5.6 %fusion.3 = bf16[224,8,2,128]{3,0,1,2:T(8,128)(2,1)S(1)} fusion(bf16[2,8,2048,128]{3,2,1,0:T(8,128)(2,1)} %bitcast.108, bf16[224,2048,1,1]{1,0,2,3:T(8,128)(2,1)S(1)} %copy-done.8), kind=kOutput, calls=%fused_computation.16 | convolution fusion | flops 1879506944 | bytes 10223616 | tf_op jit(solution)/shard_map/tf,czfe->tzce/dot_general | solution.py:213
  111.0 0.1 copy.39
  111.1 0.0 copy-done.5
  111.1 0.0 copy-done.6
  111.1 1.6 maximum_bitcast_fusion
  112.7 3.8 %reshape.229.x_ref = bf16[16,280,128]{2,1,0:T(8,128)(2,1)} reshape(bf16[16,224,160]{2,1,0:T(8,128)(2,1)S(1)} %maximum_bitcast_fusion) | data formatting | bytes 2293760 | tf_op jit(solution)/shard_map/reshape | solution.py:220
  116.6 32.9 %shard_map.65 = bf16[16,280,128]{2,1,0:T(8,128)(2,1)} custom-call(bf16[16,280,128]{2,1,0:T(8,128)(2,1)} %reshape.229.x_ref), custom_call_target="tpu_custom_call" | custom-call | tf_op jit(solution)/shard_map/pallas_call | solution.py:76
  149.4 3.4 %reshape.230 = bf16[3584,1,160]{2,0,1:T(8,128)(2,1)S(1)} reshape(bf16[16,280,128]{2,1,0:T(8,128)(2,1)} %shard_map.65) | data formatting | bytes 2293760 | tf_op jit(solution)/shard_map/reshape | solution.py:221
  152.9 0.0 copy-start.1
  152.9 1.2 copy-done.1
  154.2 1.6 fusion.29
  155.8 1.8 slice.28
  157.6 1.5 copy.45
  159.1 0.5 convolution_bitcast_fusion.1
  159.6 0.1 convert_reduce_fusion
  159.8 0.4 multiply_multiply_fusion.1
  160.2 0.0 copy-start.3
  160.2 1.8 convolution_bitcast_fusion
  162.0 0.1 fusion.14
  162.1 0.7 fusion.13.x_ref
  162.7 0.0 copy-done.3
  162.7 0.9 copy.44
  163.7 1.0 convert_element_type.88
  164.7 24.6 %shard_map.66 = bf16[16,273,128]{2,1,0:T(8,128)(2,1)} custom-call(bf16[273,128]{1,0:T(8,128)(2,1)} %fusion.13.x_ref), custom_call_target="tpu_custom_call" | custom-call | tf_op jit(solution)/shard_map/pallas_call | solution.py:133
  189.3 1.6 select_reduce_fusion
  190.9 0.0 copy-done.7
  190.9 2.9 %fusion.15 = f32[4,128,896]{2,1,0:T(8,128)} fusion(bf16[4,896,16]{1,2,0:T(8,128)(2,1)S(1)} %copy-done.7, f32[4,1,273,128]{3,2,0,1:T(8,128)S(1)} %pad_add_fusion), kind=kOutput, calls=%fused_computation.36 | convolution fusion | flops 88195072 | bytes 1982464 | tf_op jit(solution)/shard_map/bthf,bhfe->bthe/dot_general | solution.py:183
  193.8 0.4 multiply_multiply_fusion
  194.2 0.0 copy-start.2
  194.2 3.5 %fusion.12 = f32[4,128,896]{2,1,0:T(8,128)} fusion(f32[4,896,256]{1,2,0:T(8,128)S(1)} %bitcast.91, f32[4,1,273,128]{3,2,0,1:T(8,128)S(1)} %pad_add_fusion), kind=kOutput, calls=%fused_computation.33 | convolution fusion | flops 1409286144 | bytes 6029312 | tf_op jit(solution)/shard_map/bthf,bhfe->bthe/dot_general | solution.py:186
  197.7 0.0 copy-done.2
  197.7 8.8 %multiply_reduce_fusion = (f32[4,896]{1,0:T(4,128)S(1)}, f32[4,896,1,128]{1,3,0,2:T(8,128)}) fusion(f32[4,128,896]{2,1,0:T(8,128)} %fusion.12, f32[4,128,896]{2,1,0:T(8,128)} %fusion.15, f32[4,128]{1,0:T(4,128)S(1)} %bitcast.107, bf16[4,896,128]{2,1,0:T(8,128)(2,1)S(1)} %bitcast.89, bf16[4,896,16]{2,1,0:T(8,128)(2,1)} %bitcast.96, ...), kind=kOutput, calls=%fused_computation.13 | convolution fusion | flops 949613056 | bytes 7471104 | tf_op jit(solution)/shard_map/bhts,bshe->bthe/dot_general | solution.py:195
  206.6 1.8 copy.51
  208.4 0.1 rsqrt.12
  208.5 1.5 multiply_convert_fusion.x_ref
  209.9 29.1 %shard_map.67 = bf16[16,224,128]{2,1,0:T(8,128)(2,1)} custom-call(bf16[16,224,128]{2,1,0:T(8,128)(2,1)} %multiply_convert_fusion.x_ref), custom_call_target="tpu_custom_call" | custom-call | tf_op jit(solution)/shard_map/pallas_call | solution.py:76
  239.1 5.7 %fusion.4 = bf16[28,16,8,128]{3,2,1,0:T(8,128)(2,1)S(1)} fusion(bf16[2048,2048]{1,0:T(8,128)(2,1)} %param.10, bf16[16,224,128]{2,1,0:T(8,128)(2,1)} %shard_map.67), kind=kOutput, calls=%fused_computation.17 | convolution fusion | flops 1879506944 | bytes 10223616 | tf_op jit(solution)/shard_map/dot_general | solution.py:233
  244.8 1.1 copy.80
  245.9 28.5 %shard_map.68 = bf16[16,224,128]{2,1,0:T(8,128)(2,1)} custom-call(bf16[16,224,128]{2,1,0:T(8,128)(2,1)} %bitcast.99), custom_call_target="tpu_custom_call" | custom-call | tf_op jit(solution)/shard_map/pallas_call | solution.py:76
  274.5 2.2 copy.82
  (8 shorter events, 0.1 us)
Async XLA Ops:
  6.5 92.1 %copy-start = (bf16[2048,256]{1,0:T(8,128)(2,1)S(1)}, bf16[2048,256]{1,0:T(8,128)(2,1)}, u32[]{:S(2)}) copy-start(bf16[2048,256]{1,0:T(8,128)(2,1)} %param.8) | copy-start | bytes 3145732
  6.5 61.3 %all-gather.5.cloned.1.call-start = ((), (), s32[]{:S(2)}) async-start(), calls=%async_computation | async-start | bytes 4718592 | tf_op jit(solution)/shard_map/all_gather | solution.py:207
  7.3 98.2 %all-gather.7.cloned.1.call-start = ((), (), s32[]{:S(2)}) async-start(), calls=%async_computation.1 | async-start | bytes 12582912 | tf_op jit(solution)/shard_map/all_gather | solution.py:208
  95.7 2.9 %copy-start.4 = (bf16[16,224,128]{2,1,0:T(8,128)(2,1)S(1)}, bf16[16,224,128]{2,1,0:T(8,128)(2,1)}, u32[]{:S(2)}) copy-start(bf16[16,224,128]{2,1,0:T(8,128)(2,1)} %shard_map.64) | copy-start | bytes 2752516
  98.7 6.8 %copy-start.8 = (bf16[224,2048,1,1]{1,0,2,3:T(8,128)(2,1)S(1)}, bf16[224,2048,1,1]{1,0,2,3:T(8,128)(2,1)}, u32[]{:S(2)}) copy-start(bf16[224,2048,1,1]{1,0,2,3:T(8,128)(2,1)} %reshape.242) | copy-start | bytes 2752516
  105.4 5.7 %copy-start.5 = (bf16[224,16,16]{2,0,1:T(8,128)(2,1)S(1)}, bf16[224,16,16]{2,0,1:T(8,128)(2,1)}, u32[]{:S(2)}) copy-start(bf16[224,16,16]{2,0,1:T(8,128)(2,1)} %copy.41) | copy-start | bytes 344068
  105.4 5.7 %copy-start.6 = (bf16[224,16,16]{2,0,1:T(8,128)(2,1)S(1)}, bf16[224,16,16]{2,0,1:T(8,128)(2,1)}, u32[]{:S(2)}) copy-start(bf16[224,16,16]{2,0,1:T(8,128)(2,1)} %copy.40) | copy-start | bytes 344068
  152.9 1.3 copy-start.1
  160.2 2.6 copy-start.3
  163.7 27.3 %copy-start.7 = (bf16[4,896,16]{1,2,0:T(8,128)(2,1)S(1)}, bf16[4,896,16]{1,2,0:T(8,128)(2,1)}, u32[]{:S(2)}) copy-start(bf16[4,896,16]{1,2,0:T(8,128)(2,1)} %copy.44) | copy-start | bytes 344068
  194.2 3.5 %copy-start.2 = (bf16[3584,1,16]{2,0,1:T(8,128)(2,1)S(1)}, bf16[3584,1,16]{2,0,1:T(8,128)(2,1)}, u32[]{:S(2)}) copy-start(bf16[3584,1,16]{2,0,1:T(8,128)(2,1)} %get-tuple-element.5) | copy-start | bytes 344068
Sparse Core Ops, SparseCore 0:
  9.1 58.6 all-gather.4
  69.6 24.5 all-gather.6

commit v4 on v3

--- a/solution.py
+++ b/solution.py
@@ -141,6 +141,35 @@
             pltpu.SemaphoreType.DMA((slabs,)),
             pltpu.SemaphoreType.DMA(()),
         ],
+        compiler_params=pltpu.CompilerParams(collective_id=collective_id, has_side_effects=True),
+    )(x)
+
+
+def swap_kernel(x_ref, y_ref, send_sem, recv_sem):
+    here = (lax.axis_index("seq"), lax.axis_index("z"))
+    other = lax.axis_size("core") - 1 - lax.axis_index("core")
+    barrier = pltpu.get_barrier_semaphore()
+    pl.semaphore_signal(barrier, inc=1, device_id=here + (other,), device_id_type=MESH)
+    pl.semaphore_wait(barrier, 1)
+    copy = pltpu.make_async_remote_copy(
+        src_ref=x_ref,
+        dst_ref=y_ref,
+        send_sem=send_sem,
+        recv_sem=recv_sem,
+        device_id=here + (other,),
+        device_id_type=MESH,
+    )
+    copy.start()
+    copy.wait()
+
+
+def swap_cores(x, collective_id):
+    return pl.pallas_call(
+        swap_kernel,
+        out_shape=jax.ShapeDtypeStruct(x.shape, x.dtype),
+        in_specs=[pl.BlockSpec(memory_space=pl.ANY)],
+        out_specs=pl.BlockSpec(memory_space=pl.ANY),
+        scratch_shapes=[pltpu.SemaphoreType.DMA(()), pltpu.SemaphoreType.DMA(())],
         compiler_params=pltpu.CompilerParams(collective_id=collective_id, has_side_effects=True),
     )(x)
 
@@ -205,12 +234,20 @@
     my_group = chan_index()
     my_slab = lax.axis_index("seq")
     value_z = lax.all_gather(w_value, "z", axis=0)
-    value_all = lax.all_gather(value_z, "core", axis=0)
     rows = split_rows(tokens, groups, 1)
+    value_z, rows = lax.optimization_barrier((value_z, rows))
+    value_other = swap_cores(value_z, 6)
     chunk = rows.shape[0]
     query = jnp.dot(rows, w_query, preferred_element_type=jnp.float32).astype(jnp.bfloat16)
     key = jnp.dot(rows, w_key, preferred_element_type=jnp.float32).astype(jnp.bfloat16)
-    value = jnp.einsum("tf,czfe->tzce", rows, value_all, preferred_element_type=jnp.float32)
+    value_mine = jnp.einsum("tf,zfe->tze", rows, value_z, preferred_element_type=jnp.float32)
+    value_pair = jnp.einsum("tf,zfe->tze", rows, value_other, preferred_element_type=jnp.float32)
+    first = lax.axis_index("core") == 0
+    value = jnp.where(
+        first,
+        jnp.stack([value_mine, value_pair], axis=2),
+        jnp.stack([value_pair, value_mine], axis=2),
+    )
     value = value.astype(jnp.bfloat16).reshape(chunk, groups, per_group * HEAD_DIM)
     query = query.reshape(chunk, groups, per_group * FEAT)
     key = key.reshape(chunk, groups, per_group * FEAT)

time: 284 us -> 270 us (0.951)
  waiting for transfers between devices: 61.2 us -> 29 us
  Pallas kernels: 143 us -> 162 us
    all_gather x1, waiting for transfers between devices: 60.5 us -> 28.3 us  [per_device(): value_z = lax.all_gather(w_value, 'z', axis=0)]
    pallas_call x4, Pallas kernels: 118 us -> 131 us  [exchange(): pl.pallas_call(exchange_kernel, out_shape=jax.ShapeDtypeStruct(x.shape, x...]
    pallas_call x0 -> x1, Pallas kernels: none -> 7.6 us  [swap_cores(): pl.pallas_call(swap_kernel, out_shape=jax.ShapeDtypeStruct(x.shape, x.dty...]
  transfers between devices with their start and end apart: 2 -> 1, of which waited for: 1 -> 1; matrix products, arithmetic and copies ran while one was open for 3% -> 1% of each run, Pallas kernels for 10% -> 15%
where the time goes in v4:
time: 270 us; the launch traced here: 269 us
  Pallas kernels  162 us (60%)
  waiting for transfers between devices  29 us (11%)
  matrix products  28.7 us (11%)
  local copies, waits for them, and re-layouts  25.5 us (9%)
  between operations  13.7 us (5%)
  other arithmetic  10.4 us (4%)
    pallas_call x4, Pallas kernels, exchange(): pl.pallas_call(exchange_kernel, out_shape=jax.ShapeDtypeStruct(x.shape, x...  131 us
    all_gather x1, waiting for transfers between devices, per_device(): value_z = lax.all_gather(w_value, 'z', axis=0)  28.3 us
    pallas_call x1, Pallas kernels, gather_seq(): pl.pallas_call(gather_kernel, out_shape=jax.ShapeDtypeStruct(shape, x.dty...  22.8 us
    dot_general x1, matrix products, attend(): jnp.einsum('bhts,bshe->bthe', weights, value_blocks, preferred_element_ty...  8.82 us
    pallas_call x1, Pallas kernels, swap_cores(): pl.pallas_call(swap_kernel, out_shape=jax.ShapeDtypeStruct(x.shape, x.dty...  7.6 us
    dot_general x1, matrix products, per_device(): jnp.dot(hidden_rows, w_out, preferred_element_type=jnp.float32)  5.75 us
  transfers between devices with their start and end apart: 1, of which 1 were waited for; matrix products, arithmetic and copies ran while one was open for 1% of the time, Pallas kernels for 15%

profile of v4, /device:TPU:1, one launch (start us, length us, event | category | flops | bytes accessed | tf_op | source)
XLA Modules:
  0.0 269.2 jit_solution(14623691742765353737)
XLA Ops:
  6.5 0.0 copy-start
  6.5 0.0 all-gather.3.cloned.1.call-start
  6.5 0.7 all-gather.3.cloned.1.call-update
  7.3 39.7 %shard_map.64 = bf16[16,224,128]{2,1,0:T(8,128)(2,1)} custom-call(bf16[16,224,128]{2,1,0:T(8,128)(2,1)} %bitcast.101), custom_call_target="tpu_custom_call" | custom-call | tf_op jit(solution)/shard_map/pallas_call | solution.py:76
  47.0 0.8 dynamic_slice.3
  47.7 1.2 iota_compare_fusion
  48.9 1.3 copy_bitcast_fusion
  50.2 28.3 %all-gather.3.cloned.1.call-done = bf16[16384,128]{1,0:T(8,128)(2,1)} async-done(((bf16[2048,128]{1,0:T(8,128)(2,1)}), bf16[16384,128]{1,0:T(8,128)(2,1)}) %all-gather.3.cloned.1.call-update) | async-done | bytes 4194320 | tf_op jit(solution)/shard_map/all_gather | solution.py:236
  78.5 7.6 %shard_map.65 = bf16[8,2048,128]{2,1,0:T(8,128)(2,1)} custom-call(bf16[8,2048,128]{2,1,0:T(8,128)(2,1)} %bitcast.92), custom_call_target="tpu_custom_call" | custom-call | tf_op jit(solution)/shard_map/pallas_call | solution.py:167
  86.1 0.0 copy-start.2
  86.2 3.5 %convolution_bitcast_fusion.1 = bf16[224,8,1,128]{3,0,1,2:T(8,128)(2,1)S(1)} fusion(bf16[8,2048,128]{2,1,0:T(8,128)(2,1)} %bitcast.93, bf16[224,2048]{1,0:T(8,128)(2,1)S(1)} %copy_bitcast_fusion), kind=kOutput, calls=%fused_computation.19 | convolution fusion | flops 939524096 | bytes 5570560 | tf_op jit(solution)/shard_map/tf,zfe->tze/dot_general | solution.py:243
  89.6 0.0 copy-done.2
  89.6 1.1 convolution_bitcast_fusion
  90.8 0.0 copy-start.5
  90.8 0.2 fusion.1
  91.0 1.0 copy.21
  91.9 0.0 copy-done
  91.9 0.4 convolution_convert_fusion.2
  92.4 0.1 copy.19
  92.5 1.3 copy.22
  93.8 0.0 copy-done.5
  93.8 0.4 convolution_convert_fusion.1
  94.2 0.1 copy.20
  94.3 1.3 copy.23
  95.5 3.4 %maximum_bitcast_fusion = bf16[16,224,160]{2,1,0:T(8,128)(2,1)S(1)} fusion(bf16[224,16,128]{2,0,1:T(8,128)(2,1)} %bitcast.100, bf16[224,16,16]{2,0,1:T(8,128)(2,1)} %copy.23, bf16[224,16,16]{2,0,1:T(8,128)(2,1)} %copy.22), kind=kLoop, calls=%fused_computation.9 | loop fusion | flops 3440640 | bytes 2293760 | tf_op jit(solution)/shard_map/transpose | solution.py:257
  98.9 3.8 %reshape.231.x_ref = bf16[16,280,128]{2,1,0:T(8,128)(2,1)} reshape(bf16[16,224,160]{2,1,0:T(8,128)(2,1)S(1)} %maximum_bitcast_fusion) | data formatting | bytes 2293760 | tf_op jit(solution)/shard_map/reshape | solution.py:257
  102.7 33.1 %shard_map.66 = bf16[16,280,128]{2,1,0:T(8,128)(2,1)} custom-call(bf16[16,280,128]{2,1,0:T(8,128)(2,1)} %reshape.231.x_ref), custom_call_target="tpu_custom_call" | custom-call | tf_op jit(solution)/shard_map/pallas_call | solution.py:76
  135.8 3.4 %reshape.232 = bf16[3584,1,160]{2,0,1:T(8,128)(2,1)S(1)} reshape(bf16[16,280,128]{2,1,0:T(8,128)(2,1)} %shard_map.66) | data formatting | bytes 2293760 | tf_op jit(solution)/shard_map/reshape | solution.py:258
  139.3 0.0 copy-start.1
  139.3 1.2 copy-done.1
  140.5 1.6 fusion.26
  142.2 1.8 slice.28
  144.0 1.5 copy.27
  145.5 0.5 convolution_bitcast_fusion.3
  146.0 0.1 convert_reduce_fusion
  146.2 0.4 multiply_multiply_fusion.1
  146.6 0.0 copy-start.4
  146.6 1.8 convolution_bitcast_fusion.2
  148.4 0.7 fusion.10.x_ref
  149.1 0.1 fusion.11
  149.1 22.8 %shard_map.67 = bf16[16,273,128]{2,1,0:T(8,128)(2,1)} custom-call(bf16[273,128]{1,0:T(8,128)(2,1)} %fusion.10.x_ref), custom_call_target="tpu_custom_call" | custom-call | tf_op jit(solution)/shard_map/pallas_call | solution.py:133
  172.0 0.8 slice.31
  172.8 0.0 copy-done.4
  172.8 0.3 copy.26
  173.1 1.6 select_reduce_fusion
  174.7 1.0 pad_add_fusion
  175.7 2.9 %fusion.12 = f32[4,128,896]{2,1,0:T(8,128)} fusion(bf16[4,896,16]{1,2,0:T(8,128)(2,1)S(1)} %copy.26, f32[4,1,273,128]{3,2,0,1:T(8,128)S(1)} %pad_add_fusion), kind=kOutput, calls=%fused_computation.36 | convolution fusion | flops 88195072 | bytes 1982464 | tf_op jit(solution)/shard_map/bthf,bhfe->bthe/dot_general | solution.py:212
  178.6 0.4 multiply_multiply_fusion
  179.0 0.0 copy-start.3
  179.0 3.5 %fusion.9 = f32[4,128,896]{2,1,0:T(8,128)} fusion(f32[4,896,256]{1,2,0:T(8,128)S(1)} %bitcast.90, f32[4,1,273,128]{3,2,0,1:T(8,128)S(1)} %pad_add_fusion), kind=kOutput, calls=%fused_computation.33 | convolution fusion | flops 1409286144 | bytes 6029312 | tf_op jit(solution)/shard_map/bthf,bhfe->bthe/dot_general | solution.py:215
  182.5 0.0 copy-done.3
  182.5 8.8 %multiply_reduce_fusion = (f32[4,896]{1,0:T(4,128)S(1)}, f32[4,896,1,128]{1,3,0,2:T(8,128)}) fusion(f32[4,128,896]{2,1,0:T(8,128)} %fusion.9, f32[4,128,896]{2,1,0:T(8,128)} %fusion.12, f32[4,128]{1,0:T(4,128)S(1)} %bitcast.106, bf16[4,896,128]{2,1,0:T(8,128)(2,1)S(1)} %bitcast.88, bf16[4,896,16]{2,1,0:T(8,128)(2,1)} %bitcast.96, ...), kind=kOutput, calls=%fused_computation.15 | convolution fusion | flops 949613056 | bytes 7471104 | tf_op jit(solution)/shard_map/bhts,bshe->bthe/dot_general | solution.py:224
  191.3 1.8 copy.33
  193.2 0.1 rsqrt.12
  193.2 1.5 multiply_convert_fusion.x_ref
  194.7 30.6 %shard_map.68 = bf16[16,224,128]{2,1,0:T(8,128)(2,1)} custom-call(bf16[16,224,128]{2,1,0:T(8,128)(2,1)} %multiply_convert_fusion.x_ref), custom_call_target="tpu_custom_call" | custom-call | tf_op jit(solution)/shard_map/pallas_call | solution.py:76
  225.4 5.7 %fusion.4 = bf16[28,16,8,128]{3,2,1,0:T(8,128)(2,1)S(1)} fusion(bf16[2048,2048]{1,0:T(8,128)(2,1)} %param.10, bf16[16,224,128]{2,1,0:T(8,128)(2,1)} %shard_map.68), kind=kOutput, calls=%fused_computation.17 | convolution fusion | flops 1879506944 | bytes 10223616 | tf_op jit(solution)/shard_map/dot_general | solution.py:270
  231.1 1.1 copy.54
  232.2 28.0 %shard_map.69 = bf16[16,224,128]{2,1,0:T(8,128)(2,1)} custom-call(bf16[16,224,128]{2,1,0:T(8,128)(2,1)} %bitcast.98), custom_call_target="tpu_custom_call" | custom-call | tf_op jit(solution)/shard_map/pallas_call | solution.py:76
  260.2 2.2 copy.56
  (5 shorter events, 0.1 us)
Async XLA Ops:
  6.5 85.4 %copy-start = (bf16[2048,256]{1,0:T(8,128)(2,1)S(1)}, bf16[2048,256]{1,0:T(8,128)(2,1)}, u32[]{:S(2)}) copy-start(bf16[2048,256]{1,0:T(8,128)(2,1)} %param.7) | copy-start | bytes 3145732
  6.5 72.0 %all-gather.3.cloned.1.call-start = ((), (), s32[]{:S(2)}) async-start(), calls=%async_computation | async-start | bytes 4718592 | tf_op jit(solution)/shard_map/all_gather | solution.py:236
  86.1 3.5 %copy-start.2 = (bf16[8,2048,128]{2,1,0:T(8,128)(2,1)S(1)}, bf16[8,2048,128]{2,1,0:T(8,128)(2,1)}, u32[]{:S(2)}) copy-start(bf16[8,2048,128]{2,1,0:T(8,128)(2,1)} %shard_map.65) | copy-start | bytes 12582916
  90.8 3.0 %copy-start.5 = (bf16[2048,256]{1,0:T(8,128)(2,1)S(1)}, bf16[2048,256]{1,0:T(8,128)(2,1)}, u32[]{:S(2)}) copy-start(bf16[2048,256]{1,0:T(8,128)(2,1)} %param.8) | copy-start | bytes 3145732
  139.3 1.3 copy-start.1
  146.6 26.2 %copy-start.4 = (bf16[3584,1,16]{2,0,1:T(8,128)(2,1)S(1)}, bf16[3584,1,16]{2,0,1:T(8,128)(2,1)}, u32[]{:S(2)}) copy-start(bf16[3584,1,16]{2,0,1:T(8,128)(2,1)} %get-tuple-element.10) | copy-start | bytes 344068
  179.0 3.5 %copy-start.3 = (bf16[3584,1,16]{2,0,1:T(8,128)(2,1)S(1)}, bf16[3584,1,16]{2,0,1:T(8,128)(2,1)}, u32[]{:S(2)}) copy-start(bf16[3584,1,16]{2,0,1:T(8,128)(2,1)} %get-tuple-element.9) | copy-start | bytes 344068
Sparse Core Ops, SparseCore 0:
  9.1 69.3 all-gather.2

commit v5 on v4

--- a/solution.py
+++ b/solution.py
@@ -172,6 +172,125 @@
         scratch_shapes=[pltpu.SemaphoreType.DMA(()), pltpu.SemaphoreType.DMA(())],
         compiler_params=pltpu.CompilerParams(collective_id=collective_id, has_side_effects=True),
     )(x)
+
+
+def opening_kernel(x_ref, w_ref, y_ref, w_all, buf, send_sem, recv_sem, own_sem, w_send, w_recv, w_own):
+    n = x_ref.shape[0]
+    cores = lax.axis_size("core")
+    ring = n // cores
+    me = chan_index()
+    slab = lax.axis_index("seq")
+    z = lax.axis_index("z")
+    core = lax.axis_index("core")
+    barrier = pltpu.get_barrier_semaphore()
+    for step in range(1, n):
+        peer = lax.rem(me + step, n)
+        pl.semaphore_signal(barrier, inc=1, device_id=chan_device(slab, peer), device_id_type=MESH)
+    pl.semaphore_wait(barrier, n - 1)
+    own = pltpu.make_async_copy(x_ref.at[me], buf.at[me], own_sem)
+    own.start()
+    sends = []
+    for step in range(1, n):
+        peer = lax.rem(me + step, n)
+        copy = pltpu.make_async_remote_copy(
+            src_ref=x_ref.at[peer],
+            dst_ref=buf.at[me],
+            send_sem=send_sem.at[peer],
+            recv_sem=recv_sem.at[me],
+            device_id=chan_device(slab, peer),
+            device_id_type=MESH,
+        )
+        copy.start()
+        sends.append(copy)
+    w_local = pltpu.make_async_copy(w_ref, w_all.at[me], w_own)
+    w_local.start()
+    right = (slab, lax.rem(z + 1, ring), core)
+    left = (slab, lax.rem(z + ring - 1, ring), core)
+    partner = (slab, z, cores - 1 - core)
+
+    def slot(origin):
+        return lax.rem(origin + ring, ring) * cores + core
+
+    def send(source, h, kind, target):
+        copy = pltpu.make_async_remote_copy(
+            src_ref=source,
+            dst_ref=w_all.at[h],
+            send_sem=w_send.at[h, kind],
+            recv_sem=w_recv.at[h],
+            device_id=target,
+            device_id_type=MESH,
+        )
+        copy.start()
+        sends.append(copy)
+
+    def arrive(h, source):
+        pltpu.make_async_remote_copy(
+            src_ref=w_ref,
+            dst_ref=w_all.at[h],
+            send_sem=w_send.at[h, 0],
+            recv_sem=w_recv.at[h],
+            device_id=source,
+            device_id_type=MESH,
+        ).wait_recv()
+
+    rightward = ring // 2
+    leftward = ring - 1 - rightward
+    send(w_ref, me, 0, right)
+    if leftward > 0:
+        send(w_ref, me, 1, left)
+    send(w_ref, me, 2, partner)
+    for step in range(1, rightward + 1):
+        h = slot(z - step)
+        arrive(h, left)
+        if step < rightward:
+            send(w_all.at[h], h, 0, right)
+        send(w_all.at[h], h, 2, partner)
+        if step <= leftward:
+            h = slot(z + step)
+            arrive(h, right)
+            if step < leftward:
+                send(w_all.at[h], h, 1, left)
+            send(w_all.at[h], h, 2, partner)
+    for origin in range(ring):
+        arrive(origin * cores + (cores - 1 - core), partner)
+    for step in range(1, n):
+        source = lax.rem(me + n - step, n)
+        pltpu.make_async_remote_copy(
+            src_ref=x_ref.at[source],
+            dst_ref=buf.at[source],
+            send_sem=send_sem.at[source],
+            recv_sem=recv_sem.at[source],
+            device_id=chan_device(slab, source),
+            device_id_type=MESH,
+        ).wait_recv()
+    for copy in sends:
+        copy.wait_send()
+    own.wait()
+    w_local.wait()
+    y_ref[...] = buf[...]
+
+
+def opening(x, w, collective_id):
+    n = x.shape[0]
+    return pl.pallas_call(
+        opening_kernel,
+        out_shape=(
+            jax.ShapeDtypeStruct(x.shape, x.dtype),
+            jax.ShapeDtypeStruct((n,) + w.shape, w.dtype),
+        ),
+        in_specs=[pl.BlockSpec(memory_space=pltpu.VMEM), pl.BlockSpec(memory_space=pl.ANY)],
+        out_specs=(pl.BlockSpec(memory_space=pltpu.VMEM), pl.BlockSpec(memory_space=pl.ANY)),
+        scratch_shapes=[
+            pltpu.VMEM(x.shape, x.dtype),
+            pltpu.SemaphoreType.DMA((n,)),
+            pltpu.SemaphoreType.DMA((n,)),
+            pltpu.SemaphoreType.DMA(()),
+            pltpu.SemaphoreType.DMA((n, 3)),
+            pltpu.SemaphoreType.DMA((n,)),
+            pltpu.SemaphoreType.DMA(()),
+        ],
+        compiler_params=pltpu.CompilerParams(collective_id=collective_id, has_side_effects=True),
+    )(x, w)
 
 
 def split_rows(x, groups, collective_id):
@@ -233,21 +352,13 @@
     per_group = HEADS // groups
     my_group = chan_index()
     my_slab = lax.axis_index("seq")
-    value_z = lax.all_gather(w_value, "z", axis=0)
-    rows = split_rows(tokens, groups, 1)
-    value_z, rows = lax.optimization_barrier((value_z, rows))
-    value_other = swap_cores(value_z, 6)
+    tok_rows_total, tok_cols = tokens.shape
+    got, value_all = opening(tokens.reshape(groups, tok_rows_total // groups, tok_cols), w_value, 1)
+    rows = got.transpose(1, 0, 2).reshape(tok_rows_total // groups, groups * tok_cols)
     chunk = rows.shape[0]
     query = jnp.dot(rows, w_query, preferred_element_type=jnp.float32).astype(jnp.bfloat16)
     key = jnp.dot(rows, w_key, preferred_element_type=jnp.float32).astype(jnp.bfloat16)
-    value_mine = jnp.einsum("tf,zfe->tze", rows, value_z, preferred_element_type=jnp.float32)
-    value_pair = jnp.einsum("tf,zfe->tze", rows, value_other, preferred_element_type=jnp.float32)
-    first = lax.axis_index("core") == 0
-    value = jnp.where(
-        first,
-        jnp.stack([value_mine, value_pair], axis=2),
-        jnp.stack([value_pair, value_mine], axis=2),
-    )
+    value = jnp.einsum("tf,hfe->the", rows, value_all, preferred_element_type=jnp.float32)
     value = value.astype(jnp.bfloat16).reshape(chunk, groups, per_group * HEAD_DIM)
     query = query.reshape(chunk, groups, per_group * FEAT)
     key = key.reshape(chunk, groups, per_group * FEAT)

time: 270 us -> 263 us (0.974)
  Pallas kernels: 162 us -> 197 us
  waiting for transfers between devices: 29 us -> 0 us
  between operations: 13.7 us -> 0.24 us
    pallas_call x1, Pallas kernels: 7.6 us -> 83.7 us  [opening(): pl.pallas_call(opening_kernel, out_shape=(jax.ShapeDtypeStruct(x.shape, x...]
    pallas_call x4 -> x3, Pallas kernels: 131 us -> 88.3 us  [exchange(): pl.pallas_call(exchange_kernel, out_shape=jax.ShapeDtypeStruct(x.shape, x...]
    all_gather x1 -> x0, waiting for transfers between devices: 28.3 us -> none  [per_device(): value_z = lax.all_gather(w_value, 'z', axis=0)]
    dot_general x2 -> x1, matrix products: 4.6 us -> 6.45 us  [per_device(): jnp.einsum('tf,hfe->the', rows, value_all, preferred_element_type=jnp.flo...]
  transfers between devices with their start and end apart: 1 -> 0, of which waited for: 1 -> 0; matrix products, arithmetic and copies ran while one was open for 1% -> 0% of each run, Pallas kernels for 15% -> 0%
where the time goes in v5:
time: 263 us; the launch traced here: 262 us
  Pallas kernels  197 us (75%)
  matrix products  31.4 us (12%)
  local copies, waits for them, and re-layouts  23.3 us (9%)
  other arithmetic  10 us (4%)
    pallas_call x3, Pallas kernels, exchange(): pl.pallas_call(exchange_kernel, out_shape=jax.ShapeDtypeStruct(x.shape, x...  88.3 us
    pallas_call x1, Pallas kernels, opening(): pl.pallas_call(opening_kernel, out_shape=(jax.ShapeDtypeStruct(x.shape, x...  83.7 us
    pallas_call x1, Pallas kernels, gather_seq(): pl.pallas_call(gather_kernel, out_shape=jax.ShapeDtypeStruct(shape, x.dty...  24.9 us
    dot_general x1, matrix products, attend(): jnp.einsum('bhts,bshe->bthe', weights, value_blocks, preferred_element_ty...  8.82 us
    dot_general x1, matrix products, per_device(): jnp.einsum('tf,hfe->the', rows, value_all, preferred_element_type=jnp.flo...  6.45 us
    dot_general x1, matrix products, per_device(): jnp.dot(hidden_rows, w_out, preferred_element_type=jnp.float32)  5.75 us

profile of v5, /device:TPU:1, one launch (start us, length us, event | category | flops | bytes accessed | tf_op | source)
XLA Modules:
  0.0 261.9 jit_solution(17040707594303348296)
XLA Ops:
  0.0 0.0 copy-start
  0.0 83.7 %shard_map.64 = (bf16[16,224,128]{2,1,0:T(8,128)(2,1)}, bf16[16,2048,128]{2,1,0:T(8,128)(2,1)}) custom-call(bf16[16,224,128]{2,1,0:T(8,128)(2,1)} %bitcast.93, bf16[2048,128]{1,0:T(8,128)(2,1)} %w_ref.1), custom_call_target="tpu_custom_call" | custom-call | tf_op jit(solution)/shard_map/pallas_call | solution.py:275
  83.7 1.5 copy.18
  85.3 0.4 reshape.236
  85.7 0.0 copy-start.5
  85.7 6.4 %convolution_convert_fusion.1 = bf16[224,16,128]{2,0,1:T(8,128)(2,1)} fusion(bf16[224,2048,1]{1,0,2:T(8,128)(2,1)S(1)} %reshape.236, bf16[16,2048,128]{2,1,0:T(8,128)(2,1)} %get-tuple-element.8), kind=kOutput, calls=%fused_computation.15 | convolution fusion | flops 1879506944 | bytes 10223616 | tf_op jit(solution)/shard_map/tf,hfe->the/dot_general | solution.py:361
  92.1 0.0 copy-done
  92.1 0.0 copy-done.5
  92.1 0.0 copy-start.6
  92.1 0.4 convolution_convert_fusion.3
  92.5 0.1 copy.19
  92.6 1.3 copy.21
  93.9 0.0 copy-done.6
  93.9 0.4 convolution_convert_fusion.2
  94.3 0.1 copy.20
  94.5 1.3 copy.22
  95.7 3.4 %maximum_bitcast_fusion = bf16[16,224,160]{2,1,0:T(8,128)(2,1)S(1)} fusion(bf16[224,16,128]{2,0,1:T(8,128)(2,1)} %convolution_convert_fusion.1, bf16[224,16,16]{2,0,1:T(8,128)(2,1)} %copy.22, bf16[224,16,16]{2,0,1:T(8,128)(2,1)} %copy.21), kind=kLoop, calls=%fused_computation.7 | loop fusion | flops 3440640 | bytes 2293760 | tf_op jit(solution)/shard_map/transpose | solution.py:368
  99.1 3.8 %reshape.225.x_ref = bf16[16,280,128]{2,1,0:T(8,128)(2,1)} reshape(bf16[16,224,160]{2,1,0:T(8,128)(2,1)S(1)} %maximum_bitcast_fusion) | data formatting | bytes 2293760 | tf_op jit(solution)/shard_map/reshape | solution.py:368
  102.9 32.8 %shard_map.65 = bf16[16,280,128]{2,1,0:T(8,128)(2,1)} custom-call(bf16[16,280,128]{2,1,0:T(8,128)(2,1)} %reshape.225.x_ref), custom_call_target="tpu_custom_call" | custom-call | tf_op jit(solution)/shard_map/pallas_call | solution.py:76
  135.7 3.4 %reshape.226 = bf16[3584,1,160]{2,0,1:T(8,128)(2,1)S(1)} reshape(bf16[16,280,128]{2,1,0:T(8,128)(2,1)} %shard_map.65) | data formatting | bytes 2293760 | tf_op jit(solution)/shard_map/reshape | solution.py:369
  139.2 0.0 copy-start.1
  139.2 1.8 fusion.27
  141.0 0.0 copy-done.1
  141.0 1.5 copy.26
  142.5 1.9 slice.28
  144.3 0.5 convolution_bitcast_fusion.1
  144.9 0.4 multiply_multiply_fusion.1
  145.2 1.8 convolution_bitcast_fusion
  147.0 0.0 copy-start.3
  147.1 0.1 convert_reduce_fusion
  147.2 0.7 fusion.11.x_ref
  147.9 24.9 %shard_map.66 = bf16[16,273,128]{2,1,0:T(8,128)(2,1)} custom-call(bf16[273,128]{1,0:T(8,128)(2,1)} %fusion.11.x_ref), custom_call_target="tpu_custom_call" | custom-call | tf_op jit(solution)/shard_map/pallas_call | solution.py:133
  172.8 1.6 select_reduce_fusion
  174.4 0.1 fusion.12
  174.5 0.9 pad_add_fusion
  175.3 0.0 copy-done.3
  175.3 0.3 copy.25
  175.6 0.0 copy-start.4
  175.6 3.8 %fusion.13 = f32[4,128,896]{2,1,0:T(8,128)} fusion(bf16[4,896,16]{1,2,0:T(8,128)(2,1)S(1)} %copy.25, f32[4,1,273,128]{3,2,0,1:T(8,128)} %pad_add_fusion), kind=kOutput, calls=%fused_computation.34 | convolution fusion | flops 88195072 | bytes 1982464 | tf_op jit(solution)/shard_map/bthf,bhfe->bthe/dot_general | solution.py:331
  179.4 0.4 multiply_multiply_fusion
  179.8 0.0 copy-start.2
  179.8 0.0 copy-done.4
  179.8 3.5 %fusion.10 = f32[4,128,896]{2,1,0:T(8,128)} fusion(f32[4,896,256]{1,2,0:T(8,128)S(1)} %bitcast.84, f32[4,1,273,128]{3,2,0,1:T(8,128)S(1)} %copy-done.4), kind=kOutput, calls=%fused_computation.31 | convolution fusion | flops 1409286144 | bytes 6029312 | tf_op jit(solution)/shard_map/bthf,bhfe->bthe/dot_general | solution.py:334
  183.3 1.1 iota_compare_fusion
  184.4 0.0 copy-done.2
  184.4 8.8 %multiply_reduce_fusion = (f32[4,896]{1,0:T(4,128)S(1)}, f32[4,896,1,128]{1,3,0,2:T(8,128)}) fusion(f32[4,128,896]{2,1,0:T(8,128)} %fusion.10, f32[4,128,896]{2,1,0:T(8,128)} %fusion.13, f32[4,128]{1,0:T(4,128)S(1)} %bitcast.98, bf16[4,896,128]{2,1,0:T(8,128)(2,1)S(1)} %bitcast.82, bf16[4,896,16]{2,1,0:T(8,128)(2,1)} %bitcast.88, ...), kind=kOutput, calls=%fused_computation.13 | convolution fusion | flops 949613056 | bytes 7471104 | tf_op jit(solution)/shard_map/bhts,bshe->bthe/dot_general | solution.py:343
  193.3 1.8 copy.32
  195.1 0.1 rsqrt.12
  195.2 0.8 dynamic_slice.3
  195.9 1.5 multiply_convert_fusion.x_ref
  197.4 26.9 %shard_map.67 = bf16[16,224,128]{2,1,0:T(8,128)(2,1)} custom-call(bf16[16,224,128]{2,1,0:T(8,128)(2,1)} %multiply_convert_fusion.x_ref), custom_call_target="tpu_custom_call" | custom-call | tf_op jit(solution)/shard_map/pallas_call | solution.py:76
  224.3 5.7 %fusion.3 = bf16[28,16,8,128]{3,2,1,0:T(8,128)(2,1)S(1)} fusion(bf16[2048,2048]{1,0:T(8,128)(2,1)} %param.10, bf16[16,224,128]{2,1,0:T(8,128)(2,1)} %shard_map.67), kind=kOutput, calls=%fused_computation.16 | convolution fusion | flops 1879506944 | bytes 10223616 | tf_op jit(solution)/shard_map/dot_general | solution.py:381
  230.1 1.1 copy.60
  231.2 28.5 %shard_map.68 = bf16[16,224,128]{2,1,0:T(8,128)(2,1)} custom-call(bf16[16,224,128]{2,1,0:T(8,128)(2,1)} %bitcast.90), custom_call_target="tpu_custom_call" | custom-call | tf_op jit(solution)/shard_map/pallas_call | solution.py:76
  259.7 2.2 copy.62
  (6 shorter events, 0.1 us)
Async XLA Ops:
  0.0 92.1 %copy-start = (bf16[2048,256]{1,0:T(8,128)(2,1)S(1)}, bf16[2048,256]{1,0:T(8,128)(2,1)}, u32[]{:S(2)}) copy-start(bf16[2048,256]{1,0:T(8,128)(2,1)} %param.7) | copy-start | bytes 3145732
  85.7 6.5 %copy-start.5 = (bf16[16,224,128]{2,1,0:T(8,128)(2,1)S(1)}, bf16[16,224,128]{2,1,0:T(8,128)(2,1)}, u32[]{:S(2)}) copy-start(bf16[16,224,128]{2,1,0:T(8,128)(2,1)} %get-tuple-element.7) | copy-start | bytes 2752516
  92.1 1.8 copy-start.6
  139.2 1.8 copy-start.1
  147.0 28.3 %copy-start.3 = (bf16[3584,1,16]{2,0,1:T(8,128)(2,1)S(1)}, bf16[3584,1,16]{2,0,1:T(8,128)(2,1)}, u32[]{:S(2)}) copy-start(bf16[3584,1,16]{2,0,1:T(8,128)(2,1)} %get-tuple-element.10) | copy-start | bytes 344068
  175.6 4.2 %copy-start.4 = (f32[4,1,273,128]{3,2,0,1:T(8,128)S(1)}, f32[4,1,273,128]{3,2,0,1:T(8,128)}, u32[]{:S(2)}) copy-start(f32[4,1,273,128]{3,2,0,1:T(8,128)} %pad_add_fusion) | copy-start | bytes 1677316
  179.8 4.7 %copy-start.2 = (bf16[3584,1,16]{2,0,1:T(8,128)(2,1)S(1)}, bf16[3584,1,16]{2,0,1:T(8,128)(2,1)}, u32[]{:S(2)}) copy-start(bf16[3584,1,16]{2,0,1:T(8,128)(2,1)} %get-tuple-element.9) | copy-start | bytes 344068

commit v6 on v5

--- a/solution.py
+++ b/solution.py
@@ -7,6 +7,7 @@
 
 MESH = pl.DeviceIdType.MESH
 CHAN = ("z", "core")
+W_PIECES = 4
 
 
 def chan_index():
@@ -208,51 +209,61 @@
     left = (slab, lax.rem(z + ring - 1, ring), core)
     partner = (slab, z, cores - 1 - core)
 
+    pieces = W_PIECES
+    depth = w_ref.shape[0] // pieces
+
     def slot(origin):
         return lax.rem(origin + ring, ring) * cores + core
 
-    def send(source, h, kind, target):
+    def held(h, j):
+        return w_all.at[h, pl.ds(j * depth, depth)]
+
+    def send(source, h, j, kind, target):
         copy = pltpu.make_async_remote_copy(
             src_ref=source,
-            dst_ref=w_all.at[h],
-            send_sem=w_send.at[h, kind],
-            recv_sem=w_recv.at[h],
+            dst_ref=held(h, j),
+            send_sem=w_send.at[h, kind, j],
+            recv_sem=w_recv.at[h, j],
             device_id=target,
             device_id_type=MESH,
         )
         copy.start()
         sends.append(copy)
 
-    def arrive(h, source):
+    def arrive(h, j, source):
         pltpu.make_async_remote_copy(
-            src_ref=w_ref,
-            dst_ref=w_all.at[h],
-            send_sem=w_send.at[h, 0],
-            recv_sem=w_recv.at[h],
+            src_ref=w_ref.at[pl.ds(j * depth, depth)],
+            dst_ref=held(h, j),
+            send_sem=w_send.at[h, 0, j],
+            recv_sem=w_recv.at[h, j],
             device_id=source,
             device_id_type=MESH,
         ).wait_recv()
 
     rightward = ring // 2
     leftward = ring - 1 - rightward
-    send(w_ref, me, 0, right)
-    if leftward > 0:
-        send(w_ref, me, 1, left)
-    send(w_ref, me, 2, partner)
+    for j in range(pieces):
+        mine = w_ref.at[pl.ds(j * depth, depth)]
+        send(mine, me, j, 0, right)
+        if leftward > 0:
+            send(mine, me, j, 1, left)
+        send(mine, me, j, 2, partner)
     for step in range(1, rightward + 1):
-        h = slot(z - step)
-        arrive(h, left)
-        if step < rightward:
-            send(w_all.at[h], h, 0, right)
-        send(w_all.at[h], h, 2, partner)
-        if step <= leftward:
-            h = slot(z + step)
-            arrive(h, right)
-            if step < leftward:
-                send(w_all.at[h], h, 1, left)
-            send(w_all.at[h], h, 2, partner)
+        for j in range(pieces):
+            h = slot(z - step)
+            arrive(h, j, left)
+            if step < rightward:
+                send(held(h, j), h, j, 0, right)
+            send(held(h, j), h, j, 2, partner)
+            if step <= leftward:
+                h = slot(z + step)
+                arrive(h, j, right)
+                if step < leftward:
+                    send(held(h, j), h, j, 1, left)
+                send(held(h, j), h, j, 2, partner)
     for origin in range(ring):
-        arrive(origin * cores + (cores - 1 - core), partner)
+        for j in range(pieces):
+            arrive(origin * cores + (cores - 1 - core), j, partner)
     for step in range(1, n):
         source = lax.rem(me + n - step, n)
         pltpu.make_async_remote_copy(
@@ -285,8 +296,8 @@
             pltpu.SemaphoreType.DMA((n,)),
             pltpu.SemaphoreType.DMA((n,)),
             pltpu.SemaphoreType.DMA(()),
-            pltpu.SemaphoreType.DMA((n, 3)),
-            pltpu.SemaphoreType.DMA((n,)),
+            pltpu.SemaphoreType.DMA((n, 3, W_PIECES)),
+            pltpu.SemaphoreType.DMA((n, W_PIECES)),
             pltpu.SemaphoreType.DMA(()),
         ],
         compiler_params=pltpu.CompilerParams(collective_id=collective_id, has_side_effects=True),

time: 263 us -> 260 us (0.989)
  Pallas kernels: 197 us -> 194 us
where the time goes in v6:
time: 260 us; the launch traced here: 259 us
  Pallas kernels  194 us (75%)
  matrix products  31.4 us (12%)
  local copies, waits for them, and re-layouts  23.3 us (9%)
  other arithmetic  10 us (4%)
    pallas_call x3, Pallas kernels, exchange(): pl.pallas_call(exchange_kernel, out_shape=jax.ShapeDtypeStruct(x.shape, x...  89.6 us
    pallas_call x1, Pallas kernels, opening(): pl.pallas_call(opening_kernel, out_shape=(jax.ShapeDtypeStruct(x.shape, x...  81.3 us
    pallas_call x1, Pallas kernels, gather_seq(): pl.pallas_call(gather_kernel, out_shape=jax.ShapeDtypeStruct(shape, x.dty...  23 us
    dot_general x1, matrix products, attend(): jnp.einsum('bhts,bshe->bthe', weights, value_blocks, preferred_element_ty...  8.84 us
    dot_general x1, matrix products, per_device(): jnp.einsum('tf,hfe->the', rows, value_all, preferred_element_type=jnp.flo...  6.45 us
    dot_general x1, matrix products, per_device(): jnp.dot(hidden_rows, w_out, preferred_element_type=jnp.float32)  5.75 us

profile of v6, /device:TPU:1, one launch (start us, length us, event | category | flops | bytes accessed | tf_op | source)
XLA Modules:
  0.0 258.9 jit_solution(11490407515723107024)
XLA Ops:
  0.0 0.0 copy-start
  0.0 81.3 %shard_map.64 = (bf16[16,224,128]{2,1,0:T(8,128)(2,1)}, bf16[16,2048,128]{2,1,0:T(8,128)(2,1)}) custom-call(bf16[16,224,128]{2,1,0:T(8,128)(2,1)} %bitcast.93, bf16[2048,128]{1,0:T(8,128)(2,1)} %w_ref.1), custom_call_target="tpu_custom_call" | custom-call | tf_op jit(solution)/shard_map/pallas_call | solution.py:286
  81.3 1.5 copy.18
  82.8 0.4 reshape.236
  83.2 0.0 copy-start.5
  83.2 6.4 %convolution_convert_fusion.1 = bf16[224,16,128]{2,0,1:T(8,128)(2,1)} fusion(bf16[224,2048,1]{1,0,2:T(8,128)(2,1)S(1)} %reshape.236, bf16[16,2048,128]{2,1,0:T(8,128)(2,1)} %get-tuple-element.8), kind=kOutput, calls=%fused_computation.15 | convolution fusion | flops 1879506944 | bytes 10223616 | tf_op jit(solution)/shard_map/tf,hfe->the/dot_general | solution.py:372
  89.7 0.0 copy-done
  89.7 0.0 copy-done.5
  89.7 0.0 copy-start.6
  89.7 0.4 convolution_convert_fusion.3
  90.1 0.1 copy.19
  90.2 1.3 copy.21
  91.5 0.0 copy-done.6
  91.5 0.4 convolution_convert_fusion.2
  91.9 0.1 copy.20
  92.0 1.3 copy.22
  93.3 3.4 %maximum_bitcast_fusion = bf16[16,224,160]{2,1,0:T(8,128)(2,1)S(1)} fusion(bf16[224,16,128]{2,0,1:T(8,128)(2,1)} %convolution_convert_fusion.1, bf16[224,16,16]{2,0,1:T(8,128)(2,1)} %copy.22, bf16[224,16,16]{2,0,1:T(8,128)(2,1)} %copy.21), kind=kLoop, calls=%fused_computation.7 | loop fusion | flops 3440640 | bytes 2293760 | tf_op jit(solution)/shard_map/transpose | solution.py:379
  96.6 3.8 %reshape.225.x_ref = bf16[16,280,128]{2,1,0:T(8,128)(2,1)} reshape(bf16[16,224,160]{2,1,0:T(8,128)(2,1)S(1)} %maximum_bitcast_fusion) | data formatting | bytes 2293760 | tf_op jit(solution)/shard_map/reshape | solution.py:379
  100.5 33.2 %shard_map.65 = bf16[16,280,128]{2,1,0:T(8,128)(2,1)} custom-call(bf16[16,280,128]{2,1,0:T(8,128)(2,1)} %reshape.225.x_ref), custom_call_target="tpu_custom_call" | custom-call | tf_op jit(solution)/shard_map/pallas_call | solution.py:77
  133.7 3.4 %reshape.226 = bf16[3584,1,160]{2,0,1:T(8,128)(2,1)S(1)} reshape(bf16[16,280,128]{2,1,0:T(8,128)(2,1)} %shard_map.65) | data formatting | bytes 2293760 | tf_op jit(solution)/shard_map/reshape | solution.py:380
  137.1 0.0 copy-start.1
  137.1 1.8 fusion.27
  139.0 0.0 copy-done.1
  139.0 1.5 copy.26
  140.4 1.9 slice.28
  142.3 0.5 convolution_bitcast_fusion.1
  142.8 0.4 multiply_multiply_fusion.1
  143.2 1.8 convolution_bitcast_fusion
  145.0 0.0 copy-start.3
  145.0 0.1 convert_reduce_fusion
  145.1 0.7 fusion.11.x_ref
  145.8 23.0 %shard_map.66 = bf16[16,273,128]{2,1,0:T(8,128)(2,1)} custom-call(bf16[273,128]{1,0:T(8,128)(2,1)} %fusion.11.x_ref), custom_call_target="tpu_custom_call" | custom-call | tf_op jit(solution)/shard_map/pallas_call | solution.py:134
  168.8 1.6 select_reduce_fusion
  170.4 0.1 fusion.12
  170.5 0.9 pad_add_fusion
  171.4 0.0 copy-done.3
  171.4 0.3 copy.25
  171.7 0.0 copy-start.4
  171.7 3.8 %fusion.13 = f32[4,128,896]{2,1,0:T(8,128)} fusion(bf16[4,896,16]{1,2,0:T(8,128)(2,1)S(1)} %copy.25, f32[4,1,273,128]{3,2,0,1:T(8,128)} %pad_add_fusion), kind=kOutput, calls=%fused_computation.34 | convolution fusion | flops 88195072 | bytes 1982464 | tf_op jit(solution)/shard_map/bthf,bhfe->bthe/dot_general | solution.py:342
  175.5 0.4 multiply_multiply_fusion
  175.8 0.0 copy-start.2
  175.8 0.0 copy-done.4
  175.9 3.5 %fusion.10 = f32[4,128,896]{2,1,0:T(8,128)} fusion(f32[4,896,256]{1,2,0:T(8,128)S(1)} %bitcast.84, f32[4,1,273,128]{3,2,0,1:T(8,128)S(1)} %copy-done.4), kind=kOutput, calls=%fused_computation.31 | convolution fusion | flops 1409286144 | bytes 6029312 | tf_op jit(solution)/shard_map/bthf,bhfe->bthe/dot_general | solution.py:345
  179.4 1.1 iota_compare_fusion
  180.5 0.0 copy-done.2
  180.5 8.8 %multiply_reduce_fusion = (f32[4,896]{1,0:T(4,128)S(1)}, f32[4,896,1,128]{1,3,0,2:T(8,128)}) fusion(f32[4,128,896]{2,1,0:T(8,128)} %fusion.10, f32[4,128,896]{2,1,0:T(8,128)} %fusion.13, f32[4,128]{1,0:T(4,128)S(1)} %bitcast.98, bf16[4,896,128]{2,1,0:T(8,128)(2,1)S(1)} %bitcast.82, bf16[4,896,16]{2,1,0:T(8,128)(2,1)} %bitcast.88, ...), kind=kOutput, calls=%fused_computation.13 | convolution fusion | flops 949613056 | bytes 7471104 | tf_op jit(solution)/shard_map/bhts,bshe->bthe/dot_general | solution.py:354
  189.3 1.8 copy.32
  191.1 0.1 rsqrt.12
  191.2 0.8 dynamic_slice.3
  192.0 1.5 multiply_convert_fusion.x_ref
  193.5 28.6 %shard_map.67 = bf16[16,224,128]{2,1,0:T(8,128)(2,1)} custom-call(bf16[16,224,128]{2,1,0:T(8,128)(2,1)} %multiply_convert_fusion.x_ref), custom_call_target="tpu_custom_call" | custom-call | tf_op jit(solution)/shard_map/pallas_call | solution.py:77
  222.0 5.7 %fusion.3 = bf16[28,16,8,128]{3,2,1,0:T(8,128)(2,1)S(1)} fusion(bf16[2048,2048]{1,0:T(8,128)(2,1)} %param.10, bf16[16,224,128]{2,1,0:T(8,128)(2,1)} %shard_map.67), kind=kOutput, calls=%fused_computation.16 | convolution fusion | flops 1879506944 | bytes 10223616 | tf_op jit(solution)/shard_map/dot_general | solution.py:392
  227.8 1.1 copy.60
  228.9 27.9 %shard_map.68 = bf16[16,224,128]{2,1,0:T(8,128)(2,1)} custom-call(bf16[16,224,128]{2,1,0:T(8,128)(2,1)} %bitcast.90), custom_call_target="tpu_custom_call" | custom-call | tf_op jit(solution)/shard_map/pallas_call | solution.py:77
  256.7 2.2 copy.62
  (6 shorter events, 0.1 us)
Async XLA Ops:
  0.0 89.7 %copy-start = (bf16[2048,256]{1,0:T(8,128)(2,1)S(1)}, bf16[2048,256]{1,0:T(8,128)(2,1)}, u32[]{:S(2)}) copy-start(bf16[2048,256]{1,0:T(8,128)(2,1)} %param.7) | copy-start | bytes 3145732
  83.2 6.5 %copy-start.5 = (bf16[16,224,128]{2,1,0:T(8,128)(2,1)S(1)}, bf16[16,224,128]{2,1,0:T(8,128)(2,1)}, u32[]{:S(2)}) copy-start(bf16[16,224,128]{2,1,0:T(8,128)(2,1)} %get-tuple-element.7) | copy-start | bytes 2752516
  89.7 1.8 copy-start.6
  137.1 1.8 copy-start.1
  145.0 26.4 %copy-start.3 = (bf16[3584,1,16]{2,0,1:T(8,128)(2,1)S(1)}, bf16[3584,1,16]{2,0,1:T(8,128)(2,1)}, u32[]{:S(2)}) copy-start(bf16[3584,1,16]{2,0,1:T(8,128)(2,1)} %get-tuple-element.10) | copy-start | bytes 344068
  171.7 4.2 %copy-start.4 = (f32[4,1,273,128]{3,2,0,1:T(8,128)S(1)}, f32[4,1,273,128]{3,2,0,1:T(8,128)}, u32[]{:S(2)}) copy-start(f32[4,1,273,128]{3,2,0,1:T(8,128)} %pad_add_fusion) | copy-start | bytes 1677316
  175.8 4.7 %copy-start.2 = (bf16[3584,1,16]{2,0,1:T(8,128)(2,1)S(1)}, bf16[3584,1,16]{2,0,1:T(8,128)(2,1)}, u32[]{:S(2)}) copy-start(bf16[3584,1,16]{2,0,1:T(8,128)(2,1)} %get-tuple-element.9) | copy-start | bytes 344068

commit v7 on v6

--- a/solution.py
+++ b/solution.py
@@ -240,25 +240,34 @@
             device_id_type=MESH,
         ).wait_recv()
 
-    rightward = ring // 2
-    leftward = ring - 1 - rightward
+    half = ring // 2
+    full = half - 1 if ring % 2 == 0 else half
+
+    def goes_right(step):
+        return range(pieces) if step <= full else range(pieces // 2) if step == half else range(0)
+
+    def goes_left(step):
+        return range(pieces) if step <= full else range(pieces // 2, pieces) if step == half else range(0)
+
     for j in range(pieces):
         mine = w_ref.at[pl.ds(j * depth, depth)]
-        send(mine, me, j, 0, right)
-        if leftward > 0:
+        if j in goes_right(1):
+            send(mine, me, j, 0, right)
+        if j in goes_left(1):
             send(mine, me, j, 1, left)
         send(mine, me, j, 2, partner)
-    for step in range(1, rightward + 1):
+    for step in range(1, half + 1):
         for j in range(pieces):
-            h = slot(z - step)
-            arrive(h, j, left)
-            if step < rightward:
-                send(held(h, j), h, j, 0, right)
-            send(held(h, j), h, j, 2, partner)
-            if step <= leftward:
+            if j in goes_right(step):
+                h = slot(z - step)
+                arrive(h, j, left)
+                if j in goes_right(step + 1):
+                    send(held(h, j), h, j, 0, right)
+                send(held(h, j), h, j, 2, partner)
+            if j in goes_left(step):
                 h = slot(z + step)
                 arrive(h, j, right)
-                if step < leftward:
+                if j in goes_left(step + 1):
                     send(held(h, j), h, j, 1, left)
                 send(held(h, j), h, j, 2, partner)
     for origin in range(ring):

time: 260 us -> 256 us (0.985)
  Pallas kernels: 194 us -> 191 us
    pallas_call x1, Pallas kernels: 81.3 us -> 76.2 us  [opening(): pl.pallas_call(opening_kernel, out_shape=(jax.ShapeDtypeStruct(x.shape, x...]
where the time goes in v7:
time: 256 us
  Pallas kernels  191 us (75%)
  matrix products  31.4 us (12%)
  local copies, waits for them, and re-layouts  23.3 us (9%)
  other arithmetic  10 us (4%)
    pallas_call x3, Pallas kernels, exchange(): pl.pallas_call(exchange_kernel, out_shape=jax.ShapeDtypeStruct(x.shape, x...  91.9 us
    pallas_call x1, Pallas kernels, opening(): pl.pallas_call(opening_kernel, out_shape=(jax.ShapeDtypeStruct(x.shape, x...  76.2 us
    pallas_call x1, Pallas kernels, gather_seq(): pl.pallas_call(gather_kernel, out_shape=jax.ShapeDtypeStruct(shape, x.dty...  22.4 us
    dot_general x1, matrix products, attend(): jnp.einsum('bhts,bshe->bthe', weights, value_blocks, preferred_element_ty...  8.82 us
    dot_general x1, matrix products, per_device(): jnp.einsum('tf,hfe->the', rows, value_all, preferred_element_type=jnp.flo...  6.45 us
    dot_general x1, matrix products, per_device(): jnp.dot(hidden_rows, w_out, preferred_element_type=jnp.float32)  5.75 us

profile of v7, /device:TPU:1, one launch (start us, length us, event | category | flops | bytes accessed | tf_op | source)
XLA Modules:
  0.0 255.6 jit_solution(10116453367975096983)
XLA Ops:
  0.0 0.0 copy-start
  0.0 76.2 %shard_map.64 = (bf16[16,224,128]{2,1,0:T(8,128)(2,1)}, bf16[16,2048,128]{2,1,0:T(8,128)(2,1)}) custom-call(bf16[16,224,128]{2,1,0:T(8,128)(2,1)} %bitcast.93, bf16[2048,128]{1,0:T(8,128)(2,1)} %w_ref.1), custom_call_target="tpu_custom_call" | custom-call | tf_op jit(solution)/shard_map/pallas_call | solution.py:295
  76.2 1.5 copy.18
  77.8 0.4 reshape.236
  78.2 0.0 copy-start.5
  78.2 6.4 %convolution_convert_fusion.1 = bf16[224,16,128]{2,0,1:T(8,128)(2,1)} fusion(bf16[224,2048,1]{1,0,2:T(8,128)(2,1)S(1)} %reshape.236, bf16[16,2048,128]{2,1,0:T(8,128)(2,1)} %get-tuple-element.8), kind=kOutput, calls=%fused_computation.15 | convolution fusion | flops 1879506944 | bytes 10223616 | tf_op jit(solution)/shard_map/tf,hfe->the/dot_general | solution.py:381
  84.6 0.0 copy-done
  84.6 0.0 copy-done.5
  84.6 0.0 copy-start.6
  84.6 0.4 convolution_convert_fusion.3
  85.0 0.1 copy.19
  85.1 1.3 copy.21
  86.4 0.0 copy-done.6
  86.4 0.4 convolution_convert_fusion.2
  86.8 0.1 copy.20
  87.0 1.3 copy.22
  88.2 3.4 %maximum_bitcast_fusion = bf16[16,224,160]{2,1,0:T(8,128)(2,1)S(1)} fusion(bf16[224,16,128]{2,0,1:T(8,128)(2,1)} %convolution_convert_fusion.1, bf16[224,16,16]{2,0,1:T(8,128)(2,1)} %copy.22, bf16[224,16,16]{2,0,1:T(8,128)(2,1)} %copy.21), kind=kLoop, calls=%fused_computation.7 | loop fusion | flops 3440640 | bytes 2293760 | tf_op jit(solution)/shard_map/transpose | solution.py:388
  91.6 3.8 %reshape.225.x_ref = bf16[16,280,128]{2,1,0:T(8,128)(2,1)} reshape(bf16[16,224,160]{2,1,0:T(8,128)(2,1)S(1)} %maximum_bitcast_fusion) | data formatting | bytes 2293760 | tf_op jit(solution)/shard_map/reshape | solution.py:388
  95.4 33.3 %shard_map.65 = bf16[16,280,128]{2,1,0:T(8,128)(2,1)} custom-call(bf16[16,280,128]{2,1,0:T(8,128)(2,1)} %reshape.225.x_ref), custom_call_target="tpu_custom_call" | custom-call | tf_op jit(solution)/shard_map/pallas_call | solution.py:77
  128.8 3.4 %reshape.226 = bf16[3584,1,160]{2,0,1:T(8,128)(2,1)S(1)} reshape(bf16[16,280,128]{2,1,0:T(8,128)(2,1)} %shard_map.65) | data formatting | bytes 2293760 | tf_op jit(solution)/shard_map/reshape | solution.py:389
  132.2 0.0 copy-start.1
  132.2 1.8 fusion.27
  134.0 0.0 copy-done.1
  134.0 1.5 copy.26
  135.5 1.9 slice.28
  137.3 0.5 convolution_bitcast_fusion.1
  137.9 0.4 multiply_multiply_fusion.1
  138.3 1.8 convolution_bitcast_fusion
  140.1 0.0 copy-start.3
  140.1 0.1 convert_reduce_fusion
  140.2 0.7 fusion.11.x_ref
  140.9 22.4 %shard_map.66 = bf16[16,273,128]{2,1,0:T(8,128)(2,1)} custom-call(bf16[273,128]{1,0:T(8,128)(2,1)} %fusion.11.x_ref), custom_call_target="tpu_custom_call" | custom-call | tf_op jit(solution)/shard_map/pallas_call | solution.py:134
  163.4 1.6 select_reduce_fusion
  164.9 0.1 fusion.12
  165.0 0.9 pad_add_fusion
  165.9 0.0 copy-done.3
  165.9 0.3 copy.25
  166.2 0.0 copy-start.4
  166.2 3.8 %fusion.13 = f32[4,128,896]{2,1,0:T(8,128)} fusion(bf16[4,896,16]{1,2,0:T(8,128)(2,1)S(1)} %copy.25, f32[4,1,273,128]{3,2,0,1:T(8,128)} %pad_add_fusion), kind=kOutput, calls=%fused_computation.34 | convolution fusion | flops 88195072 | bytes 1982464 | tf_op jit(solution)/shard_map/bthf,bhfe->bthe/dot_general | solution.py:351
  170.0 0.4 multiply_multiply_fusion
  170.4 0.0 copy-start.2
  170.4 0.0 copy-done.4
  170.4 3.5 %fusion.10 = f32[4,128,896]{2,1,0:T(8,128)} fusion(f32[4,896,256]{1,2,0:T(8,128)S(1)} %bitcast.84, f32[4,1,273,128]{3,2,0,1:T(8,128)S(1)} %copy-done.4), kind=kOutput, calls=%fused_computation.31 | convolution fusion | flops 1409286144 | bytes 6029312 | tf_op jit(solution)/shard_map/bthf,bhfe->bthe/dot_general | solution.py:354
  173.9 1.1 iota_compare_fusion
  175.0 0.0 copy-done.2
  175.0 8.8 %multiply_reduce_fusion = (f32[4,896]{1,0:T(4,128)S(1)}, f32[4,896,1,128]{1,3,0,2:T(8,128)}) fusion(f32[4,128,896]{2,1,0:T(8,128)} %fusion.10, f32[4,128,896]{2,1,0:T(8,128)} %fusion.13, f32[4,128]{1,0:T(4,128)S(1)} %bitcast.98, bf16[4,896,128]{2,1,0:T(8,128)(2,1)S(1)} %bitcast.82, bf16[4,896,16]{2,1,0:T(8,128)(2,1)} %bitcast.88, ...), kind=kOutput, calls=%fused_computation.13 | convolution fusion | flops 949613056 | bytes 7471104 | tf_op jit(solution)/shard_map/bhts,bshe->bthe/dot_general | solution.py:363
  183.8 1.8 copy.32
  185.7 0.1 rsqrt.12
  185.7 0.8 dynamic_slice.3
  186.5 1.5 multiply_convert_fusion.x_ref
  188.0 30.7 %shard_map.67 = bf16[16,224,128]{2,1,0:T(8,128)(2,1)} custom-call(bf16[16,224,128]{2,1,0:T(8,128)(2,1)} %multiply_convert_fusion.x_ref), custom_call_target="tpu_custom_call" | custom-call | tf_op jit(solution)/shard_map/pallas_call | solution.py:77
  218.7 5.7 %fusion.3 = bf16[28,16,8,128]{3,2,1,0:T(8,128)(2,1)S(1)} fusion(bf16[2048,2048]{1,0:T(8,128)(2,1)} %param.10, bf16[16,224,128]{2,1,0:T(8,128)(2,1)} %shard_map.67), kind=kOutput, calls=%fused_computation.16 | convolution fusion | flops 1879506944 | bytes 10223616 | tf_op jit(solution)/shard_map/dot_general | solution.py:401
  224.4 1.1 copy.60
  225.5 27.9 %shard_map.68 = bf16[16,224,128]{2,1,0:T(8,128)(2,1)} custom-call(bf16[16,224,128]{2,1,0:T(8,128)(2,1)} %bitcast.90), custom_call_target="tpu_custom_call" | custom-call | tf_op jit(solution)/shard_map/pallas_call | solution.py:77
  253.4 2.2 copy.62
  (6 shorter events, 0.1 us)
Async XLA Ops:
  0.0 84.6 %copy-start = (bf16[2048,256]{1,0:T(8,128)(2,1)S(1)}, bf16[2048,256]{1,0:T(8,128)(2,1)}, u32[]{:S(2)}) copy-start(bf16[2048,256]{1,0:T(8,128)(2,1)} %param.7) | copy-start | bytes 3145732
  78.2 6.5 %copy-start.5 = (bf16[16,224,128]{2,1,0:T(8,128)(2,1)S(1)}, bf16[16,224,128]{2,1,0:T(8,128)(2,1)}, u32[]{:S(2)}) copy-start(bf16[16,224,128]{2,1,0:T(8,128)(2,1)} %get-tuple-element.7) | copy-start | bytes 2752516
  84.6 1.8 copy-start.6
  132.2 1.8 copy-start.1
  140.1 25.8 %copy-start.3 = (bf16[3584,1,16]{2,0,1:T(8,128)(2,1)S(1)}, bf16[3584,1,16]{2,0,1:T(8,128)(2,1)}, u32[]{:S(2)}) copy-start(bf16[3584,1,16]{2,0,1:T(8,128)(2,1)} %get-tuple-element.10) | copy-start | bytes 344068
  166.2 4.2 %copy-start.4 = (f32[4,1,273,128]{3,2,0,1:T(8,128)S(1)}, f32[4,1,273,128]{3,2,0,1:T(8,128)}, u32[]{:S(2)}) copy-start(f32[4,1,273,128]{3,2,0,1:T(8,128)} %pad_add_fusion) | copy-start | bytes 1677316
  170.4 4.7 %copy-start.2 = (bf16[3584,1,16]{2,0,1:T(8,128)(2,1)S(1)}, bf16[3584,1,16]{2,0,1:T(8,128)(2,1)}, u32[]{:S(2)}) copy-start(bf16[3584,1,16]{2,0,1:T(8,128)(2,1)} %get-tuple-element.9) | copy-start | bytes 344068

commit v8 on v7

--- a/solution.py
+++ b/solution.py
@@ -1,3 +1,5 @@
+import functools
+
 import jax
 import jax.numpy as jnp
 from jax import lax
@@ -32,8 +34,10 @@
     return (linear, square)
 
 
-def exchange_kernel(x_ref, y_ref, buf, send_sem, recv_sem, own_sem):
-    n = x_ref.shape[0]
+def exchange_kernel(count, *refs):
+    xs, ys, bufs = refs[:count], refs[count : 2 * count], refs[2 * count : 3 * count]
+    send_sem, recv_sem, own_sem = refs[3 * count :]
+    n = xs[0].shape[0]
     me = chan_index()
     slab = lax.axis_index("seq")
     barrier = pltpu.get_barrier_semaphore()
@@ -41,52 +45,63 @@
         peer = lax.rem(me + step, n)
         pl.semaphore_signal(barrier, inc=1, device_id=chan_device(slab, peer), device_id_type=MESH)
     pl.semaphore_wait(barrier, n - 1)
-    own = pltpu.make_async_copy(x_ref.at[me], buf.at[me], own_sem)
-    own.start()
+    owns = []
     sends = []
-    for step in range(1, n):
-        peer = lax.rem(me + step, n)
-        copy = pltpu.make_async_remote_copy(
-            src_ref=x_ref.at[peer],
-            dst_ref=buf.at[me],
-            send_sem=send_sem.at[peer],
-            recv_sem=recv_sem.at[me],
-            device_id=chan_device(slab, peer),
-            device_id_type=MESH,
-        )
-        copy.start()
-        sends.append(copy)
+    for a in range(count):
+        own = pltpu.make_async_copy(xs[a].at[me], bufs[a].at[me], own_sem.at[a])
+        own.start()
+        owns.append(own)
+    for step in range(1, n):
+        peer = lax.rem(me + step, n)
+        for a in range(count):
+            copy = pltpu.make_async_remote_copy(
+                src_ref=xs[a].at[peer],
+                dst_ref=bufs[a].at[me],
+                send_sem=send_sem.at[a, peer],
+                recv_sem=recv_sem.at[a, me],
+                device_id=chan_device(slab, peer),
+                device_id_type=MESH,
+            )
+            copy.start()
+            sends.append(copy)
     for step in range(1, n):
         source = lax.rem(me + n - step, n)
-        pltpu.make_async_remote_copy(
-            src_ref=x_ref.at[source],
-            dst_ref=buf.at[source],
-            send_sem=send_sem.at[source],
-            recv_sem=recv_sem.at[source],
-            device_id=chan_device(slab, source),
-            device_id_type=MESH,
-        ).wait_recv()
+        for a in range(count):
+            pltpu.make_async_remote_copy(
+                src_ref=xs[a].at[source],
+                dst_ref=bufs[a].at[source],
+                send_sem=send_sem.at[a, source],
+                recv_sem=recv_sem.at[a, source],
+                device_id=chan_device(slab, source),
+                device_id_type=MESH,
+            ).wait_recv()
     for copy in sends:
         copy.wait_send()
-    own.wait()
-    y_ref[...] = buf[...]
-
-
-def exchange(x, collective_id):
-    n = x.shape[0]
+    for a in range(count):
+        owns[a].wait()
+        ys[a][...] = bufs[a][...]
+
+
+def exchange_many(xs, collective_id):
+    count = len(xs)
+    n = xs[0].shape[0]
     return pl.pallas_call(
-        exchange_kernel,
-        out_shape=jax.ShapeDtypeStruct(x.shape, x.dtype),
-        in_specs=[pl.BlockSpec(memory_space=pltpu.VMEM)],
-        out_specs=pl.BlockSpec(memory_space=pltpu.VMEM),
-        scratch_shapes=[
-            pltpu.VMEM(x.shape, x.dtype),
-            pltpu.SemaphoreType.DMA((n,)),
-            pltpu.SemaphoreType.DMA((n,)),
-            pltpu.SemaphoreType.DMA(()),
+        functools.partial(exchange_kernel, count),
+        out_shape=tuple(jax.ShapeDtypeStruct(x.shape, x.dtype) for x in xs),
+        in_specs=[pl.BlockSpec(memory_space=pltpu.VMEM)] * count,
+        out_specs=tuple(pl.BlockSpec(memory_space=pltpu.VMEM) for _ in xs),
+        scratch_shapes=[pltpu.VMEM(x.shape, x.dtype) for x in xs]
+        + [
+            pltpu.SemaphoreType.DMA((count, n)),
+            pltpu.SemaphoreType.DMA((count, n)),
+            pltpu.SemaphoreType.DMA((count,)),
         ],
         compiler_params=pltpu.CompilerParams(collective_id=collective_id, has_side_effects=True),
-    )(x)
+    )(*xs)
+
+
+def exchange(x, collective_id):
+    return exchange_many((x,), collective_id)[0]
 
 
 def gather_kernel(x_ref, y_ref, buf, send_sem, recv_sem, own_sem):
@@ -376,30 +391,33 @@
     got, value_all = opening(tokens.reshape(groups, tok_rows_total // groups, tok_cols), w_value, 1)
     rows = got.transpose(1, 0, 2).reshape(tok_rows_total // groups, groups * tok_cols)
     chunk = rows.shape[0]
-    query = jnp.dot(rows, w_query, preferred_element_type=jnp.float32).astype(jnp.bfloat16)
-    key = jnp.dot(rows, w_key, preferred_element_type=jnp.float32).astype(jnp.bfloat16)
-    value = jnp.einsum("tf,hfe->the", rows, value_all, preferred_element_type=jnp.float32)
-    value = value.astype(jnp.bfloat16).reshape(chunk, groups, per_group * HEAD_DIM)
-    query = query.reshape(chunk, groups, per_group * FEAT)
-    key = key.reshape(chunk, groups, per_group * FEAT)
-    packed = jnp.concatenate([query, key, value], axis=2)
-    width = packed.shape[2]
-    lanes = chunk * width // HEAD_DIM
-    sent = exchange(packed.transpose(1, 0, 2).reshape(groups, lanes, HEAD_DIM), 2)
-    mine = sent.reshape(groups * chunk, 1, width)
-    tok_rows = mine.shape[0]
-    qf = per_group * FEAT
-    query_rows = mine[:, 0, :qf].reshape(tok_rows, per_group, FEAT)
-    key_rows = mine[:, 0, qf : 2 * qf].reshape(tok_rows, per_group, FEAT)
-    value_rows = mine[:, 0, 2 * qf :].reshape(tok_rows, per_group, HEAD_DIM)
+    pf = per_group * FEAT
+    d_model = w_query.shape[0]
+    w_qk = jnp.concatenate(
+        [w_query.reshape(d_model, groups, pf), w_key.reshape(d_model, groups, pf)], axis=2
+    )
+    qk_t = jnp.einsum("tf,fgd->gdt", rows, w_qk, preferred_element_type=jnp.float32).astype(jnp.bfloat16)
+    value = jnp.einsum("tf,gfe->gte", rows, value_all, preferred_element_type=jnp.float32).astype(jnp.bfloat16)
+    qk_got, value_got = exchange_many((qk_t, value), 2)
+    tok_rows = groups * chunk
+    qk_rows = qk_got.transpose(0, 2, 1).reshape(tok_rows, 2 * pf)
+    query_rows = qk_rows[:, :pf].reshape(tok_rows, per_group, FEAT)
+    key_rows = qk_rows[:, pf:].reshape(tok_rows, per_group, FEAT)
+    value_rows = value_got.reshape(tok_rows, per_group, HEAD_DIM)
     value_cols = per_group * HEAD_DIM
     gain_mine = lax.dynamic_slice_in_dim(gain, my_group * value_cols, value_cols, 0).reshape(
         per_group, HEAD_DIM
     )
     hidden = attend(query_rows, key_rows, value_rows, gain_mine, my_slab)
-    hidden_rows = split_rows(hidden, groups, 3)
-    mixed_rows = jnp.dot(hidden_rows, w_out, preferred_element_type=jnp.float32).astype(jnp.bfloat16)
-    return split_cols(mixed_rows.reshape(chunk, groups, -1), groups, 4)
+    hidden_got = exchange(hidden.reshape(groups, chunk, per_group * HEAD_DIM), 3)
+    out_cols = w_out.shape[1] // groups
+    mixed_blocks = jnp.einsum(
+        "gte,gecj->ctj",
+        hidden_got,
+        w_out.reshape(groups, per_group * HEAD_DIM, groups, out_cols),
+        preferred_element_type=jnp.float32,
+    ).astype(jnp.bfloat16)
+    return exchange(mixed_blocks, 4).reshape(tok_rows, out_cols)
 
 
 def solution(mesh):

time: 256 us -> 252 us (0.984)
  other arithmetic: 10 us -> 5.9 us
  local copies, waits for them, and re-layouts: 23.3 us -> 20.4 us
    unnamed x15 -> x14, local copies, waits for them, and re-layouts: 2.19 us -> 14.2 us
    reshape x6 -> x1, local copies, waits for them, and re-layouts: 11.2 us -> 0.35 us  [per_device(): qk_rows = qk_got.transpose(0, 2, 1).reshape(tok_rows, 2 * pf)]
    dot_general x4 -> x3, matrix products: 13 us -> 16.9 us  [the longest x1 7.75 us: per_device(): jnp.einsum('gte,gecj->ctj', hidden_got, w_out.reshape(groups, per_group *...]
    slice x2 -> x1, local copies, waits for them, and re-layouts: 3.67 us -> 0.02 us  [per_device(): key_rows = qk_rows[:, pf:].reshape(tok_rows, per_group, FEAT)]
    transpose x1 -> x0, other arithmetic: 3.35 us -> none  [per_device(): packed.transpose(1, 0, 2).reshape(groups, lanes, HEAD_DIM)]
where the time goes in v8:
time: 252 us
  Pallas kernels  192 us (76%)
  matrix products  33.5 us (13%)
  local copies, waits for them, and re-layouts  20.4 us (8%)
  other arithmetic  5.9 us (2%)
    pallas_call x3, Pallas kernels, exchange_many(): pl.pallas_call(functools.partial(exchange_kernel, count), out_shape=tuple...  93 us
    pallas_call x1, Pallas kernels, opening(): pl.pallas_call(opening_kernel, out_shape=(jax.ShapeDtypeStruct(x.shape, x...  76.1 us
    pallas_call x1, Pallas kernels, gather_seq(): pl.pallas_call(gather_kernel, out_shape=jax.ShapeDtypeStruct(shape, x.dty...  22.4 us
    unnamed x14, local copies, waits for them, and re-layouts  14.2 us
    dot_general x1, matrix products, attend(): jnp.einsum('bhts,bshe->bthe', weights, value_blocks, preferred_element_ty...  7.9 us
    dot_general x1, matrix products, per_device(): jnp.einsum('gte,gecj->ctj', hidden_got, w_out.reshape(groups, per_group *...  7.75 us
    dot_general x1, matrix products, per_device(): jnp.einsum('tf,gfe->gte', rows, value_all, preferred_element_type=jnp.flo...  6.59 us

profile of v8, /device:TPU:1, one launch (start us, length us, event | category | flops | bytes accessed | tf_op | source)
XLA Modules:
  0.0 251.5 jit_solution(6312852391944512725)
XLA Ops:
  0.0 76.1 %shard_map.64 = (bf16[16,224,128]{2,1,0:T(8,128)(2,1)}, bf16[16,2048,128]{2,1,0:T(8,128)(2,1)}) custom-call(bf16[16,224,128]{2,1,0:T(8,128)(2,1)} %bitcast.102, bf16[2048,128]{1,0:T(8,128)(2,1)} %w_ref.1), custom_call_target="tpu_custom_call" | custom-call | tf_op jit(solution)/shard_map/pallas_call | solution.py:310
  76.1 1.5 copy.33
  77.7 0.4 reshape.217
  78.1 0.0 copy-start.3
  78.1 0.9 copy-done.3
  79.0 0.0 copy-start.1
  79.0 0.0 copy-start.2
  79.0 6.6 %fusion.11.refs_1_ = bf16[16,224,128]{2,1,0:T(8,128)(2,1)} fusion(bf16[224,2048,1]{1,0,2:T(8,128)(2,1)S(1)} %reshape.217, bf16[16,2048,128]{2,1,0:T(8,128)(2,1)} %get-tuple-element.10), kind=kOutput, calls=%fused_computation.21 | convolution fusion | flops 1879506944 | bytes 10223616 | tf_op jit(solution)/shard_map/tf,gfe->gte/dot_general | solution.py:400
  85.6 0.0 copy-done.1
  85.6 0.6 copy.31
  86.2 0.0 copy-done.2
  86.2 0.6 copy.32
  86.9 2.6 %fusion.15.refs_0_ = bf16[16,32,224]{2,1,0:T(8,128)(2,1)} fusion(bf16[224,2048,1]{1,0,2:T(8,128)(2,1)} %copy-done.3, bf16[2048,16,16]{0,2,1:T(8,128)(2,1)S(1)} %bitcast.94, bf16[2048,16,16]{0,2,1:T(8,128)(2,1)S(1)} %bitcast.93), kind=kOutput, calls=%fused_computation.24 | convolution fusion | flops 474071040 | bytes 3244032 | tf_op jit(solution)/shard_map/tf,fgd->gdt/dot_general | solution.py:399
  89.5 34.5 %shard_map.65 = (bf16[16,32,224]{2,1,0:T(8,128)(2,1)}, bf16[16,224,128]{2,1,0:T(8,128)(2,1)}) custom-call(bf16[16,32,224]{2,1,0:T(8,128)(2,1)} %fusion.15.refs_0_, bf16[16,224,128]{2,1,0:T(8,128)(2,1)} %fusion.11.refs_1_), custom_call_target="tpu_custom_call" | custom-call | tf_op jit(solution)/shard_map/pallas_call | solution.py:88
  124.0 0.0 copy-start
  124.0 1.2 copy.34
  125.2 0.4 reshape.209
  125.6 1.7 convolution_bitcast_fusion.1
  127.3 0.4 multiply_multiply_fusion.1
  127.7 0.0 copy-done
  127.7 1.8 convolution_bitcast_fusion
  129.5 0.1 convert_reduce_fusion
  129.6 0.7 fusion.20.x_ref
  130.3 22.4 %shard_map.66 = bf16[16,273,128]{2,1,0:T(8,128)(2,1)} custom-call(bf16[273,128]{1,0:T(8,128)(2,1)} %fusion.20.x_ref), custom_call_target="tpu_custom_call" | custom-call | tf_op jit(solution)/shard_map/pallas_call | solution.py:149
  152.8 1.6 select_reduce_fusion
  154.3 0.1 fusion.21
  154.5 1.6 fusion.22
  156.1 0.4 multiply_multiply_fusion
  156.5 3.5 %fusion.19 = f32[4,128,896]{2,1,0:T(8,128)} fusion(f32[4,896,256]{1,2,0:T(8,128)S(1)} %bitcast.85, f32[4,1,273,128]{3,2,0,1:T(8,128)S(1)} %pad_add_fusion), kind=kOutput, calls=%fused_computation.30 | convolution fusion | flops 1409286144 | bytes 6029312 | tf_op jit(solution)/shard_map/bthf,bhfe->bthe/dot_general | solution.py:369
  160.1 1.1 iota_compare_fusion
  161.2 7.9 %multiply_reduce_fusion = (f32[4,896]{1,0:T(4,128)S(1)}, f32[4,896,1,128]{1,3,0,2:T(8,128)}) fusion(f32[4,128,896]{2,1,0:T(8,128)} %fusion.19, f32[4,128,896]{2,1,0:T(8,128)S(1)} %fusion.22, f32[4,128]{1,0:T(4,128)S(1)} %bitcast.107, bf16[4,896,128]{2,1,0:T(8,128)(2,1)S(1)} %bitcast.90, pred[896,896]{1,0:T(8,128)(4,1)} %iota_compare_fusion, ...), kind=kOutput, calls=%fused_computation.18 | convolution fusion | flops 949613056 | bytes 7471104 | tf_op jit(solution)/shard_map/bhts,bshe->bthe/dot_general | solution.py:378
  169.1 1.8 copy.42
  170.9 0.1 rsqrt.12
  171.0 0.8 dynamic_slice.3
  171.7 1.5 multiply_convert_fusion.refs_0_
  173.2 30.7 %shard_map.67 = bf16[16,224,128]{2,1,0:T(8,128)(2,1)} custom-call(bf16[16,224,128]{2,1,0:T(8,128)(2,1)} %multiply_convert_fusion.refs_0_), custom_call_target="tpu_custom_call" | custom-call | tf_op jit(solution)/shard_map/pallas_call | solution.py:88
  204.0 0.0 copy-start.4
  204.0 9.8 %copy.50 = bf16[256,8,16,128]{3,2,1,0:T(8,128)(2,1)} copy(bf16[256,8,16,128]{3,1,2,0:T(8,128)(2,1)} %bitcast.86) | data formatting | bytes 16777216
  213.8 0.0 copy-done.4
  213.8 7.7 %fusion.12.refs_0_ = bf16[16,224,128]{2,1,0:T(8,128)(2,1)} fusion(bf16[16,128,16,128]{3,2,1,0:T(8,128)(2,1)} %bitcast.87, bf16[16,224,128]{2,1,0:T(8,128)(2,1)S(1)} %copy-done.4), kind=kOutput, calls=%fused_computation.22 | convolution fusion | flops 1879506944 | bytes 10223616 | tf_op jit(solution)/shard_map/gte,gecj->ctj/dot_general | solution.py:414
  221.6 27.8 %shard_map.68 = bf16[16,224,128]{2,1,0:T(8,128)(2,1)} custom-call(bf16[16,224,128]{2,1,0:T(8,128)(2,1)} %fusion.12.refs_0_), custom_call_target="tpu_custom_call" | custom-call | tf_op jit(solution)/shard_map/pallas_call | solution.py:88
  249.4 2.2 copy.80
  (9 shorter events, 0.2 us)
Async XLA Ops:
  78.1 0.9 copy-start.3
  79.0 6.6 %copy-start.1 = (bf16[2048,256]{1,0:T(8,128)(2,1)S(1)}, bf16[2048,256]{1,0:T(8,128)(2,1)}, u32[]{:S(2)}) copy-start(bf16[2048,256]{1,0:T(8,128)(2,1)} %param.7) | copy-start | bytes 3145732
  79.0 7.2 %copy-start.2 = (bf16[2048,256]{1,0:T(8,128)(2,1)S(1)}, bf16[2048,256]{1,0:T(8,128)(2,1)}, u32[]{:S(2)}) copy-start(bf16[2048,256]{1,0:T(8,128)(2,1)} %param.8) | copy-start | bytes 3145732
  124.0 3.7 %copy-start = (bf16[16,224,128]{2,1,0:T(8,128)(2,1)S(1)}, bf16[16,224,128]{2,1,0:T(8,128)(2,1)}, u32[]{:S(2)}) copy-start(bf16[16,224,128]{2,1,0:T(8,128)(2,1)} %get-tuple-element.11) | copy-start | bytes 2752516
  204.0 9.9 %copy-start.4 = (bf16[16,224,128]{2,1,0:T(8,128)(2,1)S(1)}, bf16[16,224,128]{2,1,0:T(8,128)(2,1)}, u32[]{:S(2)}) copy-start(bf16[16,224,128]{2,1,0:T(8,128)(2,1)} %shard_map.67) | copy-start | bytes 2752516

commit v9 on v8

--- a/solution.py
+++ b/solution.py
@@ -411,12 +411,13 @@
     hidden = attend(query_rows, key_rows, value_rows, gain_mine, my_slab)
     hidden_got = exchange(hidden.reshape(groups, chunk, per_group * HEAD_DIM), 3)
     out_cols = w_out.shape[1] // groups
-    mixed_blocks = jnp.einsum(
-        "gte,gecj->ctj",
+    mixed_rows = jnp.einsum(
+        "gte,gef->tf",
         hidden_got,
-        w_out.reshape(groups, per_group * HEAD_DIM, groups, out_cols),
+        w_out.reshape(groups, per_group * HEAD_DIM, w_out.shape[1]),
         preferred_element_type=jnp.float32,
     ).astype(jnp.bfloat16)
+    mixed_blocks = mixed_rows.reshape(chunk, groups, out_cols).transpose(1, 0, 2)
     return exchange(mixed_blocks, 4).reshape(tok_rows, out_cols)
 
 

time: 252 us -> 242 us (0.960)
  local copies, waits for them, and re-layouts: 20.4 us -> 11.6 us
    unnamed x14 -> x9, local copies, waits for them, and re-layouts: 14.2 us -> 3.45 us
where the time goes in v9:
time: 242 us; the launch traced here: 241 us
  Pallas kernels  191 us (79%)
  matrix products  31.8 us (13%)
  local copies, waits for them, and re-layouts  11.6 us (5%)
  other arithmetic  5.9 us (2%)
    pallas_call x3, Pallas kernels, exchange_many(): pl.pallas_call(functools.partial(exchange_kernel, count), out_shape=tuple...  92.9 us
    pallas_call x1, Pallas kernels, opening(): pl.pallas_call(opening_kernel, out_shape=(jax.ShapeDtypeStruct(x.shape, x...  76.1 us
    pallas_call x1, Pallas kernels, gather_seq(): pl.pallas_call(gather_kernel, out_shape=jax.ShapeDtypeStruct(shape, x.dty...  22.4 us
    dot_general x1, matrix products, attend(): jnp.einsum('bhts,bshe->bthe', weights, value_blocks, preferred_element_ty...  7.9 us
    dot_general x1, matrix products, per_device(): jnp.einsum('tf,gfe->gte', rows, value_all, preferred_element_type=jnp.flo...  6.86 us
    dot_general x1, matrix products, per_device(): jnp.einsum('gte,gef->tf', hidden_got, w_out.reshape(groups, per_group * H...  5.75 us

profile of v9, /device:TPU:1, one launch (start us, length us, event | category | flops | bytes accessed | tf_op | source)
XLA Modules:
  0.0 240.9 jit_solution(13059875886218068934)
XLA Ops:
  0.0 76.1 %shard_map.64 = (bf16[16,224,128]{2,1,0:T(8,128)(2,1)}, bf16[16,2048,128]{2,1,0:T(8,128)(2,1)}) custom-call(bf16[16,224,128]{2,1,0:T(8,128)(2,1)} %bitcast.105, bf16[2048,128]{1,0:T(8,128)(2,1)} %w_ref.1), custom_call_target="tpu_custom_call" | custom-call | tf_op jit(solution)/shard_map/pallas_call | solution.py:310
  76.1 1.5 copy.32
  77.7 1.3 reshape.221
  79.0 0.0 copy-start.1
  79.0 0.0 copy-start.2
  79.0 6.9 %fusion.8.refs_1_ = bf16[16,224,128]{2,1,0:T(8,128)(2,1)} fusion(bf16[224,2048,1]{1,0,2:T(8,128)(2,1)} %reshape.221, bf16[16,2048,128]{2,1,0:T(8,128)(2,1)} %get-tuple-element.10), kind=kOutput, calls=%fused_computation.20 | convolution fusion | flops 1879506944 | bytes 10223616 | tf_op jit(solution)/shard_map/tf,gfe->gte/dot_general | solution.py:400
  85.9 0.0 copy-done.1
  85.9 0.6 copy.30
  86.5 0.0 copy-done.2
  86.5 0.6 copy.31
  87.2 2.6 %fusion.10.refs_0_ = bf16[16,32,224]{2,1,0:T(8,128)(2,1)} fusion(bf16[224,2048,1]{1,0,2:T(8,128)(2,1)} %reshape.221, bf16[2048,16,16]{0,2,1:T(8,128)(2,1)S(1)} %bitcast.97, bf16[2048,16,16]{0,2,1:T(8,128)(2,1)S(1)} %bitcast.96), kind=kOutput, calls=%fused_computation.23 | convolution fusion | flops 474071040 | bytes 3244032 | tf_op jit(solution)/shard_map/tf,fgd->gdt/dot_general | solution.py:399
  89.8 34.5 %shard_map.65 = (bf16[16,32,224]{2,1,0:T(8,128)(2,1)}, bf16[16,224,128]{2,1,0:T(8,128)(2,1)}) custom-call(bf16[16,32,224]{2,1,0:T(8,128)(2,1)} %fusion.10.refs_0_, bf16[16,224,128]{2,1,0:T(8,128)(2,1)} %fusion.8.refs_1_), custom_call_target="tpu_custom_call" | custom-call | tf_op jit(solution)/shard_map/pallas_call | solution.py:88
  124.3 0.0 copy-start
  124.3 1.2 copy.33
  125.5 0.4 reshape.212
  125.8 1.7 convolution_bitcast_fusion.2
  127.6 0.4 multiply_multiply_fusion.1
  127.9 0.0 copy-done
  128.0 1.8 convolution_bitcast_fusion.1
  129.8 0.1 convert_reduce_fusion
  129.9 0.7 fusion.14.x_ref
  130.6 22.4 %shard_map.66 = bf16[16,273,128]{2,1,0:T(8,128)(2,1)} custom-call(bf16[273,128]{1,0:T(8,128)(2,1)} %fusion.14.x_ref), custom_call_target="tpu_custom_call" | custom-call | tf_op jit(solution)/shard_map/pallas_call | solution.py:149
  153.1 1.6 select_reduce_fusion
  154.6 0.1 fusion.15
  154.8 1.6 fusion.16
  156.5 0.4 multiply_multiply_fusion
  156.8 3.5 %fusion.13 = f32[4,128,896]{2,1,0:T(8,128)} fusion(f32[4,896,256]{1,2,0:T(8,128)S(1)} %bitcast.89, f32[4,1,273,128]{3,2,0,1:T(8,128)S(1)} %pad_add_fusion), kind=kOutput, calls=%fused_computation.29 | convolution fusion | flops 1409286144 | bytes 6029312 | tf_op jit(solution)/shard_map/bthf,bhfe->bthe/dot_general | solution.py:369
  160.4 1.1 iota_compare_fusion
  161.5 7.9 %multiply_reduce_fusion = (f32[4,896]{1,0:T(4,128)S(1)}, f32[4,896,1,128]{1,3,0,2:T(8,128)}) fusion(f32[4,128,896]{2,1,0:T(8,128)} %fusion.13, f32[4,128,896]{2,1,0:T(8,128)S(1)} %fusion.16, f32[4,128]{1,0:T(4,128)S(1)} %bitcast.110, bf16[4,896,128]{2,1,0:T(8,128)(2,1)S(1)} %bitcast.92, pred[896,896]{1,0:T(8,128)(4,1)} %iota_compare_fusion, ...), kind=kOutput, calls=%fused_computation.17 | convolution fusion | flops 949613056 | bytes 7471104 | tf_op jit(solution)/shard_map/bhts,bshe->bthe/dot_general | solution.py:378
  169.4 1.8 copy.41
  171.2 0.1 rsqrt.12
  171.3 0.8 dynamic_slice.3
  172.1 1.5 multiply_convert_fusion.refs_0_
  173.5 30.6 %shard_map.67 = bf16[16,224,128]{2,1,0:T(8,128)(2,1)} custom-call(bf16[16,224,128]{2,1,0:T(8,128)(2,1)} %multiply_convert_fusion.refs_0_), custom_call_target="tpu_custom_call" | custom-call | tf_op jit(solution)/shard_map/pallas_call | solution.py:88
  204.2 5.7 %fusion.9 = bf16[28,16,8,128]{3,2,1,0:T(8,128)(2,1)S(1)} fusion(bf16[16,224,128]{2,1,0:T(8,128)(2,1)} %shard_map.67, bf16[16,128,2048]{2,1,0:T(8,128)(2,1)} %bitcast.111), kind=kOutput, calls=%fused_computation.21 | convolution fusion | flops 1879506944 | bytes 10223616 | tf_op jit(solution)/shard_map/gte,gef->tf/dot_general | solution.py:414
  209.9 1.1 copy.72
  211.0 27.8 %shard_map.68 = bf16[16,224,128]{2,1,0:T(8,128)(2,1)} custom-call(bf16[16,224,128]{2,1,0:T(8,128)(2,1)} %bitcast.94), custom_call_target="tpu_custom_call" | custom-call | tf_op jit(solution)/shard_map/pallas_call | solution.py:88
  238.8 2.2 copy.74
  (9 shorter events, 0.2 us)
Async XLA Ops:
  79.0 6.9 %copy-start.1 = (bf16[2048,256]{1,0:T(8,128)(2,1)S(1)}, bf16[2048,256]{1,0:T(8,128)(2,1)}, u32[]{:S(2)}) copy-start(bf16[2048,256]{1,0:T(8,128)(2,1)} %param.7) | copy-start | bytes 3145732
  79.0 7.5 %copy-start.2 = (bf16[2048,256]{1,0:T(8,128)(2,1)S(1)}, bf16[2048,256]{1,0:T(8,128)(2,1)}, u32[]{:S(2)}) copy-start(bf16[2048,256]{1,0:T(8,128)(2,1)} %param.8) | copy-start | bytes 3145732
  124.3 3.7 %copy-start = (bf16[16,224,128]{2,1,0:T(8,128)(2,1)S(1)}, bf16[16,224,128]{2,1,0:T(8,128)(2,1)}, u32[]{:S(2)}) copy-start(bf16[16,224,128]{2,1,0:T(8,128)(2,1)} %get-tuple-element.11) | copy-start | bytes 2752516

commit v10 on v9

--- a/solution.py
+++ b/solution.py
@@ -104,21 +104,19 @@
     return exchange_many((x,), collective_id)[0]
 
 
-def gather_kernel(x_ref, y_ref, buf, send_sem, recv_sem, own_sem):
+def gather_kernel(x_ref, y_ref, buf, send_sem, recv_sem):
     n = buf.shape[0]
     me = lax.axis_index("seq")
     here = (lax.axis_index("z"), lax.axis_index("core"))
+    buf[...] = jnp.zeros_like(buf)
     barrier = pltpu.get_barrier_semaphore()
     for step in range(1, n):
         peer = lax.rem(me + step, n)
         pl.semaphore_signal(barrier, inc=1, device_id=(peer,) + here, device_id_type=MESH)
     pl.semaphore_wait(barrier, n - 1)
-    own = pltpu.make_async_copy(x_ref, buf.at[me], own_sem)
-    own.start()
-    sends = []
-    for step in range(1, n):
-        peer = lax.rem(me + step, n)
-        copy = pltpu.make_async_remote_copy(
+
+    def copy_to(peer):
+        return pltpu.make_async_remote_copy(
             src_ref=x_ref,
             dst_ref=buf.at[me],
             send_sem=send_sem.at[peer],
@@ -126,21 +124,32 @@
             device_id=(peer,) + here,
             device_id_type=MESH,
         )
-        copy.start()
-        sends.append(copy)
-    for step in range(1, n):
-        source = lax.rem(me + n - step, n)
-        pltpu.make_async_remote_copy(
+
+    def copy_from(source):
+        return pltpu.make_async_remote_copy(
             src_ref=x_ref,
             dst_ref=buf.at[source],
             send_sem=send_sem.at[source],
             recv_sem=recv_sem.at[source],
             device_id=(source,) + here,
             device_id_type=MESH,
-        ).wait_recv()
-    for copy in sends:
-        copy.wait_send()
-    own.wait()
+        )
+
+    for step in range(1, n):
+        @pl.when(me + step < n)
+        def _():
+            copy_to(me + step).start()
+
+    for step in range(1, n):
+        @pl.when(me - step >= 0)
+        def _():
+            copy_from(me - step).wait_recv()
+
+    for step in range(1, n):
+        @pl.when(me + step < n)
+        def _():
+            copy_to(me + step).wait_send()
+
     y_ref[...] = buf[...]
 
 
@@ -155,7 +164,6 @@
             pltpu.VMEM(shape, x.dtype),
             pltpu.SemaphoreType.DMA((slabs,)),
             pltpu.SemaphoreType.DMA((slabs,)),
-            pltpu.SemaphoreType.DMA(()),
         ],
         compiler_params=pltpu.CompilerParams(collective_id=collective_id, has_side_effects=True),
     )(x)

time: 242 us -> 240 us (level)
  Pallas kernels: 191 us -> 188 us
    pallas_call x3, Pallas kernels: 92.9 us -> 90.4 us  [exchange_many(): pl.pallas_call(functools.partial(exchange_kernel, count), out_shape=tuple...]
where the time goes in v10:
time: 240 us; the launch traced here: 237 us
  Pallas kernels  188 us (78%)
  matrix products  32 us (13%)
  local copies, waits for them, and re-layouts  11.6 us (5%)
  other arithmetic  5.9 us (2%)
    pallas_call x3, Pallas kernels, exchange_many(): pl.pallas_call(functools.partial(exchange_kernel, count), out_shape=tuple...  90.4 us
    pallas_call x1, Pallas kernels, opening(): pl.pallas_call(opening_kernel, out_shape=(jax.ShapeDtypeStruct(x.shape, x...  76.1 us
    pallas_call x1, Pallas kernels, gather_seq(): pl.pallas_call(gather_kernel, out_shape=jax.ShapeDtypeStruct(shape, x.dty...  21 us
    dot_general x1, matrix products, attend(): jnp.einsum('bhts,bshe->bthe', weights, value_blocks, preferred_element_ty...  8.11 us
    dot_general x1, matrix products, per_device(): jnp.einsum('tf,gfe->gte', rows, value_all, preferred_element_type=jnp.flo...  6.86 us
    dot_general x1, matrix products, per_device(): jnp.einsum('gte,gef->tf', hidden_got, w_out.reshape(groups, per_group * H...  5.75 us

profile of v10, /device:TPU:1, one launch (start us, length us, event | category | flops | bytes accessed | tf_op | source)
XLA Modules:
  0.0 237.3 jit_solution(6041268429307372637)
XLA Ops:
  0.0 76.1 %shard_map.64 = (bf16[16,224,128]{2,1,0:T(8,128)(2,1)}, bf16[16,2048,128]{2,1,0:T(8,128)(2,1)}) custom-call(bf16[16,224,128]{2,1,0:T(8,128)(2,1)} %bitcast.105, bf16[2048,128]{1,0:T(8,128)(2,1)} %w_ref.1), custom_call_target="tpu_custom_call" | custom-call | tf_op jit(solution)/shard_map/pallas_call | solution.py:318
  76.1 1.5 copy.32
  77.7 1.3 reshape.221
  79.0 0.0 copy-start.1
  79.0 0.0 copy-start.2
  79.0 6.9 %fusion.8.refs_1_ = bf16[16,224,128]{2,1,0:T(8,128)(2,1)} fusion(bf16[224,2048,1]{1,0,2:T(8,128)(2,1)} %reshape.221, bf16[16,2048,128]{2,1,0:T(8,128)(2,1)} %get-tuple-element.10), kind=kOutput, calls=%fused_computation.20 | convolution fusion | flops 1879506944 | bytes 10223616 | tf_op jit(solution)/shard_map/tf,gfe->gte/dot_general | solution.py:408
  85.9 0.0 copy-done.1
  85.9 0.6 copy.30
  86.5 0.0 copy-done.2
  86.5 0.6 copy.31
  87.2 2.6 %fusion.10.refs_0_ = bf16[16,32,224]{2,1,0:T(8,128)(2,1)} fusion(bf16[224,2048,1]{1,0,2:T(8,128)(2,1)} %reshape.221, bf16[2048,16,16]{0,2,1:T(8,128)(2,1)S(1)} %bitcast.97, bf16[2048,16,16]{0,2,1:T(8,128)(2,1)S(1)} %bitcast.96), kind=kOutput, calls=%fused_computation.23 | convolution fusion | flops 474071040 | bytes 3244032 | tf_op jit(solution)/shard_map/tf,fgd->gdt/dot_general | solution.py:407
  89.8 34.7 %shard_map.65 = (bf16[16,32,224]{2,1,0:T(8,128)(2,1)}, bf16[16,224,128]{2,1,0:T(8,128)(2,1)}) custom-call(bf16[16,32,224]{2,1,0:T(8,128)(2,1)} %fusion.10.refs_0_, bf16[16,224,128]{2,1,0:T(8,128)(2,1)} %fusion.8.refs_1_), custom_call_target="tpu_custom_call" | custom-call | tf_op jit(solution)/shard_map/pallas_call | solution.py:88
  124.5 0.0 copy-start
  124.5 1.2 copy.33
  125.6 0.4 reshape.212
  126.0 1.7 convolution_bitcast_fusion.2
  127.8 0.4 multiply_multiply_fusion.1
  128.1 0.0 copy-done
  128.1 1.8 convolution_bitcast_fusion.1
  129.9 0.1 convert_reduce_fusion
  130.1 0.7 fusion.14.x_ref
  130.8 21.0 %shard_map.66 = bf16[16,273,128]{2,1,0:T(8,128)(2,1)} custom-call(bf16[273,128]{1,0:T(8,128)(2,1)} %fusion.14.x_ref), custom_call_target="tpu_custom_call" | custom-call | tf_op jit(solution)/shard_map/pallas_call | solution.py:158
  151.8 1.6 select_reduce_fusion
  153.4 0.1 fusion.15
  153.5 1.6 fusion.16
  155.2 0.4 multiply_multiply_fusion
  155.6 3.5 %fusion.13 = f32[4,128,896]{2,1,0:T(8,128)} fusion(f32[4,896,256]{1,2,0:T(8,128)S(1)} %bitcast.89, f32[4,1,273,128]{3,2,0,1:T(8,128)S(1)} %pad_add_fusion), kind=kOutput, calls=%fused_computation.29 | convolution fusion | flops 1409286144 | bytes 6029312 | tf_op jit(solution)/shard_map/bthf,bhfe->bthe/dot_general | solution.py:377
  159.1 1.1 iota_compare_fusion
  160.2 8.1 %multiply_reduce_fusion = (f32[4,896]{1,0:T(4,128)S(1)}, f32[4,896,1,128]{1,3,0,2:T(8,128)}) fusion(f32[4,128,896]{2,1,0:T(8,128)} %fusion.13, f32[4,128,896]{2,1,0:T(8,128)S(1)} %fusion.16, f32[4,128]{1,0:T(4,128)S(1)} %bitcast.110, bf16[4,896,128]{2,1,0:T(8,128)(2,1)S(1)} %bitcast.92, pred[896,896]{1,0:T(8,128)(4,1)} %iota_compare_fusion, ...), kind=kOutput, calls=%fused_computation.17 | convolution fusion | flops 949613056 | bytes 7471104 | tf_op jit(solution)/shard_map/bhts,bshe->bthe/dot_general | solution.py:386
  168.3 1.8 copy.41
  170.2 0.1 rsqrt.12
  170.2 0.8 dynamic_slice.3
  171.0 1.5 multiply_convert_fusion.refs_0_
  172.5 27.2 %shard_map.67 = bf16[16,224,128]{2,1,0:T(8,128)(2,1)} custom-call(bf16[16,224,128]{2,1,0:T(8,128)(2,1)} %multiply_convert_fusion.refs_0_), custom_call_target="tpu_custom_call" | custom-call | tf_op jit(solution)/shard_map/pallas_call | solution.py:88
  199.7 5.7 %fusion.9 = bf16[28,16,8,128]{3,2,1,0:T(8,128)(2,1)S(1)} fusion(bf16[16,224,128]{2,1,0:T(8,128)(2,1)} %shard_map.67, bf16[16,128,2048]{2,1,0:T(8,128)(2,1)} %bitcast.111), kind=kOutput, calls=%fused_computation.21 | convolution fusion | flops 1879506944 | bytes 10223616 | tf_op jit(solution)/shard_map/gte,gef->tf/dot_general | solution.py:422
  205.5 1.1 copy.72
  206.5 28.5 %shard_map.68 = bf16[16,224,128]{2,1,0:T(8,128)(2,1)} custom-call(bf16[16,224,128]{2,1,0:T(8,128)(2,1)} %bitcast.94), custom_call_target="tpu_custom_call" | custom-call | tf_op jit(solution)/shard_map/pallas_call | solution.py:88
  235.1 2.2 copy.74
  (9 shorter events, 0.2 us)
Async XLA Ops:
  79.0 6.9 %copy-start.1 = (bf16[2048,256]{1,0:T(8,128)(2,1)S(1)}, bf16[2048,256]{1,0:T(8,128)(2,1)}, u32[]{:S(2)}) copy-start(bf16[2048,256]{1,0:T(8,128)(2,1)} %param.7) | copy-start | bytes 3145732
  79.0 7.5 %copy-start.2 = (bf16[2048,256]{1,0:T(8,128)(2,1)S(1)}, bf16[2048,256]{1,0:T(8,128)(2,1)}, u32[]{:S(2)}) copy-start(bf16[2048,256]{1,0:T(8,128)(2,1)} %param.8) | copy-start | bytes 3145732
  124.5 3.7 %copy-start = (bf16[16,224,128]{2,1,0:T(8,128)(2,1)S(1)}, bf16[16,224,128]{2,1,0:T(8,128)(2,1)}, u32[]{:S(2)}) copy-start(bf16[16,224,128]{2,1,0:T(8,128)(2,1)} %get-tuple-element.11) | copy-start | bytes 2752516

commit v11 on v10

--- a/solution.py
+++ b/solution.py
@@ -164,6 +164,110 @@
             pltpu.VMEM(shape, x.dtype),
             pltpu.SemaphoreType.DMA((slabs,)),
             pltpu.SemaphoreType.DMA((slabs,)),
+        ],
+        compiler_params=pltpu.CompilerParams(collective_id=collective_id, has_side_effects=True),
+    )(x)
+
+
+def scan_kernel(width, x_ref, y_ref, row_buf, col_buf, total, row_send, row_recv, col_send, col_recv):
+    n = lax.axis_size("seq")
+    height = n // width
+    me = lax.axis_index("seq")
+    row, col = me // width, me % width
+    here = (lax.axis_index("z"), lax.axis_index("core"))
+    row_buf[...] = jnp.zeros_like(row_buf)
+    col_buf[...] = jnp.zeros_like(col_buf)
+    barrier = pltpu.get_barrier_semaphore()
+    for step in range(1, width):
+        peer = row * width + lax.rem(col + step, width)
+        pl.semaphore_signal(barrier, inc=1, device_id=(peer,) + here, device_id_type=MESH)
+    for step in range(1, height):
+        peer = lax.rem(row + step, height) * width + col
+        pl.semaphore_signal(barrier, inc=1, device_id=(peer,) + here, device_id_type=MESH)
+    pl.semaphore_wait(barrier, width + height - 2)
+
+    def row_copy(c, slot):
+        return pltpu.make_async_remote_copy(
+            src_ref=x_ref,
+            dst_ref=row_buf.at[slot],
+            send_sem=row_send.at[c],
+            recv_sem=row_recv.at[slot],
+            device_id=(row * width + c,) + here,
+            device_id_type=MESH,
+        )
+
+    sends = []
+    for step in range(1, width):
+        c = lax.rem(col + step, width)
+        copy = row_copy(c, col)
+        copy.start()
+        sends.append(copy)
+    for step in range(1, width):
+        c = lax.rem(col + width - step, width)
+        row_copy(c, c).wait_recv()
+    mine = x_ref[...].astype(jnp.float32)
+    row_total = mine
+    row_prefix = jnp.zeros_like(mine)
+    for c in range(width):
+        part = jnp.where(c == col, 0.0, row_buf[c].astype(jnp.float32))
+        row_total = row_total + part
+        row_prefix = row_prefix + jnp.where(c < col, part, 0.0)
+    total[...] = row_total
+
+    def col_copy(r, slot):
+        return pltpu.make_async_remote_copy(
+            src_ref=total,
+            dst_ref=col_buf.at[slot],
+            send_sem=col_send.at[r],
+            recv_sem=col_recv.at[slot],
+            device_id=(r * width + col,) + here,
+            device_id_type=MESH,
+        )
+
+    for step in range(1, height):
+        @pl.when(row + step < height)
+        def _():
+            col_copy(row + step, row).start()
+
+    for step in range(1, height):
+        @pl.when(row - step >= 0)
+        def _():
+            col_copy(row - step, row - step).wait_recv()
+
+    for step in range(1, height):
+        @pl.when(row + step < height)
+        def _():
+            col_copy(row + step, row).wait_send()
+
+    for copy in sends:
+        copy.wait_send()
+    prefix = row_prefix
+    for r in range(height):
+        prefix = prefix + col_buf[r]
+    y_ref[...] = prefix
+
+
+def scan_seq(x, collective_id):
+    n = lax.axis_size("seq")
+    width = 1
+    while (width + 1) * (width + 1) <= n:
+        width += 1
+    while n % width:
+        width -= 1
+    height = n // width
+    return pl.pallas_call(
+        functools.partial(scan_kernel, width),
+        out_shape=jax.ShapeDtypeStruct(x.shape, jnp.float32),
+        in_specs=[pl.BlockSpec(memory_space=pltpu.VMEM)],
+        out_specs=pl.BlockSpec(memory_space=pltpu.VMEM),
+        scratch_shapes=[
+            pltpu.VMEM((width,) + x.shape, x.dtype),
+            pltpu.VMEM((height,) + x.shape, jnp.float32),
+            pltpu.VMEM(x.shape, jnp.float32),
+            pltpu.SemaphoreType.DMA((width,)),
+            pltpu.SemaphoreType.DMA((width,)),
+            pltpu.SemaphoreType.DMA((height,)),
+            pltpu.SemaphoreType.DMA((height,)),
         ],
         compiler_params=pltpu.CompilerParams(collective_id=collective_id, has_side_effects=True),
     )(x)
@@ -363,12 +467,7 @@
     own = jnp.concatenate([own_zero, own_one, own_two], axis=2)
     slab_total = jnp.sum(own, axis=0)
     state_rows = slab_total.shape[0] * slab_total.shape[1]
-    pieces = gather_seq(
-        slab_total.astype(jnp.bfloat16).reshape(state_rows, HEAD_DIM), lax.axis_size("seq"), 5
-    ).astype(jnp.float32).reshape((-1,) + slab_total.shape)
-    count = pieces.shape[0]
-    earlier_mask = jnp.arange(count, dtype=jnp.int32) < my_slab
-    prefix = jnp.sum(jnp.where(earlier_mask[:, None, None, None], pieces, 0.0), axis=0)
+    prefix = scan_seq(slab_total.astype(jnp.bfloat16).reshape(state_rows, HEAD_DIM), 7).reshape(slab_total.shape)
     earlier = jnp.concatenate([jnp.zeros_like(own[:1]), jnp.cumsum(own, axis=0)[:-1]], axis=0) + prefix[None]
     query_linear, query_square = feature_parts(query_blocks.astype(jnp.float32))
     inter = earlier[:, :, 0][:, None] + jnp.einsum(

time: 240 us -> 234 us (0.975)
  Pallas kernels: 188 us -> 184 us
    pallas_call x1, Pallas kernels: 21 us -> 16.8 us  [scan_seq(): pl.pallas_call(functools.partial(scan_kernel, width), out_shape=jax.Shape...]
where the time goes in v11:
time: 234 us; the launch traced here: 233 us
  Pallas kernels  184 us (79%)
  matrix products  32 us (14%)
  local copies, waits for them, and re-layouts  11.6 us (5%)
  other arithmetic  5.23 us (2%)
    pallas_call x3, Pallas kernels, exchange_many(): pl.pallas_call(functools.partial(exchange_kernel, count), out_shape=tuple...  91.5 us
    pallas_call x1, Pallas kernels, opening(): pl.pallas_call(opening_kernel, out_shape=(jax.ShapeDtypeStruct(x.shape, x...  76.1 us
    pallas_call x1, Pallas kernels, scan_seq(): pl.pallas_call(functools.partial(scan_kernel, width), out_shape=jax.Shape...  16.8 us
    dot_general x1, matrix products, attend(): jnp.einsum('bhts,bshe->bthe', weights, value_blocks, preferred_element_ty...  8.11 us
    dot_general x1, matrix products, per_device(): jnp.einsum('tf,gfe->gte', rows, value_all, preferred_element_type=jnp.flo...  6.86 us
    dot_general x1, matrix products, per_device(): jnp.einsum('gte,gef->tf', hidden_got, w_out.reshape(groups, per_group * H...  5.75 us

profile of v11, /device:TPU:1, one launch (start us, length us, event | category | flops | bytes accessed | tf_op | source)
XLA Modules:
  0.0 233.4 jit_solution(3494516824730854258)
XLA Ops:
  0.0 76.1 %shard_map.64 = (bf16[16,224,128]{2,1,0:T(8,128)(2,1)}, bf16[16,2048,128]{2,1,0:T(8,128)(2,1)}) custom-call(bf16[16,224,128]{2,1,0:T(8,128)(2,1)} %bitcast.105, bf16[2048,128]{1,0:T(8,128)(2,1)} %w_ref.1), custom_call_target="tpu_custom_call" | custom-call | tf_op jit(solution)/shard_map/pallas_call | solution.py:422
  76.1 1.5 copy.32
  77.7 1.3 reshape.211
  79.0 0.0 copy-start.1
  79.0 0.0 copy-start.2
  79.0 6.9 %fusion.8.refs_1_ = bf16[16,224,128]{2,1,0:T(8,128)(2,1)} fusion(bf16[224,2048,1]{1,0,2:T(8,128)(2,1)} %reshape.211, bf16[16,2048,128]{2,1,0:T(8,128)(2,1)} %get-tuple-element.10), kind=kOutput, calls=%fused_computation.19 | convolution fusion | flops 1879506944 | bytes 10223616 | tf_op jit(solution)/shard_map/tf,gfe->gte/dot_general | solution.py:507
  85.9 0.0 copy-done.1
  85.9 0.6 copy.30
  86.5 0.0 copy-done.2
  86.5 0.6 copy.31
  87.2 2.6 %fusion.10.refs_0_ = bf16[16,32,224]{2,1,0:T(8,128)(2,1)} fusion(bf16[224,2048,1]{1,0,2:T(8,128)(2,1)} %reshape.211, bf16[2048,16,16]{0,2,1:T(8,128)(2,1)S(1)} %bitcast.97, bf16[2048,16,16]{0,2,1:T(8,128)(2,1)S(1)} %bitcast.96), kind=kOutput, calls=%fused_computation.22 | convolution fusion | flops 474071040 | bytes 3244032 | tf_op jit(solution)/shard_map/tf,fgd->gdt/dot_general | solution.py:506
  89.8 34.7 %shard_map.65 = (bf16[16,32,224]{2,1,0:T(8,128)(2,1)}, bf16[16,224,128]{2,1,0:T(8,128)(2,1)}) custom-call(bf16[16,32,224]{2,1,0:T(8,128)(2,1)} %fusion.10.refs_0_, bf16[16,224,128]{2,1,0:T(8,128)(2,1)} %fusion.8.refs_1_), custom_call_target="tpu_custom_call" | custom-call | tf_op jit(solution)/shard_map/pallas_call | solution.py:88
  124.5 0.0 copy-start
  124.5 1.2 copy.33
  125.6 0.4 reshape.202
  126.0 1.7 convolution_bitcast_fusion.2
  127.8 0.4 multiply_multiply_fusion.1
  128.1 0.0 copy-done
  128.1 1.8 convolution_bitcast_fusion.1
  129.9 0.1 convert_reduce_fusion
  130.1 0.7 fusion.14.x_ref
  130.8 16.8 %shard_map.66 = f32[273,128]{1,0:T(8,128)} custom-call(bf16[273,128]{1,0:T(8,128)(2,1)} %fusion.14.x_ref), custom_call_target="tpu_custom_call" | custom-call | tf_op jit(solution)/shard_map/pallas_call | solution.py:258
  147.6 0.1 fusion.15
  147.7 1.0 pad_add_fusion
  148.6 1.6 fusion.16
  150.3 0.4 multiply_multiply_fusion
  150.7 3.5 %fusion.13 = f32[4,128,896]{2,1,0:T(8,128)} fusion(f32[4,896,256]{1,2,0:T(8,128)S(1)} %bitcast.89, f32[4,1,273,128]{3,2,0,1:T(8,128)S(1)} %pad_add_fusion), kind=kOutput, calls=%fused_computation.28 | convolution fusion | flops 1409286144 | bytes 6029312 | tf_op jit(solution)/shard_map/bthf,bhfe->bthe/dot_general | solution.py:476
  154.2 1.1 iota_compare_fusion
  155.3 8.1 %multiply_reduce_fusion = (f32[4,896]{1,0:T(4,128)S(1)}, f32[4,896,1,128]{1,3,0,2:T(8,128)}) fusion(f32[4,128,896]{2,1,0:T(8,128)} %fusion.13, f32[4,128,896]{2,1,0:T(8,128)S(1)} %fusion.16, f32[4,128]{1,0:T(4,128)S(1)} %bitcast.110, bf16[4,896,128]{2,1,0:T(8,128)(2,1)S(1)} %bitcast.92, pred[896,896]{1,0:T(8,128)(4,1)} %iota_compare_fusion, ...), kind=kOutput, calls=%fused_computation.16 | convolution fusion | flops 949613056 | bytes 7471104 | tf_op jit(solution)/shard_map/bhts,bshe->bthe/dot_general | solution.py:485
  163.4 1.8 copy.41
  165.3 0.1 rsqrt.12
  165.3 0.8 dynamic_slice.3
  166.1 1.5 multiply_convert_fusion.refs_0_
  167.6 27.8 %shard_map.67 = bf16[16,224,128]{2,1,0:T(8,128)(2,1)} custom-call(bf16[16,224,128]{2,1,0:T(8,128)(2,1)} %multiply_convert_fusion.refs_0_), custom_call_target="tpu_custom_call" | custom-call | tf_op jit(solution)/shard_map/pallas_call | solution.py:88
  195.4 5.7 %fusion.9 = bf16[28,16,8,128]{3,2,1,0:T(8,128)(2,1)S(1)} fusion(bf16[16,224,128]{2,1,0:T(8,128)(2,1)} %shard_map.67, bf16[16,128,2048]{2,1,0:T(8,128)(2,1)} %bitcast.111), kind=kOutput, calls=%fused_computation.20 | convolution fusion | flops 1879506944 | bytes 10223616 | tf_op jit(solution)/shard_map/gte,gef->tf/dot_general | solution.py:521
  201.2 1.1 copy.72
  202.3 29.0 %shard_map.68 = bf16[16,224,128]{2,1,0:T(8,128)(2,1)} custom-call(bf16[16,224,128]{2,1,0:T(8,128)(2,1)} %bitcast.94), custom_call_target="tpu_custom_call" | custom-call | tf_op jit(solution)/shard_map/pallas_call | solution.py:88
  231.2 2.2 copy.74
  (7 shorter events, 0.1 us)
Async XLA Ops:
  79.0 6.9 %copy-start.1 = (bf16[2048,256]{1,0:T(8,128)(2,1)S(1)}, bf16[2048,256]{1,0:T(8,128)(2,1)}, u32[]{:S(2)}) copy-start(bf16[2048,256]{1,0:T(8,128)(2,1)} %param.7) | copy-start | bytes 3145732
  79.0 7.5 %copy-start.2 = (bf16[2048,256]{1,0:T(8,128)(2,1)S(1)}, bf16[2048,256]{1,0:T(8,128)(2,1)}, u32[]{:S(2)}) copy-start(bf16[2048,256]{1,0:T(8,128)(2,1)} %param.8) | copy-start | bytes 3145732
  124.5 3.7 %copy-start = (bf16[16,224,128]{2,1,0:T(8,128)(2,1)S(1)}, bf16[16,224,128]{2,1,0:T(8,128)(2,1)}, u32[]{:S(2)}) copy-start(bf16[16,224,128]{2,1,0:T(8,128)(2,1)} %get-tuple-element.11) | copy-start | bytes 2752516

commit v12 on v11

--- a/solution.py
+++ b/solution.py
@@ -452,6 +452,37 @@
     return got.reshape(groups * rows, cols)
 
 
+def intra_kernel(q_ref, k_ref, v_ref, o_ref):
+    scores = lax.dot_general(
+        q_ref[0], k_ref[0], (((1,), (1,)), ((), ())), preferred_element_type=jnp.float32
+    ) * FEAT ** (-0.5)
+    kernel = 1.0 + scores + 0.5 * scores * scores
+    rows = lax.broadcasted_iota(jnp.int32, kernel.shape, 0)
+    cols = lax.broadcasted_iota(jnp.int32, kernel.shape, 1)
+    weights = jnp.where(rows >= cols, kernel, 0.0).astype(jnp.bfloat16)
+    o_ref[0] = jnp.dot(weights, v_ref[0], preferred_element_type=jnp.float32)
+
+
+def intra_attention(query_rows, key_rows, value_rows):
+    tok_rows, per_group, _ = value_rows.shape
+    blocks = tok_rows // BLOCK
+    q = query_rows.transpose(1, 0, 2)
+    k = key_rows.transpose(1, 0, 2)
+    v = value_rows.transpose(1, 0, 2)
+    out = pl.pallas_call(
+        intra_kernel,
+        out_shape=jax.ShapeDtypeStruct((per_group, tok_rows, HEAD_DIM), jnp.float32),
+        grid=(per_group, blocks),
+        in_specs=[
+            pl.BlockSpec((1, BLOCK, FEAT), lambda h, b: (h, b, 0)),
+            pl.BlockSpec((1, BLOCK, FEAT), lambda h, b: (h, b, 0)),
+            pl.BlockSpec((1, BLOCK, HEAD_DIM), lambda h, b: (h, b, 0)),
+        ],
+        out_specs=pl.BlockSpec((1, BLOCK, HEAD_DIM), lambda h, b: (h, b, 0)),
+    )(q, k, v)
+    return out.transpose(1, 0, 2)
+
+
 def attend(query_rows, key_rows, value_rows, gain_mine, my_slab):
     highest = lax.Precision.HIGHEST
     tok_rows, per_group, _ = value_rows.shape
@@ -476,13 +507,7 @@
     inter = inter + jnp.einsum(
         "bthf,bhfe->bthe", query_square, earlier[:, :, 1 + FEAT :], precision=highest
     )
-    scores = jnp.einsum(
-        "bthf,bshf->bhts", query_blocks, key_blocks, preferred_element_type=jnp.float32
-    ) * FEAT ** (-0.5)
-    kernel = 1.0 + scores + 0.5 * scores * scores
-    causal = jnp.arange(BLOCK)[:, None] >= jnp.arange(BLOCK)[None, :]
-    weights = jnp.where(causal, kernel, 0.0).astype(jnp.bfloat16)
-    intra = jnp.einsum("bhts,bshe->bthe", weights, value_blocks, preferred_element_type=jnp.float32)
+    intra = intra_attention(query_rows, key_rows, value_rows).reshape(blocks, BLOCK, per_group, HEAD_DIM)
     numerator = (intra + inter).reshape(tok_rows, per_group, HEAD_DIM)
     mean_square = jnp.mean(numerator * numerator, axis=-1, keepdims=True)
     hidden = (numerator * lax.rsqrt(mean_square + 1e-05) * gain_mine).astype(jnp.bfloat16)

time: 234 us -> 240 us (1.026)
  matrix products: 32 us -> 24.9 us
  Pallas kernels: 184 us -> 191 us
  local copies, waits for them, and re-layouts: 11.6 us -> 18.2 us
    dot_general x1 -> x0, matrix products: 8.11 us -> none  [attend(): jnp.einsum('bhts,bshe->bthe', weights, value_blocks, preferred_element_ty...]
    pallas_call x0 -> x1, Pallas kernels: none -> 6.33 us  [intra_attention(): pl.pallas_call(intra_kernel, out_shape=jax.ShapeDtypeStruct((per_group, t...]
where the time goes in v12:
time: 240 us; the launch traced here: 238 us
  Pallas kernels  191 us (80%)
  matrix products  24.9 us (10%)
  local copies, waits for them, and re-layouts  18.2 us (8%)
  other arithmetic  4.06 us (2%)
    pallas_call x3, Pallas kernels, exchange_many(): pl.pallas_call(functools.partial(exchange_kernel, count), out_shape=tuple...  91.7 us
    pallas_call x1, Pallas kernels, opening(): pl.pallas_call(opening_kernel, out_shape=(jax.ShapeDtypeStruct(x.shape, x...  76.1 us
    pallas_call x1, Pallas kernels, scan_seq(): pl.pallas_call(functools.partial(scan_kernel, width), out_shape=jax.Shape...  16.8 us
    dot_general x1, matrix products, per_device(): jnp.einsum('tf,gfe->gte', rows, value_all, preferred_element_type=jnp.flo...  6.86 us
    pallas_call x1, Pallas kernels, intra_attention(): pl.pallas_call(intra_kernel, out_shape=jax.ShapeDtypeStruct((per_group, t...  6.33 us
    dot_general x1, matrix products, per_device(): jnp.einsum('gte,gef->tf', hidden_got, w_out.reshape(groups, per_group * H...  5.75 us

profile of v12, /device:TPU:1, one launch (start us, length us, event | category | flops | bytes accessed | tf_op | source)
XLA Modules:
  0.0 238.4 jit_solution(5341011079763716188)
XLA Ops:
  0.0 76.1 %shard_map.64 = (bf16[16,224,128]{2,1,0:T(8,128)(2,1)}, bf16[16,2048,128]{2,1,0:T(8,128)(2,1)}) custom-call(bf16[16,224,128]{2,1,0:T(8,128)(2,1)} %bitcast.87, bf16[2048,128]{1,0:T(8,128)(2,1)} %w_ref.1), custom_call_target="tpu_custom_call" | custom-call | tf_op jit(solution)/shard_map/pallas_call | solution.py:422
  76.1 1.5 copy.33
  77.7 1.3 reshape.194
  79.0 0.0 copy-start.2
  79.0 0.0 copy-start.3
  79.0 6.9 %fusion.5.refs_1_ = bf16[16,224,128]{2,1,0:T(8,128)(2,1)} fusion(bf16[224,2048,1]{1,0,2:T(8,128)(2,1)} %reshape.194, bf16[16,2048,128]{2,1,0:T(8,128)(2,1)} %get-tuple-element.10), kind=kOutput, calls=%fused_computation.15 | convolution fusion | flops 1879506944 | bytes 10223616 | tf_op jit(solution)/shard_map/tf,gfe->gte/dot_general | solution.py:532
  85.9 0.0 copy-done.2
  85.9 0.6 copy.31
  86.5 0.0 copy-done.3
  86.5 0.6 copy.32
  87.2 2.6 %fusion.7.refs_0_ = bf16[16,32,224]{2,1,0:T(8,128)(2,1)} fusion(bf16[224,2048,1]{1,0,2:T(8,128)(2,1)} %reshape.194, bf16[2048,16,16]{0,2,1:T(8,128)(2,1)S(1)} %bitcast.85, bf16[2048,16,16]{0,2,1:T(8,128)(2,1)S(1)} %bitcast.84), kind=kOutput, calls=%fused_computation.18 | convolution fusion | flops 474071040 | bytes 3244032 | tf_op jit(solution)/shard_map/tf,fgd->gdt/dot_general | solution.py:531
  89.8 34.7 %shard_map.65 = (bf16[16,32,224]{2,1,0:T(8,128)(2,1)}, bf16[16,224,128]{2,1,0:T(8,128)(2,1)}) custom-call(bf16[16,32,224]{2,1,0:T(8,128)(2,1)} %fusion.7.refs_0_, bf16[16,224,128]{2,1,0:T(8,128)(2,1)} %fusion.5.refs_1_), custom_call_target="tpu_custom_call" | custom-call | tf_op jit(solution)/shard_map/pallas_call | solution.py:88
  124.4 0.0 copy-start
  124.4 1.4 copy.34
  125.9 2.1 fusion.21
  128.0 1.4 copy.35
  129.4 0.0 copy-done
  129.4 0.5 convolution_bitcast_fusion.2
  129.9 0.4 multiply_multiply_fusion.1
  130.3 1.8 convolution_bitcast_fusion.1
  132.1 0.1 convert_reduce_fusion
  132.3 0.7 fusion.10.x_ref
  133.0 16.8 %shard_map.67 = f32[273,128]{1,0:T(8,128)} custom-call(bf16[273,128]{1,0:T(8,128)(2,1)} %fusion.10.x_ref), custom_call_target="tpu_custom_call" | custom-call | tf_op jit(solution)/shard_map/pallas_call | solution.py:258
  149.8 0.1 fusion.11
  149.9 1.0 pad_add_fusion
  150.8 0.3 copy.38
  151.1 2.9 %fusion.12 = f32[4,128,896]{2,1,0:T(8,128)} fusion(f32[4,896,16]{1,2,0:T(8,128)S(1)} %copy.38, f32[4,1,273,128]{3,2,0,1:T(8,128)S(1)} %pad_add_fusion), kind=kOutput, calls=%fused_computation.26 | convolution fusion | flops 88137728 | bytes 2097152 | tf_op jit(solution)/shard_map/bthf,bhfe->bthe/dot_general | solution.py:504
  154.0 6.3 %shard_map.66 = f32[1,3584,128]{2,1,0:T(8,128)} custom-call(bf16[1,3584,16]{2,1,0:T(8,128)(2,1)} %get-tuple-element.14.q_ref, bf16[1,3584,16]{2,1,0:T(8,128)(2,1)} %get-tuple-element.15.k_ref, bf16[1,3584,128]{2,1,0:T(8,128)(2,1)} %bitcast.73), custom_call_target="tpu_custom_call" | custom-call | tf_op jit(solution)/shard_map/pallas_call | solution.py:472
  160.3 1.8 copy.43
  162.1 0.0 copy-start.1
  162.1 0.4 multiply_multiply_fusion
  162.5 1.1 copy-done.1
  163.6 4.5 %multiply_reduce_fusion = (f32[4,896]{1,0:T(4,128)}, f32[4,896,1,128]{1,3,0,2:T(8,128)}) fusion(f32[4,896,1,128]{1,3,0,2:T(8,128)S(1)} %copy.43, f32[4,896,256]{1,2,0:T(8,128)S(1)} %bitcast.76, f32[4,1,273,128]{3,2,0,1:T(8,128)S(1)} %pad_add_fusion, f32[4,128,896]{2,1,0:T(8,128)S(1)} %copy-done.1, f32[4,128]{1,0:T(4,128)S(1)} %bitcast.92), kind=kOutput, calls=%fused_computation.12 | convolution fusion | flops 1411576320 | bytes 9715712 | tf_op jit(solution)/shard_map/bthf,bhfe->bthe/dot_general | solution.py:507
  168.1 0.0 copy-start.4
  168.1 1.8 copy.44
  169.9 0.0 copy-done.4
  170.0 0.1 rsqrt.12
  170.1 0.8 dynamic_slice.3
  170.8 1.5 multiply_convert_fusion.refs_0_
  172.3 28.1 %shard_map.68 = bf16[16,224,128]{2,1,0:T(8,128)(2,1)} custom-call(bf16[16,224,128]{2,1,0:T(8,128)(2,1)} %multiply_convert_fusion.refs_0_), custom_call_target="tpu_custom_call" | custom-call | tf_op jit(solution)/shard_map/pallas_call | solution.py:88
  200.4 5.7 %fusion.6 = bf16[28,16,8,128]{3,2,1,0:T(8,128)(2,1)S(1)} fusion(bf16[16,224,128]{2,1,0:T(8,128)(2,1)} %shard_map.68, bf16[16,128,2048]{2,1,0:T(8,128)(2,1)} %bitcast.93), kind=kOutput, calls=%fused_computation.16 | convolution fusion | flops 1879506944 | bytes 10223616 | tf_op jit(solution)/shard_map/gte,gef->tf/dot_general | solution.py:546
  206.1 1.1 copy.50
  207.2 29.0 %shard_map.69 = bf16[16,224,128]{2,1,0:T(8,128)(2,1)} custom-call(bf16[16,224,128]{2,1,0:T(8,128)(2,1)} %bitcast.80), custom_call_target="tpu_custom_call" | custom-call | tf_op jit(solution)/shard_map/pallas_call | solution.py:88
  236.2 2.2 copy.52
  (4 shorter events, 0.1 us)
Async XLA Ops:
  79.0 6.9 %copy-start.2 = (bf16[2048,256]{1,0:T(8,128)(2,1)S(1)}, bf16[2048,256]{1,0:T(8,128)(2,1)}, u32[]{:S(2)}) copy-start(bf16[2048,256]{1,0:T(8,128)(2,1)} %param.7) | copy-start | bytes 3145732
  79.0 7.5 %copy-start.3 = (bf16[2048,256]{1,0:T(8,128)(2,1)S(1)}, bf16[2048,256]{1,0:T(8,128)(2,1)}, u32[]{:S(2)}) copy-start(bf16[2048,256]{1,0:T(8,128)(2,1)} %param.8) | copy-start | bytes 3145732
  124.4 5.0 %copy-start = (bf16[16,224,128]{2,1,0:T(8,128)(2,1)S(1)}, bf16[16,224,128]{2,1,0:T(8,128)(2,1)}, u32[]{:S(2)}) copy-start(bf16[16,224,128]{2,1,0:T(8,128)(2,1)} %get-tuple-element.12) | copy-start | bytes 2752516
  162.1 1.5 copy-start.1
  168.1 1.8 copy-start.4

commit v13 on v11

--- a/solution.py
+++ b/solution.py
@@ -450,6 +450,86 @@
     rows, _, cols = x.shape
     got = exchange(x.transpose(1, 0, 2), collective_id)
     return got.reshape(groups * rows, cols)
+
+
+def closing_kernel(x_ref, w_ref, y_ref, got, rows, out, back, send_sem, recv_sem, own_sem):
+    n = x_ref.shape[0]
+    cols = out.shape[2]
+    me = chan_index()
+    slab = lax.axis_index("seq")
+    barrier = pltpu.get_barrier_semaphore()
+    for step in range(1, n):
+        peer = lax.rem(me + step, n)
+        pl.semaphore_signal(barrier, inc=1, device_id=chan_device(slab, peer), device_id_type=MESH)
+    pl.semaphore_wait(barrier, n - 1)
+
+    def remote(phase, src, dst, peer, sender):
+        return pltpu.make_async_remote_copy(
+            src_ref=src,
+            dst_ref=dst,
+            send_sem=send_sem.at[phase, peer],
+            recv_sem=recv_sem.at[phase, sender],
+            device_id=chan_device(slab, peer),
+            device_id_type=MESH,
+        )
+
+    sends = []
+    for phase, (source, landing) in enumerate(((x_ref, got), (out, back))):
+        own = pltpu.make_async_copy(source.at[me], landing.at[me], own_sem.at[phase])
+        if phase == 1:
+            hidden_rows = rows[...]
+            for step in range(n):
+                c = lax.rem(me + step, n)
+                block = w_ref[:, pl.ds(pl.multiple_of(c * cols, cols), cols)]
+                out[c] = jnp.dot(hidden_rows, block, preferred_element_type=jnp.float32).astype(out.dtype)
+                if step == 0:
+                    own.start()
+                else:
+                    copy = remote(phase, out.at[c], back.at[me], c, me)
+                    copy.start()
+                    sends.append(copy)
+        else:
+            own.start()
+            for step in range(1, n):
+                peer = lax.rem(me + step, n)
+                copy = remote(phase, x_ref.at[peer], got.at[me], peer, me)
+                copy.start()
+                sends.append(copy)
+        for step in range(1, n):
+            source_dev = lax.rem(me + n - step, n)
+            remote(phase, source.at[source_dev], landing.at[source_dev], source_dev, source_dev).wait_recv()
+        own.wait()
+        if phase == 0:
+            width = got.shape[2]
+            for g in range(n):
+                rows[:, g * width : (g + 1) * width] = got[g]
+    for copy in sends:
+        copy.wait_send()
+    y_ref[...] = back[...]
+
+
+def closing(hidden_blocks, w_out, collective_id):
+    n, chunk, width = hidden_blocks.shape
+    cols = w_out.shape[1] // n
+    block = (n, chunk, cols)
+    return pl.pallas_call(
+        closing_kernel,
+        out_shape=jax.ShapeDtypeStruct(block, hidden_blocks.dtype),
+        in_specs=[pl.BlockSpec(memory_space=pltpu.VMEM)] * 2,
+        out_specs=pl.BlockSpec(memory_space=pltpu.VMEM),
+        scratch_shapes=[
+            pltpu.VMEM(hidden_blocks.shape, hidden_blocks.dtype),
+            pltpu.VMEM((chunk, n * width), hidden_blocks.dtype),
+            pltpu.VMEM(block, hidden_blocks.dtype),
+            pltpu.VMEM(block, hidden_blocks.dtype),
+            pltpu.SemaphoreType.DMA((2, n)),
+            pltpu.SemaphoreType.DMA((2, n)),
+            pltpu.SemaphoreType.DMA((2,)),
+        ],
+        compiler_params=pltpu.CompilerParams(
+            collective_id=collective_id, has_side_effects=True, vmem_limit_bytes=48 * 1024 * 1024
+        ),
+    )(hidden_blocks, w_out)
 
 
 def attend(query_rows, key_rows, value_rows, gain_mine, my_slab):
@@ -516,17 +596,9 @@
         per_group, HEAD_DIM
     )
     hidden = attend(query_rows, key_rows, value_rows, gain_mine, my_slab)
-    hidden_got = exchange(hidden.reshape(groups, chunk, per_group * HEAD_DIM), 3)
     out_cols = w_out.shape[1] // groups
-    mixed_rows = jnp.einsum(
-        "gte,gef->tf",
-        hidden_got,
-        w_out.reshape(groups, per_group * HEAD_DIM, w_out.shape[1]),
-        preferred_element_type=jnp.float32,
-    ).astype(jnp.bfloat16)
-    mixed_blocks = mixed_rows.reshape(chunk, groups, out_cols).transpose(1, 0, 2)
-    return exchange(mixed_blocks, 4).reshape(tok_rows, out_cols)
-
+    mixed_blocks = closing(hidden.reshape(groups, chunk, per_group * HEAD_DIM), w_out, 3)
+    return mixed_blocks.reshape(tok_rows, out_cols)
 
 def solution(mesh):
     seq, chan = mesh.devices.shape

time: 234 us -> 223 us (0.953)
  matrix products: 32 us -> 26.2 us
    pallas_call x3 -> x1, Pallas kernels: 91.5 us -> 34.7 us  [exchange_many(): pl.pallas_call(functools.partial(exchange_kernel, count), out_shape=tuple...]
    pallas_call x0 -> x1, Pallas kernels: none -> 54.1 us  [closing(): pl.pallas_call(closing_kernel, out_shape=jax.ShapeDtypeStruct(block, hidd...]
    dot_general x1 -> x0, matrix products: 5.75 us -> none  [per_device(): jnp.einsum('gte,gef->tf', hidden_got, w_out.reshape(groups, per_group * H...]
where the time goes in v13:
time: 223 us; the launch traced here: 222 us
  Pallas kernels  182 us (82%)
  matrix products  26.2 us (12%)
  local copies, waits for them, and re-layouts  9.28 us (4%)
  other arithmetic  4.3 us (2%)
    pallas_call x1, Pallas kernels, opening(): pl.pallas_call(opening_kernel, out_shape=(jax.ShapeDtypeStruct(x.shape, x...  76.1 us
    pallas_call x1, Pallas kernels, closing(): pl.pallas_call(closing_kernel, out_shape=jax.ShapeDtypeStruct(block, hidd...  54.1 us
    pallas_call x1, Pallas kernels, exchange_many(): pl.pallas_call(functools.partial(exchange_kernel, count), out_shape=tuple...  34.7 us
    pallas_call x1, Pallas kernels, scan_seq(): pl.pallas_call(functools.partial(scan_kernel, width), out_shape=jax.Shape...  16.8 us
    dot_general x1, matrix products, attend(): jnp.einsum('bhts,bshe->bthe', weights, value_blocks, preferred_element_ty...  8.11 us
    dot_general x1, matrix products, per_device(): jnp.einsum('tf,gfe->gte', rows, value_all, preferred_element_type=jnp.flo...  6.86 us

profile of v13, /device:TPU:1, one launch (start us, length us, event | category | flops | bytes accessed | tf_op | source)
XLA Modules:
  0.0 221.7 jit_solution(9690273213433703899)
XLA Ops:
  0.0 76.1 %shard_map.64 = (bf16[16,224,128]{2,1,0:T(8,128)(2,1)}, bf16[16,2048,128]{2,1,0:T(8,128)(2,1)}) custom-call(bf16[16,224,128]{2,1,0:T(8,128)(2,1)} %bitcast.87, bf16[2048,128]{1,0:T(8,128)(2,1)} %w_ref.2), custom_call_target="tpu_custom_call" | custom-call | tf_op jit(solution)/shard_map/pallas_call | solution.py:422
  76.1 1.5 copy.31
  77.7 1.3 reshape.203
  79.0 0.0 copy-start.1
  79.0 0.0 copy-start.2
  79.0 6.9 %fusion.7.refs_1_ = bf16[16,224,128]{2,1,0:T(8,128)(2,1)} fusion(bf16[224,2048,1]{1,0,2:T(8,128)(2,1)} %reshape.203, bf16[16,2048,128]{2,1,0:T(8,128)(2,1)} %get-tuple-element.10), kind=kOutput, calls=%fused_computation.17 | convolution fusion | flops 1879506944 | bytes 10223616 | tf_op jit(solution)/shard_map/tf,gfe->gte/dot_general | solution.py:587
  85.9 0.0 copy-done.1
  85.9 0.6 copy.29
  86.5 0.0 copy-done.2
  86.5 0.6 copy.30
  87.2 2.6 %fusion.8.refs_0_ = bf16[16,32,224]{2,1,0:T(8,128)(2,1)} fusion(bf16[224,2048,1]{1,0,2:T(8,128)(2,1)} %reshape.203, bf16[2048,16,16]{0,2,1:T(8,128)(2,1)S(1)} %bitcast.79, bf16[2048,16,16]{0,2,1:T(8,128)(2,1)S(1)} %bitcast.78), kind=kOutput, calls=%fused_computation.19 | convolution fusion | flops 474071040 | bytes 3244032 | tf_op jit(solution)/shard_map/tf,fgd->gdt/dot_general | solution.py:586
  89.8 34.7 %shard_map.65 = (bf16[16,32,224]{2,1,0:T(8,128)(2,1)}, bf16[16,224,128]{2,1,0:T(8,128)(2,1)}) custom-call(bf16[16,32,224]{2,1,0:T(8,128)(2,1)} %fusion.8.refs_0_, bf16[16,224,128]{2,1,0:T(8,128)(2,1)} %fusion.7.refs_1_), custom_call_target="tpu_custom_call" | custom-call | tf_op jit(solution)/shard_map/pallas_call | solution.py:88
  124.5 0.0 copy-start
  124.5 1.2 copy.32
  125.6 0.4 reshape.196
  126.0 1.7 convolution_bitcast_fusion.1
  127.8 0.4 multiply_multiply_fusion.1
  128.1 0.0 copy-done
  128.1 1.8 convolution_bitcast_fusion
  129.9 0.1 convert_reduce_fusion
  130.1 0.7 fusion.12.x_ref
  130.8 16.8 %shard_map.66 = f32[273,128]{1,0:T(8,128)} custom-call(bf16[273,128]{1,0:T(8,128)(2,1)} %fusion.12.x_ref), custom_call_target="tpu_custom_call" | custom-call | tf_op jit(solution)/shard_map/pallas_call | solution.py:258
  147.6 0.1 fusion.13
  147.7 1.0 pad_add_fusion
  148.6 1.6 fusion.14
  150.3 0.4 multiply_multiply_fusion
  150.7 3.5 %fusion.11 = f32[4,128,896]{2,1,0:T(8,128)} fusion(f32[4,896,256]{1,2,0:T(8,128)S(1)} %bitcast.73, f32[4,1,273,128]{3,2,0,1:T(8,128)S(1)} %pad_add_fusion), kind=kOutput, calls=%fused_computation.24 | convolution fusion | flops 1409286144 | bytes 6029312 | tf_op jit(solution)/shard_map/bthf,bhfe->bthe/dot_general | solution.py:556
  154.2 1.1 iota_compare_fusion
  155.3 8.1 %multiply_reduce_fusion = (f32[4,896]{1,0:T(4,128)S(1)}, f32[4,896,1,128]{1,3,0,2:T(8,128)}) fusion(f32[4,128,896]{2,1,0:T(8,128)} %fusion.11, f32[4,128,896]{2,1,0:T(8,128)S(1)} %fusion.14, f32[4,128]{1,0:T(4,128)S(1)} %bitcast.92, bf16[4,896,128]{2,1,0:T(8,128)(2,1)S(1)} %bitcast.76, pred[896,896]{1,0:T(8,128)(4,1)} %iota_compare_fusion, ...), kind=kOutput, calls=%fused_computation.14 | convolution fusion | flops 949613056 | bytes 7471104 | tf_op jit(solution)/shard_map/bhts,bshe->bthe/dot_general | solution.py:565
  163.4 1.8 copy.40
  165.3 0.1 rsqrt.12
  165.3 0.8 dynamic_slice.3
  166.1 0.5 multiply_convert_fusion.x_ref
  166.7 54.1 %shard_map.67 = bf16[16,224,128]{2,1,0:T(8,128)(2,1)S(1)} custom-call(bf16[16,224,128]{2,1,0:T(8,128)(2,1)S(1)} %multiply_convert_fusion.x_ref, bf16[2048,2048]{1,0:T(8,128)(2,1)} %w_ref.3), custom_call_target="tpu_custom_call" | custom-call | tf_op jit(solution)/shard_map/pallas_call | solution.py:515
  220.7 0.9 copy.69
  (7 shorter events, 0.1 us)
Async XLA Ops:
  79.0 6.9 %copy-start.1 = (bf16[2048,256]{1,0:T(8,128)(2,1)S(1)}, bf16[2048,256]{1,0:T(8,128)(2,1)}, u32[]{:S(2)}) copy-start(bf16[2048,256]{1,0:T(8,128)(2,1)} %param.7) | copy-start | bytes 3145732
  79.0 7.5 %copy-start.2 = (bf16[2048,256]{1,0:T(8,128)(2,1)S(1)}, bf16[2048,256]{1,0:T(8,128)(2,1)}, u32[]{:S(2)}) copy-start(bf16[2048,256]{1,0:T(8,128)(2,1)} %param.8) | copy-start | bytes 3145732
  124.5 3.7 %copy-start = (bf16[16,224,128]{2,1,0:T(8,128)(2,1)S(1)}, bf16[16,224,128]{2,1,0:T(8,128)(2,1)}, u32[]{:S(2)}) copy-start(bf16[16,224,128]{2,1,0:T(8,128)(2,1)} %get-tuple-element.11) | copy-start | bytes 2752516

commit v14 on v13

--- a/solution.py
+++ b/solution.py
@@ -530,6 +530,87 @@
             collective_id=collective_id, has_side_effects=True, vmem_limit_bytes=48 * 1024 * 1024
         ),
     )(hidden_blocks, w_out)
+
+
+def middle_kernel(rows_ref, w_ref, wqk_ref, qk_out, v_out, qk_send, v_send, qk_got, v_got, send_sem, recv_sem, own_sem):
+    n = w_ref.shape[0]
+    me = chan_index()
+    slab = lax.axis_index("seq")
+    barrier = pltpu.get_barrier_semaphore()
+    for step in range(1, n):
+        peer = lax.rem(me + step, n)
+        pl.semaphore_signal(barrier, inc=1, device_id=chan_device(slab, peer), device_id_type=MESH)
+    pl.semaphore_wait(barrier, n - 1)
+    pairs = ((qk_send, qk_got), (v_send, v_got))
+
+    def remote(kind, peer, sender, slot):
+        source, landing = pairs[kind]
+        return pltpu.make_async_remote_copy(
+            src_ref=source.at[slot],
+            dst_ref=landing.at[sender],
+            send_sem=send_sem.at[kind, peer],
+            recv_sem=recv_sem.at[kind, sender],
+            device_id=chan_device(slab, peer),
+            device_id_type=MESH,
+        )
+
+    rows = rows_ref[...]
+    owns = []
+    sends = []
+    for step in range(n):
+        g = lax.rem(me + step, n)
+        v_send[g] = jnp.dot(rows, w_ref[g], preferred_element_type=jnp.float32).astype(v_send.dtype)
+        qk_send[g] = lax.dot_general(
+            wqk_ref[g], rows, (((1,), (1,)), ((), ())), preferred_element_type=jnp.float32
+        ).astype(qk_send.dtype)
+        for kind in range(2):
+            source, landing = pairs[kind]
+            if step == 0:
+                own = pltpu.make_async_copy(source.at[me], landing.at[me], own_sem.at[kind])
+                own.start()
+                owns.append(own)
+            else:
+                copy = remote(kind, g, me, g)
+                copy.start()
+                sends.append(copy)
+    for step in range(1, n):
+        source_dev = lax.rem(me + n - step, n)
+        for kind in range(2):
+            remote(kind, source_dev, source_dev, source_dev).wait_recv()
+    for own in owns:
+        own.wait()
+    for copy in sends:
+        copy.wait_send()
+    qk_out[...] = qk_got[...]
+    v_out[...] = v_got[...]
+
+
+def middle(rows, w_all, wqk_t, collective_id):
+    n = w_all.shape[0]
+    chunk = rows.shape[0]
+    qk_shape = (n, wqk_t.shape[1], chunk)
+    v_shape = (n, chunk, w_all.shape[2])
+    return pl.pallas_call(
+        middle_kernel,
+        out_shape=(
+            jax.ShapeDtypeStruct(qk_shape, rows.dtype),
+            jax.ShapeDtypeStruct(v_shape, rows.dtype),
+        ),
+        in_specs=[pl.BlockSpec(memory_space=pltpu.VMEM)] * 3,
+        out_specs=(pl.BlockSpec(memory_space=pltpu.VMEM), pl.BlockSpec(memory_space=pltpu.VMEM)),
+        scratch_shapes=[
+            pltpu.VMEM(qk_shape, rows.dtype),
+            pltpu.VMEM(v_shape, rows.dtype),
+            pltpu.VMEM(qk_shape, rows.dtype),
+            pltpu.VMEM(v_shape, rows.dtype),
+            pltpu.SemaphoreType.DMA((2, n)),
+            pltpu.SemaphoreType.DMA((2, n)),
+            pltpu.SemaphoreType.DMA((2,)),
+        ],
+        compiler_params=pltpu.CompilerParams(
+            collective_id=collective_id, has_side_effects=True, vmem_limit_bytes=48 * 1024 * 1024
+        ),
+    )(rows, w_all, wqk_t)
 
 
 def attend(query_rows, key_rows, value_rows, gain_mine, my_slab):
@@ -583,9 +664,7 @@
     w_qk = jnp.concatenate(
         [w_query.reshape(d_model, groups, pf), w_key.reshape(d_model, groups, pf)], axis=2
     )
-    qk_t = jnp.einsum("tf,fgd->gdt", rows, w_qk, preferred_element_type=jnp.float32).astype(jnp.bfloat16)
-    value = jnp.einsum("tf,gfe->gte", rows, value_all, preferred_element_type=jnp.float32).astype(jnp.bfloat16)
-    qk_got, value_got = exchange_many((qk_t, value), 2)
+    qk_got, value_got = middle(rows, value_all, w_qk.transpose(1, 2, 0), 2)
     tok_rows = groups * chunk
     qk_rows = qk_got.transpose(0, 2, 1).reshape(tok_rows, 2 * pf)
     query_rows = qk_rows[:, :pf].reshape(tok_rows, per_group, FEAT)

time: 223 us -> 220 us (0.987)
  matrix products: 26.2 us -> 15.4 us
  Pallas kernels: 182 us -> 189 us
    dot_general x2 -> x0, matrix products: 9.48 us -> none  [the longest x1 6.86 us: per_device(): jnp.einsum('tf,gfe->gte', rows, value_all, preferred_element_type=jnp.flo...]
    pallas_call x1, Pallas kernels: 34.7 us -> 39.6 us  [middle(): pl.pallas_call(middle_kernel, out_shape=(jax.ShapeDtypeStruct(qk_shape, r...]
    unnamed x9 -> x3, local copies, waits for them, and re-layouts: 2.22 us -> 4.69 us
where the time goes in v14:
time: 220 us; the launch traced here: 219 us
  Pallas kernels  189 us (86%)
  matrix products  15.4 us (7%)
  local copies, waits for them, and re-layouts  9.16 us (4%)
  other arithmetic  5.7 us (3%)
    pallas_call x1, Pallas kernels, opening(): pl.pallas_call(opening_kernel, out_shape=(jax.ShapeDtypeStruct(x.shape, x...  76.3 us
    pallas_call x1, Pallas kernels, closing(): pl.pallas_call(closing_kernel, out_shape=jax.ShapeDtypeStruct(block, hidd...  54.4 us
    pallas_call x1, Pallas kernels, middle(): pl.pallas_call(middle_kernel, out_shape=(jax.ShapeDtypeStruct(qk_shape, r...  39.6 us
    pallas_call x1, Pallas kernels, scan_seq(): pl.pallas_call(functools.partial(scan_kernel, width), out_shape=jax.Shape...  18.3 us
    dot_general x1, matrix products, attend(): jnp.einsum('bhts,bshe->bthe', weights, value_blocks, preferred_element_ty...  7.9 us
    unnamed x3, local copies, waits for them, and re-layouts  4.69 us

profile of v14, /device:TPU:1, one launch (start us, length us, event | category | flops | bytes accessed | tf_op | source)
XLA Modules:
  0.0 219.1 jit_solution(4269734533391079315)
XLA Ops:
  0.0 0.8 dynamic_slice.3
  0.8 1.1 iota_compare_fusion
  1.9 1.5 copy.31
  3.4 2.3 %copy.32 = bf16[2048,256]{0,1:T(8,128)(2,1)} copy(bf16[2048,256]{1,0:T(8,128)(2,1)} %param.8) | data formatting | bytes 2097152 | tf_op args[2]
  5.7 1.4 maximum_bitcast_fusion.wqk_ref
  7.1 76.3 %shard_map.64 = (bf16[16,224,128]{2,1,0:T(8,128)(2,1)}, bf16[16,2048,128]{2,1,0:T(8,128)(2,1)}) custom-call(bf16[16,224,128]{2,1,0:T(8,128)(2,1)} %bitcast.89, bf16[2048,128]{1,0:T(8,128)(2,1)} %w_ref.2), custom_call_target="tpu_custom_call" | custom-call | tf_op jit(solution)/shard_map/pallas_call | solution.py:422
  83.3 1.3 copy_bitcast_fusion.rows_ref
  84.6 39.6 %shard_map.65 = (bf16[16,32,224]{2,1,0:T(8,128)(2,1)S(1)}, bf16[16,224,128]{2,1,0:T(8,128)(2,1)S(1)}) custom-call(bf16[224,2048]{1,0:T(8,128)(2,1)S(1)} %copy_bitcast_fusion.rows_ref, bf16[16,2048,128]{2,1,0:T(8,128)(2,1)} %get-tuple-element.10.w_ref, bf16[16,32,2048]{2,1,0:T(8,128)(2,1)S(1)} %maximum_bitcast_fusion.wqk_ref), custom_call_target="tpu_custom_call" | custom-call | tf_op jit(solution)/shard_map/pallas_call | solution.py:593
  124.3 0.2 copy.33
  124.4 0.4 reshape.196
  124.8 0.1 convert_reduce_fusion
  125.0 0.5 convolution_bitcast_fusion.1
  125.5 0.4 multiply_multiply_fusion.1
  125.9 1.8 convolution_bitcast_fusion
  127.7 0.7 fusion.4.x_ref
  128.4 0.1 fusion.5
  128.5 18.3 %shard_map.66 = f32[273,128]{1,0:T(8,128)} custom-call(bf16[273,128]{1,0:T(8,128)(2,1)} %fusion.4.x_ref), custom_call_target="tpu_custom_call" | custom-call | tf_op jit(solution)/shard_map/pallas_call | solution.py:258
  146.8 0.9 pad_add_fusion
  147.8 1.6 fusion.6
  149.4 0.4 multiply_multiply_fusion
  149.8 3.5 %fusion.3 = f32[4,128,896]{2,1,0:T(8,128)} fusion(f32[4,896,256]{1,2,0:T(8,128)S(1)} %bitcast.79, f32[4,1,273,128]{3,2,0,1:T(8,128)S(1)} %pad_add_fusion), kind=kOutput, calls=%fused_computation.19 | convolution fusion | flops 1409286144 | bytes 6029312 | tf_op jit(solution)/shard_map/bthf,bhfe->bthe/dot_general | solution.py:637
  153.3 7.9 %multiply_reduce_fusion = (f32[4,896]{1,0:T(4,128)S(1)}, f32[4,896,1,128]{1,3,0,2:T(8,128)}) fusion(f32[4,128,896]{2,1,0:T(8,128)} %fusion.3, f32[4,128,896]{2,1,0:T(8,128)S(1)} %fusion.6, f32[4,128]{1,0:T(4,128)S(1)} %bitcast.93, bf16[4,896,128]{2,1,0:T(8,128)(2,1)S(1)} %bitcast.75, pred[896,896]{1,0:T(8,128)(4,1)} %iota_compare_fusion, ...), kind=kOutput, calls=%fused_computation.11 | convolution fusion | flops 949613056 | bytes 7471104 | tf_op jit(solution)/shard_map/bhts,bshe->bthe/dot_general | solution.py:646
  161.2 0.1 rsqrt.12
  161.3 1.8 copy.41
  163.1 0.5 multiply_convert_fusion.x_ref
  163.7 54.4 %shard_map.67 = bf16[16,224,128]{2,1,0:T(8,128)(2,1)S(1)} custom-call(bf16[16,224,128]{2,1,0:T(8,128)(2,1)S(1)} %multiply_convert_fusion.x_ref, bf16[2048,2048]{1,0:T(8,128)(2,1)} %w_ref.3), custom_call_target="tpu_custom_call" | custom-call | tf_op jit(solution)/shard_map/pallas_call | solution.py:515
  218.1 0.9 copy.72
  (7 shorter events, 0.1 us)

commit v15 on v14

--- a/solution.py
+++ b/solution.py
@@ -532,7 +532,7 @@
     )(hidden_blocks, w_out)
 
 
-def middle_kernel(rows_ref, w_ref, wqk_ref, qk_out, v_out, qk_send, v_send, qk_got, v_got, send_sem, recv_sem, own_sem):
+def middle_kernel(rows_ref, w_ref, wq_ref, wk_ref, qk_out, v_out, qk_send, v_send, qk_got, v_got, q_all, k_all, send_sem, recv_sem, own_sem):
     n = w_ref.shape[0]
     me = chan_index()
     slab = lax.axis_index("seq")
@@ -555,14 +555,17 @@
         )
 
     rows = rows_ref[...]
+    pf = qk_send.shape[1] // 2
+    q_all[...] = jnp.dot(rows, wq_ref[...], preferred_element_type=jnp.float32).T
+    k_all[...] = jnp.dot(rows, wk_ref[...], preferred_element_type=jnp.float32).T
     owns = []
     sends = []
     for step in range(n):
         g = lax.rem(me + step, n)
         v_send[g] = jnp.dot(rows, w_ref[g], preferred_element_type=jnp.float32).astype(v_send.dtype)
-        qk_send[g] = lax.dot_general(
-            wqk_ref[g], rows, (((1,), (1,)), ((), ())), preferred_element_type=jnp.float32
-        ).astype(qk_send.dtype)
+        head = pl.ds(pl.multiple_of(g * pf, pf), pf)
+        qk_send[g, :pf, :] = q_all[head, :].astype(qk_send.dtype)
+        qk_send[g, pf:, :] = k_all[head, :].astype(qk_send.dtype)
         for kind in range(2):
             source, landing = pairs[kind]
             if step == 0:
@@ -585,10 +588,10 @@
     v_out[...] = v_got[...]
 
 
-def middle(rows, w_all, wqk_t, collective_id):
+def middle(rows, w_all, w_query, w_key, collective_id):
     n = w_all.shape[0]
     chunk = rows.shape[0]
-    qk_shape = (n, wqk_t.shape[1], chunk)
+    qk_shape = (n, 2 * w_query.shape[1] // n, chunk)
     v_shape = (n, chunk, w_all.shape[2])
     return pl.pallas_call(
         middle_kernel,
@@ -596,13 +599,15 @@
             jax.ShapeDtypeStruct(qk_shape, rows.dtype),
             jax.ShapeDtypeStruct(v_shape, rows.dtype),
         ),
-        in_specs=[pl.BlockSpec(memory_space=pltpu.VMEM)] * 3,
+        in_specs=[pl.BlockSpec(memory_space=pltpu.VMEM)] * 4,
         out_specs=(pl.BlockSpec(memory_space=pltpu.VMEM), pl.BlockSpec(memory_space=pltpu.VMEM)),
         scratch_shapes=[
             pltpu.VMEM(qk_shape, rows.dtype),
             pltpu.VMEM(v_shape, rows.dtype),
             pltpu.VMEM(qk_shape, rows.dtype),
             pltpu.VMEM(v_shape, rows.dtype),
+            pltpu.VMEM((w_query.shape[1], chunk), jnp.float32),
+            pltpu.VMEM((w_key.shape[1], chunk), jnp.float32),
             pltpu.SemaphoreType.DMA((2, n)),
             pltpu.SemaphoreType.DMA((2, n)),
             pltpu.SemaphoreType.DMA((2,)),
@@ -610,7 +615,7 @@
         compiler_params=pltpu.CompilerParams(
             collective_id=collective_id, has_side_effects=True, vmem_limit_bytes=48 * 1024 * 1024
         ),
-    )(rows, w_all, wqk_t)
+    )(rows, w_all, w_query, w_key)
 
 
 def attend(query_rows, key_rows, value_rows, gain_mine, my_slab):
@@ -661,10 +666,7 @@
     chunk = rows.shape[0]
     pf = per_group * FEAT
     d_model = w_query.shape[0]
-    w_qk = jnp.concatenate(
-        [w_query.reshape(d_model, groups, pf), w_key.reshape(d_model, groups, pf)], axis=2
-    )
-    qk_got, value_got = middle(rows, value_all, w_qk.transpose(1, 2, 0), 2)
+    qk_got, value_got = middle(rows, value_all, w_query, w_key, 2)
     tok_rows = groups * chunk
     qk_rows = qk_got.transpose(0, 2, 1).reshape(tok_rows, 2 * pf)
     query_rows = qk_rows[:, :pf].reshape(tok_rows, per_group, FEAT)

time: 220 us -> 213 us (0.968)
  local copies, waits for them, and re-layouts: 9.16 us -> 5.4 us
    unnamed x3 -> x5, local copies, waits for them, and re-layouts: 4.69 us -> 0.93 us
where the time goes in v15:
time: 213 us; the launch traced here: 212 us
  Pallas kernels  187 us (88%)
  matrix products  15.6 us (7%)
  local copies, waits for them, and re-layouts  5.4 us (3%)
  other arithmetic  4.3 us (2%)
    pallas_call x1, Pallas kernels, opening(): pl.pallas_call(opening_kernel, out_shape=(jax.ShapeDtypeStruct(x.shape, x...  76.3 us
    pallas_call x1, Pallas kernels, closing(): pl.pallas_call(closing_kernel, out_shape=jax.ShapeDtypeStruct(block, hidd...  54.4 us
    pallas_call x1, Pallas kernels, middle(): pl.pallas_call(middle_kernel, out_shape=(jax.ShapeDtypeStruct(qk_shape, r...  38.3 us
    pallas_call x1, Pallas kernels, scan_seq(): pl.pallas_call(functools.partial(scan_kernel, width), out_shape=jax.Shape...  17.9 us
    dot_general x1, matrix products, attend(): jnp.einsum('bhts,bshe->bthe', weights, value_blocks, preferred_element_ty...  7.9 us

profile of v15, /device:TPU:1, one launch (start us, length us, event | category | flops | bytes accessed | tf_op | source)
XLA Modules:
  0.0 212.5 jit_solution(13360369791122354933)
XLA Ops:
  0.0 0.0 copy-start
  0.0 0.0 copy-start.1
  0.0 76.3 %shard_map.64 = (bf16[16,224,128]{2,1,0:T(8,128)(2,1)}, bf16[16,2048,128]{2,1,0:T(8,128)(2,1)}) custom-call(bf16[16,224,128]{2,1,0:T(8,128)(2,1)} %bitcast.83, bf16[2048,128]{1,0:T(8,128)(2,1)} %w_ref.2), custom_call_target="tpu_custom_call" | custom-call | tf_op jit(solution)/shard_map/pallas_call | solution.py:422
  76.3 1.3 copy_bitcast_fusion.rows_ref
  77.6 0.0 copy-done
  77.6 0.0 copy-done.1
  77.6 38.3 %shard_map.65 = (bf16[16,32,224]{2,1,0:T(8,128)(2,1)S(1)}, bf16[16,224,128]{2,1,0:T(8,128)(2,1)S(1)}) custom-call(bf16[224,2048]{1,0:T(8,128)(2,1)S(1)} %copy_bitcast_fusion.rows_ref, bf16[16,2048,128]{2,1,0:T(8,128)(2,1)} %get-tuple-element.10.w_ref, bf16[2048,256]{1,0:T(8,128)(2,1)S(1)} %copy-done, bf16[2048,256]{1,0:T(8,128)(2,1)S(1)} %copy-done.1), custom_call_target="tpu_custom_call" | custom-call | tf_op jit(solution)/shard_map/pallas_call | solution.py:596
  115.9 0.2 copy.27
  116.1 0.4 reshape.188
  116.5 0.5 convolution_bitcast_fusion.1
  117.0 0.4 multiply_multiply_fusion.1
  117.4 1.8 convolution_bitcast_fusion
  119.2 0.1 convert_reduce_fusion
  119.4 0.7 fusion.4.x_ref
  120.1 17.9 %shard_map.66 = f32[273,128]{1,0:T(8,128)} custom-call(bf16[273,128]{1,0:T(8,128)(2,1)} %fusion.4.x_ref), custom_call_target="tpu_custom_call" | custom-call | tf_op jit(solution)/shard_map/pallas_call | solution.py:258
  138.0 0.1 fusion.5
  138.1 1.0 pad_add_fusion
  139.0 1.6 fusion.6
  140.7 0.4 multiply_multiply_fusion
  141.1 3.8 %fusion.3 = f32[4,128,896]{2,1,0:T(8,128)} fusion(f32[4,896,256]{1,2,0:T(8,128)S(1)} %bitcast.75, f32[4,1,273,128]{3,2,0,1:T(8,128)S(1)} %pad_add_fusion), kind=kOutput, calls=%fused_computation.18 | convolution fusion | flops 1409286144 | bytes 6029312 | tf_op jit(solution)/shard_map/bthf,bhfe->bthe/dot_general | solution.py:642
  144.9 1.1 iota_compare_fusion
  146.0 7.9 %multiply_reduce_fusion = (f32[4,896]{1,0:T(4,128)S(1)}, f32[4,896,1,128]{1,3,0,2:T(8,128)}) fusion(f32[4,128,896]{2,1,0:T(8,128)} %fusion.3, f32[4,128,896]{2,1,0:T(8,128)S(1)} %fusion.6, f32[4,128]{1,0:T(4,128)S(1)} %bitcast.87, bf16[4,896,128]{2,1,0:T(8,128)(2,1)S(1)} %bitcast.71, pred[896,896]{1,0:T(8,128)(4,1)} %iota_compare_fusion, ...), kind=kOutput, calls=%fused_computation.10 | convolution fusion | flops 949613056 | bytes 7471104 | tf_op jit(solution)/shard_map/bhts,bshe->bthe/dot_general | solution.py:651
  153.9 1.8 copy.35
  155.7 0.1 rsqrt.12
  155.8 0.8 dynamic_slice.3
  156.6 0.5 multiply_convert_fusion.x_ref
  157.1 54.4 %shard_map.67 = bf16[16,224,128]{2,1,0:T(8,128)(2,1)S(1)} custom-call(bf16[16,224,128]{2,1,0:T(8,128)(2,1)S(1)} %multiply_convert_fusion.x_ref, bf16[2048,2048]{1,0:T(8,128)(2,1)} %w_ref.3), custom_call_target="tpu_custom_call" | custom-call | tf_op jit(solution)/shard_map/pallas_call | solution.py:515
  211.5 0.9 copy.66
  (7 shorter events, 0.1 us)
Async XLA Ops:
  0.0 77.6 %copy-start = (bf16[2048,256]{1,0:T(8,128)(2,1)S(1)}, bf16[2048,256]{1,0:T(8,128)(2,1)}, u32[]{:S(2)}) copy-start(bf16[2048,256]{1,0:T(8,128)(2,1)} %wq_ref.1) | copy-start | bytes 3145732
  0.0 77.6 %copy-start.1 = (bf16[2048,256]{1,0:T(8,128)(2,1)S(1)}, bf16[2048,256]{1,0:T(8,128)(2,1)}, u32[]{:S(2)}) copy-start(bf16[2048,256]{1,0:T(8,128)(2,1)} %wk_ref.1) | copy-start | bytes 3145732

commit v16 on v15

--- a/solution.py
+++ b/solution.py
@@ -9,7 +9,7 @@
 
 MESH = pl.DeviceIdType.MESH
 CHAN = ("z", "core")
-W_PIECES = 4
+W_PIECES = 8
 
 
 def chan_index():
@@ -414,7 +414,9 @@
         copy.wait_send()
     own.wait()
     w_local.wait()
-    y_ref[...] = buf[...]
+    width = buf.shape[2]
+    for g in range(n):
+        y_ref[:, g * width : (g + 1) * width] = buf[g]
 
 
 def opening(x, w, collective_id):
@@ -422,7 +424,7 @@
     return pl.pallas_call(
         opening_kernel,
         out_shape=(
-            jax.ShapeDtypeStruct(x.shape, x.dtype),
+            jax.ShapeDtypeStruct((x.shape[1], n * x.shape[2]), x.dtype),
             jax.ShapeDtypeStruct((n,) + w.shape, w.dtype),
         ),
         in_specs=[pl.BlockSpec(memory_space=pltpu.VMEM), pl.BlockSpec(memory_space=pl.ANY)],
@@ -661,8 +663,7 @@
     my_group = chan_index()
     my_slab = lax.axis_index("seq")
     tok_rows_total, tok_cols = tokens.shape
-    got, value_all = opening(tokens.reshape(groups, tok_rows_total // groups, tok_cols), w_value, 1)
-    rows = got.transpose(1, 0, 2).reshape(tok_rows_total // groups, groups * tok_cols)
+    rows, value_all = opening(tokens.reshape(groups, tok_rows_total // groups, tok_cols), w_value, 1)
     chunk = rows.shape[0]
     pf = per_group * FEAT
     d_model = w_query.shape[0]

time: 213 us -> 217 us (1.019)
  local copies, waits for them, and re-layouts: 5.4 us -> 7.74 us
    unnamed x5 -> x7, local copies, waits for them, and re-layouts: 0.93 us -> 4.55 us
    pallas_call x1, Pallas kernels: 76.3 us -> 78.6 us  [opening(): pl.pallas_call(opening_kernel, out_shape=(jax.ShapeDtypeStruct((x.shape[1...]
where the time goes in v16:
time: 217 us
  Pallas kernels  189 us (87%)
  matrix products  15.6 us (7%)
  local copies, waits for them, and re-layouts  7.74 us (4%)
  other arithmetic  4.3 us (2%)
    pallas_call x1, Pallas kernels, opening(): pl.pallas_call(opening_kernel, out_shape=(jax.ShapeDtypeStruct((x.shape[1...  78.6 us
    pallas_call x1, Pallas kernels, closing(): pl.pallas_call(closing_kernel, out_shape=jax.ShapeDtypeStruct(block, hidd...  54.4 us
    pallas_call x1, Pallas kernels, middle(): pl.pallas_call(middle_kernel, out_shape=(jax.ShapeDtypeStruct(qk_shape, r...  38.2 us
    pallas_call x1, Pallas kernels, scan_seq(): pl.pallas_call(functools.partial(scan_kernel, width), out_shape=jax.Shape...  17.9 us
    dot_general x1, matrix products, attend(): jnp.einsum('bhts,bshe->bthe', weights, value_blocks, preferred_element_ty...  7.9 us
    unnamed x7, local copies, waits for them, and re-layouts  4.55 us

profile of v16, /device:TPU:1, one launch (start us, length us, event | category | flops | bytes accessed | tf_op | source)
XLA Modules:
  0.0 217.0 jit_solution(770024083162339366)
XLA Ops:
  0.0 78.6 %shard_map.64 = (bf16[224,2048]{1,0:T(8,128)(2,1)}, bf16[16,2048,128]{2,1,0:T(8,128)(2,1)}) custom-call(bf16[16,224,128]{2,1,0:T(8,128)(2,1)} %bitcast.77, bf16[2048,128]{1,0:T(8,128)(2,1)} %w_ref.2), custom_call_target="tpu_custom_call" | custom-call | tf_op jit(solution)/shard_map/pallas_call | solution.py:424
  78.6 0.0 copy-start
  78.7 1.2 copy-done
  79.9 0.0 copy-start.1
  79.9 1.2 copy-done.1
  81.1 0.0 copy-start.2
  81.1 1.2 copy-done.2
  82.3 38.2 %shard_map.65 = (bf16[16,32,224]{2,1,0:T(8,128)(2,1)S(1)}, bf16[16,224,128]{2,1,0:T(8,128)(2,1)S(1)}) custom-call(bf16[224,2048]{1,0:T(8,128)(2,1)S(1)} %copy-done.2, bf16[16,2048,128]{2,1,0:T(8,128)(2,1)} %get-tuple-element.10.w_ref, bf16[2048,256]{1,0:T(8,128)(2,1)S(1)} %copy-done, bf16[2048,256]{1,0:T(8,128)(2,1)S(1)} %copy-done.1), custom_call_target="tpu_custom_call" | custom-call | tf_op jit(solution)/shard_map/pallas_call | solution.py:598
  120.5 0.2 copy.24
  120.7 0.4 reshape.184
  121.1 0.5 convolution_bitcast_fusion.1
  121.6 0.4 multiply_multiply_fusion.1
  122.0 1.8 convolution_bitcast_fusion
  123.8 0.1 convert_reduce_fusion
  123.9 0.7 fusion.4.x_ref
  124.6 17.9 %shard_map.66 = f32[273,128]{1,0:T(8,128)} custom-call(bf16[273,128]{1,0:T(8,128)(2,1)} %fusion.4.x_ref), custom_call_target="tpu_custom_call" | custom-call | tf_op jit(solution)/shard_map/pallas_call | solution.py:258
  142.6 0.1 fusion.5
  142.7 1.0 pad_add_fusion
  143.6 1.6 fusion.6
  145.3 0.4 multiply_multiply_fusion
  145.7 3.8 %fusion.3 = f32[4,128,896]{2,1,0:T(8,128)} fusion(f32[4,896,256]{1,2,0:T(8,128)S(1)} %bitcast.69, f32[4,1,273,128]{3,2,0,1:T(8,128)S(1)} %pad_add_fusion), kind=kOutput, calls=%fused_computation.17 | convolution fusion | flops 1409286144 | bytes 6029312 | tf_op jit(solution)/shard_map/bthf,bhfe->bthe/dot_general | solution.py:644
  149.4 1.1 iota_compare_fusion
  150.6 7.9 %multiply_reduce_fusion = (f32[4,896]{1,0:T(4,128)S(1)}, f32[4,896,1,128]{1,3,0,2:T(8,128)}) fusion(f32[4,128,896]{2,1,0:T(8,128)} %fusion.3, f32[4,128,896]{2,1,0:T(8,128)S(1)} %fusion.6, f32[4,128]{1,0:T(4,128)S(1)} %bitcast.81, bf16[4,896,128]{2,1,0:T(8,128)(2,1)S(1)} %bitcast.65, pred[896,896]{1,0:T(8,128)(4,1)} %iota_compare_fusion, ...), kind=kOutput, calls=%fused_computation.10 | convolution fusion | flops 949613056 | bytes 7471104 | tf_op jit(solution)/shard_map/bhts,bshe->bthe/dot_general | solution.py:653
  158.5 1.8 copy.32
  160.3 0.1 rsqrt.12
  160.4 0.8 dynamic_slice.3
  161.1 0.5 multiply_convert_fusion.x_ref
  161.7 54.4 %shard_map.67 = bf16[16,224,128]{2,1,0:T(8,128)(2,1)S(1)} custom-call(bf16[16,224,128]{2,1,0:T(8,128)(2,1)S(1)} %multiply_convert_fusion.x_ref, bf16[2048,2048]{1,0:T(8,128)(2,1)} %w_ref.3), custom_call_target="tpu_custom_call" | custom-call | tf_op jit(solution)/shard_map/pallas_call | solution.py:517
  216.1 0.9 copy.61
  (7 shorter events, 0.1 us)
Async XLA Ops:
  78.6 1.2 copy-start
  79.9 1.2 copy-start.1
  81.1 1.2 copy-start.2

commit v17 on v16

--- a/solution.py
+++ b/solution.py
@@ -9,7 +9,7 @@
 
 MESH = pl.DeviceIdType.MESH
 CHAN = ("z", "core")
-W_PIECES = 8
+W_PIECES = 4
 
 
 def chan_index():

time: 217 us -> 215 us (level)
    pallas_call x1, Pallas kernels: 78.6 us -> 76.3 us  [opening(): pl.pallas_call(opening_kernel, out_shape=(jax.ShapeDtypeStruct((x.shape[1...]
where the time goes in v17:
time: 215 us
  Pallas kernels  187 us (87%)
  matrix products  15.6 us (7%)
  local copies, waits for them, and re-layouts  7.74 us (4%)
  other arithmetic  4.3 us (2%)
    pallas_call x1, Pallas kernels, opening(): pl.pallas_call(opening_kernel, out_shape=(jax.ShapeDtypeStruct((x.shape[1...  76.3 us
    pallas_call x1, Pallas kernels, closing(): pl.pallas_call(closing_kernel, out_shape=jax.ShapeDtypeStruct(block, hidd...  54.5 us
    pallas_call x1, Pallas kernels, middle(): pl.pallas_call(middle_kernel, out_shape=(jax.ShapeDtypeStruct(qk_shape, r...  38.2 us
    pallas_call x1, Pallas kernels, scan_seq(): pl.pallas_call(functools.partial(scan_kernel, width), out_shape=jax.Shape...  17.9 us
    dot_general x1, matrix products, attend(): jnp.einsum('bhts,bshe->bthe', weights, value_blocks, preferred_element_ty...  7.9 us
    unnamed x7, local copies, waits for them, and re-layouts  4.55 us

profile of v17, /device:TPU:1, one launch (start us, length us, event | category | flops | bytes accessed | tf_op | source)
XLA Modules:
  0.0 214.7 jit_solution(5159839612827831720)
XLA Ops:
  0.0 76.3 %shard_map.64 = (bf16[224,2048]{1,0:T(8,128)(2,1)}, bf16[16,2048,128]{2,1,0:T(8,128)(2,1)}) custom-call(bf16[16,224,128]{2,1,0:T(8,128)(2,1)} %bitcast.77, bf16[2048,128]{1,0:T(8,128)(2,1)} %w_ref.2), custom_call_target="tpu_custom_call" | custom-call | tf_op jit(solution)/shard_map/pallas_call | solution.py:424
  76.3 0.0 copy-start
  76.3 1.2 copy-done
  77.6 0.0 copy-start.1
  77.6 1.2 copy-done.1
  78.8 0.0 copy-start.2
  78.8 1.2 copy-done.2
  80.0 38.2 %shard_map.65 = (bf16[16,32,224]{2,1,0:T(8,128)(2,1)S(1)}, bf16[16,224,128]{2,1,0:T(8,128)(2,1)S(1)}) custom-call(bf16[224,2048]{1,0:T(8,128)(2,1)S(1)} %copy-done.2, bf16[16,2048,128]{2,1,0:T(8,128)(2,1)} %get-tuple-element.10.w_ref, bf16[2048,256]{1,0:T(8,128)(2,1)S(1)} %copy-done, bf16[2048,256]{1,0:T(8,128)(2,1)S(1)} %copy-done.1), custom_call_target="tpu_custom_call" | custom-call | tf_op jit(solution)/shard_map/pallas_call | solution.py:598
  118.2 0.2 copy.24
  118.3 0.4 reshape.184
  118.7 0.5 convolution_bitcast_fusion.1
  119.3 0.4 multiply_multiply_fusion.1
  119.6 1.8 convolution_bitcast_fusion
  121.4 0.1 convert_reduce_fusion
  121.6 0.7 fusion.4.x_ref
  122.3 17.9 %shard_map.66 = f32[273,128]{1,0:T(8,128)} custom-call(bf16[273,128]{1,0:T(8,128)(2,1)} %fusion.4.x_ref), custom_call_target="tpu_custom_call" | custom-call | tf_op jit(solution)/shard_map/pallas_call | solution.py:258
  140.2 0.1 fusion.5
  140.3 1.0 pad_add_fusion
  141.3 1.6 fusion.6
  142.9 0.4 multiply_multiply_fusion
  143.3 3.8 %fusion.3 = f32[4,128,896]{2,1,0:T(8,128)} fusion(f32[4,896,256]{1,2,0:T(8,128)S(1)} %bitcast.69, f32[4,1,273,128]{3,2,0,1:T(8,128)S(1)} %pad_add_fusion), kind=kOutput, calls=%fused_computation.17 | convolution fusion | flops 1409286144 | bytes 6029312 | tf_op jit(solution)/shard_map/bthf,bhfe->bthe/dot_general | solution.py:644
  147.1 1.1 iota_compare_fusion
  148.2 7.9 %multiply_reduce_fusion = (f32[4,896]{1,0:T(4,128)S(1)}, f32[4,896,1,128]{1,3,0,2:T(8,128)}) fusion(f32[4,128,896]{2,1,0:T(8,128)} %fusion.3, f32[4,128,896]{2,1,0:T(8,128)S(1)} %fusion.6, f32[4,128]{1,0:T(4,128)S(1)} %bitcast.81, bf16[4,896,128]{2,1,0:T(8,128)(2,1)S(1)} %bitcast.65, pred[896,896]{1,0:T(8,128)(4,1)} %iota_compare_fusion, ...), kind=kOutput, calls=%fused_computation.10 | convolution fusion | flops 949613056 | bytes 7471104 | tf_op jit(solution)/shard_map/bhts,bshe->bthe/dot_general | solution.py:653
  156.1 1.8 copy.32
  157.9 0.1 rsqrt.12
  158.0 0.8 dynamic_slice.3
  158.8 0.5 multiply_convert_fusion.x_ref
  159.3 54.5 %shard_map.67 = bf16[16,224,128]{2,1,0:T(8,128)(2,1)S(1)} custom-call(bf16[16,224,128]{2,1,0:T(8,128)(2,1)S(1)} %multiply_convert_fusion.x_ref, bf16[2048,2048]{1,0:T(8,128)(2,1)} %w_ref.3), custom_call_target="tpu_custom_call" | custom-call | tf_op jit(solution)/shard_map/pallas_call | solution.py:517
  213.8 0.9 copy.61
  (7 shorter events, 0.1 us)
Async XLA Ops:
  76.3 1.2 copy-start
  77.6 1.2 copy-start.1
  78.8 1.2 copy-start.2

commit v18 on v15

--- a/solution.py
+++ b/solution.py
@@ -9,7 +9,7 @@
 
 MESH = pl.DeviceIdType.MESH
 CHAN = ("z", "core")
-W_PIECES = 4
+W_PIECES = 2
 
 
 def chan_index():

time: 213 us -> 214 us (level)
  no operation moved by 1% of the time
where the time goes in v18:
time: 214 us
  Pallas kernels  188 us (88%)
  matrix products  15.6 us (7%)
  local copies, waits for them, and re-layouts  5.4 us (3%)
  other arithmetic  4.3 us (2%)
    pallas_call x1, Pallas kernels, opening(): pl.pallas_call(opening_kernel, out_shape=(jax.ShapeDtypeStruct(x.shape, x...  77.1 us
    pallas_call x1, Pallas kernels, closing(): pl.pallas_call(closing_kernel, out_shape=jax.ShapeDtypeStruct(block, hidd...  55.1 us
    pallas_call x1, Pallas kernels, middle(): pl.pallas_call(middle_kernel, out_shape=(jax.ShapeDtypeStruct(qk_shape, r...  38 us
    pallas_call x1, Pallas kernels, scan_seq(): pl.pallas_call(functools.partial(scan_kernel, width), out_shape=jax.Shape...  17.9 us
    dot_general x1, matrix products, attend(): jnp.einsum('bhts,bshe->bthe', weights, value_blocks, preferred_element_ty...  7.9 us

profile of v18, /device:TPU:1, one launch (start us, length us, event | category | flops | bytes accessed | tf_op | source)
XLA Modules:
  0.0 213.7 jit_solution(8951689675821306224)
XLA Ops:
  0.0 0.0 copy-start
  0.0 0.0 copy-start.1
  0.0 77.1 %shard_map.64 = (bf16[16,224,128]{2,1,0:T(8,128)(2,1)}, bf16[16,2048,128]{2,1,0:T(8,128)(2,1)}) custom-call(bf16[16,224,128]{2,1,0:T(8,128)(2,1)} %bitcast.83, bf16[2048,128]{1,0:T(8,128)(2,1)} %w_ref.2), custom_call_target="tpu_custom_call" | custom-call | tf_op jit(solution)/shard_map/pallas_call | solution.py:422
  77.1 1.3 copy_bitcast_fusion.rows_ref
  78.4 0.0 copy-done
  78.4 0.0 copy-done.1
  78.4 38.0 %shard_map.65 = (bf16[16,32,224]{2,1,0:T(8,128)(2,1)S(1)}, bf16[16,224,128]{2,1,0:T(8,128)(2,1)S(1)}) custom-call(bf16[224,2048]{1,0:T(8,128)(2,1)S(1)} %copy_bitcast_fusion.rows_ref, bf16[16,2048,128]{2,1,0:T(8,128)(2,1)} %get-tuple-element.10.w_ref, bf16[2048,256]{1,0:T(8,128)(2,1)S(1)} %copy-done, bf16[2048,256]{1,0:T(8,128)(2,1)S(1)} %copy-done.1), custom_call_target="tpu_custom_call" | custom-call | tf_op jit(solution)/shard_map/pallas_call | solution.py:596
  116.4 0.2 copy.27
  116.6 0.4 reshape.188
  117.0 0.5 convolution_bitcast_fusion.1
  117.5 0.4 multiply_multiply_fusion.1
  117.9 1.8 convolution_bitcast_fusion
  119.7 0.1 convert_reduce_fusion
  119.9 0.7 fusion.4.x_ref
  120.5 17.9 %shard_map.66 = f32[273,128]{1,0:T(8,128)} custom-call(bf16[273,128]{1,0:T(8,128)(2,1)} %fusion.4.x_ref), custom_call_target="tpu_custom_call" | custom-call | tf_op jit(solution)/shard_map/pallas_call | solution.py:258
  138.5 0.1 fusion.5
  138.6 1.0 pad_add_fusion
  139.5 1.6 fusion.6
  141.2 0.4 multiply_multiply_fusion
  141.6 3.8 %fusion.3 = f32[4,128,896]{2,1,0:T(8,128)} fusion(f32[4,896,256]{1,2,0:T(8,128)S(1)} %bitcast.75, f32[4,1,273,128]{3,2,0,1:T(8,128)S(1)} %pad_add_fusion), kind=kOutput, calls=%fused_computation.18 | convolution fusion | flops 1409286144 | bytes 6029312 | tf_op jit(solution)/shard_map/bthf,bhfe->bthe/dot_general | solution.py:642
  145.3 1.1 iota_compare_fusion
  146.5 7.9 %multiply_reduce_fusion = (f32[4,896]{1,0:T(4,128)S(1)}, f32[4,896,1,128]{1,3,0,2:T(8,128)}) fusion(f32[4,128,896]{2,1,0:T(8,128)} %fusion.3, f32[4,128,896]{2,1,0:T(8,128)S(1)} %fusion.6, f32[4,128]{1,0:T(4,128)S(1)} %bitcast.87, bf16[4,896,128]{2,1,0:T(8,128)(2,1)S(1)} %bitcast.71, pred[896,896]{1,0:T(8,128)(4,1)} %iota_compare_fusion, ...), kind=kOutput, calls=%fused_computation.10 | convolution fusion | flops 949613056 | bytes 7471104 | tf_op jit(solution)/shard_map/bhts,bshe->bthe/dot_general | solution.py:651
  154.4 1.8 copy.35
  156.2 0.1 rsqrt.12
  156.3 0.8 dynamic_slice.3
  157.0 0.5 multiply_convert_fusion.x_ref
  157.6 55.1 %shard_map.67 = bf16[16,224,128]{2,1,0:T(8,128)(2,1)S(1)} custom-call(bf16[16,224,128]{2,1,0:T(8,128)(2,1)S(1)} %multiply_convert_fusion.x_ref, bf16[2048,2048]{1,0:T(8,128)(2,1)} %w_ref.3), custom_call_target="tpu_custom_call" | custom-call | tf_op jit(solution)/shard_map/pallas_call | solution.py:515
  212.7 0.9 copy.66
  (7 shorter events, 0.1 us)
Async XLA Ops:
  0.0 78.4 %copy-start = (bf16[2048,256]{1,0:T(8,128)(2,1)S(1)}, bf16[2048,256]{1,0:T(8,128)(2,1)}, u32[]{:S(2)}) copy-start(bf16[2048,256]{1,0:T(8,128)(2,1)} %wq_ref.1) | copy-start | bytes 3145732
  0.0 78.4 %copy-start.1 = (bf16[2048,256]{1,0:T(8,128)(2,1)S(1)}, bf16[2048,256]{1,0:T(8,128)(2,1)}, u32[]{:S(2)}) copy-start(bf16[2048,256]{1,0:T(8,128)(2,1)} %wk_ref.1) | copy-start | bytes 3145732

commit v19 on v15

--- a/solution.py
+++ b/solution.py
@@ -619,7 +619,7 @@
 
 
 def attend(query_rows, key_rows, value_rows, gain_mine, my_slab):
-    highest = lax.Precision.HIGHEST
+    highest = lax.Precision.HIGH
     tok_rows, per_group, _ = value_rows.shape
     blocks = tok_rows // BLOCK
     query_blocks = query_rows.reshape(blocks, BLOCK, per_group, FEAT)

time: 213 us -> 210 us (0.986)
  matrix products: 15.6 us -> 13.3 us
where the time goes in v19:
time: 210 us
  Pallas kernels  187 us (89%)
  matrix products  13.3 us (6%)
  local copies, waits for them, and re-layouts  5.4 us (3%)
  other arithmetic  4.3 us (2%)
    pallas_call x1, Pallas kernels, opening(): pl.pallas_call(opening_kernel, out_shape=(jax.ShapeDtypeStruct(x.shape, x...  76.3 us
    pallas_call x1, Pallas kernels, closing(): pl.pallas_call(closing_kernel, out_shape=jax.ShapeDtypeStruct(block, hidd...  54.2 us
    pallas_call x1, Pallas kernels, middle(): pl.pallas_call(middle_kernel, out_shape=(jax.ShapeDtypeStruct(qk_shape, r...  38.3 us
    pallas_call x1, Pallas kernels, scan_seq(): pl.pallas_call(functools.partial(scan_kernel, width), out_shape=jax.Shape...  17.9 us
    dot_general x1, matrix products, attend(): jnp.einsum('bhts,bshe->bthe', weights, value_blocks, preferred_element_ty...  8.15 us

profile of v19, /device:TPU:1, one launch (start us, length us, event | category | flops | bytes accessed | tf_op | source)
XLA Modules:
  0.0 209.9 jit_solution(2298799959685252257)
XLA Ops:
  0.0 0.0 copy-start
  0.0 0.0 copy-start.1
  0.0 76.3 %shard_map.64 = (bf16[16,224,128]{2,1,0:T(8,128)(2,1)}, bf16[16,2048,128]{2,1,0:T(8,128)(2,1)}) custom-call(bf16[16,224,128]{2,1,0:T(8,128)(2,1)} %bitcast.83, bf16[2048,128]{1,0:T(8,128)(2,1)} %w_ref.2), custom_call_target="tpu_custom_call" | custom-call | tf_op jit(solution)/shard_map/pallas_call | solution.py:422
  76.3 1.3 copy_bitcast_fusion.rows_ref
  77.6 0.0 copy-done
  77.6 0.0 copy-done.1
  77.6 38.3 %shard_map.65 = (bf16[16,32,224]{2,1,0:T(8,128)(2,1)S(1)}, bf16[16,224,128]{2,1,0:T(8,128)(2,1)S(1)}) custom-call(bf16[224,2048]{1,0:T(8,128)(2,1)S(1)} %copy_bitcast_fusion.rows_ref, bf16[16,2048,128]{2,1,0:T(8,128)(2,1)} %get-tuple-element.10.w_ref, bf16[2048,256]{1,0:T(8,128)(2,1)S(1)} %copy-done, bf16[2048,256]{1,0:T(8,128)(2,1)S(1)} %copy-done.1), custom_call_target="tpu_custom_call" | custom-call | tf_op jit(solution)/shard_map/pallas_call | solution.py:596
  115.9 0.2 copy.27
  116.1 0.4 reshape.188
  116.5 0.4 convolution_bitcast_fusion.1
  116.9 0.4 multiply_multiply_fusion.1
  117.3 1.1 convolution_bitcast_fusion
  118.4 0.1 convert_reduce_fusion
  118.6 0.7 fusion.4.x_ref
  119.3 17.9 %shard_map.66 = f32[273,128]{1,0:T(8,128)} custom-call(bf16[273,128]{1,0:T(8,128)(2,1)} %fusion.4.x_ref), custom_call_target="tpu_custom_call" | custom-call | tf_op jit(solution)/shard_map/pallas_call | solution.py:258
  137.2 0.1 fusion.5
  137.3 1.0 pad_add_fusion
  138.3 0.9 fusion.6
  139.2 0.4 multiply_multiply_fusion
  139.6 2.7 %fusion.3 = f32[4,128,896]{2,1,0:T(8,128)} fusion(f32[4,896,256]{1,2,0:T(8,128)S(1)} %bitcast.75, f32[4,1,273,128]{3,2,0,1:T(8,128)S(1)} %pad_add_fusion), kind=kOutput, calls=%fused_computation.18 | convolution fusion | flops 704643072 | bytes 6029312 | tf_op jit(solution)/shard_map/bthf,bhfe->bthe/dot_general | solution.py:642
  142.3 1.1 iota_compare_fusion
  143.4 8.1 %multiply_reduce_fusion = (f32[4,896]{1,0:T(4,128)S(1)}, f32[4,896,1,128]{1,3,0,2:T(8,128)}) fusion(f32[4,128,896]{2,1,0:T(8,128)} %fusion.3, f32[4,128,896]{2,1,0:T(8,128)S(1)} %fusion.6, f32[4,128]{1,0:T(4,128)S(1)} %bitcast.87, bf16[4,896,128]{2,1,0:T(8,128)(2,1)S(1)} %bitcast.71, pred[896,896]{1,0:T(8,128)(4,1)} %iota_compare_fusion, ...), kind=kOutput, calls=%fused_computation.10 | convolution fusion | flops 949613056 | bytes 7471104 | tf_op jit(solution)/shard_map/bhts,bshe->bthe/dot_general | solution.py:651
  151.5 1.8 copy.35
  153.4 0.1 rsqrt.12
  153.4 0.8 dynamic_slice.3
  154.2 0.5 multiply_convert_fusion.x_ref
  154.7 54.2 %shard_map.67 = bf16[16,224,128]{2,1,0:T(8,128)(2,1)S(1)} custom-call(bf16[16,224,128]{2,1,0:T(8,128)(2,1)S(1)} %multiply_convert_fusion.x_ref, bf16[2048,2048]{1,0:T(8,128)(2,1)} %w_ref.3), custom_call_target="tpu_custom_call" | custom-call | tf_op jit(solution)/shard_map/pallas_call | solution.py:515
  209.0 0.9 copy.66
  (7 shorter events, 0.1 us)
Async XLA Ops:
  0.0 77.6 %copy-start = (bf16[2048,256]{1,0:T(8,128)(2,1)S(1)}, bf16[2048,256]{1,0:T(8,128)(2,1)}, u32[]{:S(2)}) copy-start(bf16[2048,256]{1,0:T(8,128)(2,1)} %wq_ref.1) | copy-start | bytes 3145732
  0.0 77.6 %copy-start.1 = (bf16[2048,256]{1,0:T(8,128)(2,1)S(1)}, bf16[2048,256]{1,0:T(8,128)(2,1)}, u32[]{:S(2)}) copy-start(bf16[2048,256]{1,0:T(8,128)(2,1)} %wk_ref.1) | copy-start | bytes 3145732

commit v20 on v19

--- a/solution.py
+++ b/solution.py
@@ -619,7 +619,7 @@
 
 
 def attend(query_rows, key_rows, value_rows, gain_mine, my_slab):
-    highest = lax.Precision.HIGH
+    highest = lax.Precision.DEFAULT
     tok_rows, per_group, _ = value_rows.shape
     blocks = tok_rows // BLOCK
     query_blocks = query_rows.reshape(blocks, BLOCK, per_group, FEAT)

time: 210 us -> 208 us (level)
  matrix products: 13.3 us -> 11.2 us
where the time goes in v20:
time: 208 us
  Pallas kernels  187 us (90%)
  matrix products  11.2 us (5%)
  local copies, waits for them, and re-layouts  6.2 us (3%)
  other arithmetic  3.57 us (2%)
    pallas_call x1, Pallas kernels, opening(): pl.pallas_call(opening_kernel, out_shape=(jax.ShapeDtypeStruct(x.shape, x...  76.3 us
    pallas_call x1, Pallas kernels, closing(): pl.pallas_call(closing_kernel, out_shape=jax.ShapeDtypeStruct(block, hidd...  54.2 us
    pallas_call x1, Pallas kernels, middle(): pl.pallas_call(middle_kernel, out_shape=(jax.ShapeDtypeStruct(qk_shape, r...  38.3 us
    pallas_call x1, Pallas kernels, scan_seq(): pl.pallas_call(functools.partial(scan_kernel, width), out_shape=jax.Shape...  17.9 us
    dot_general x1, matrix products, attend(): jnp.einsum('bhts,bshe->bthe', weights, value_blocks, preferred_element_ty...  8.12 us

profile of v20, /device:TPU:1, one launch (start us, length us, event | category | flops | bytes accessed | tf_op | source)
XLA Modules:
  0.0 207.9 jit_solution(13063210005819537216)
XLA Ops:
  0.0 0.0 copy-start
  0.0 0.0 copy-start.1
  0.0 76.3 %shard_map.64 = (bf16[16,224,128]{2,1,0:T(8,128)(2,1)}, bf16[16,2048,128]{2,1,0:T(8,128)(2,1)}) custom-call(bf16[16,224,128]{2,1,0:T(8,128)(2,1)} %bitcast.83, bf16[2048,128]{1,0:T(8,128)(2,1)} %w_ref.2), custom_call_target="tpu_custom_call" | custom-call | tf_op jit(solution)/shard_map/pallas_call | solution.py:422
  76.3 1.3 copy_bitcast_fusion.rows_ref
  77.6 0.0 copy-done
  77.6 0.0 copy-done.1
  77.6 38.3 %shard_map.65 = (bf16[16,32,224]{2,1,0:T(8,128)(2,1)S(1)}, bf16[16,224,128]{2,1,0:T(8,128)(2,1)S(1)}) custom-call(bf16[224,2048]{1,0:T(8,128)(2,1)S(1)} %copy_bitcast_fusion.rows_ref, bf16[16,2048,128]{2,1,0:T(8,128)(2,1)} %get-tuple-element.10.w_ref, bf16[2048,256]{1,0:T(8,128)(2,1)S(1)} %copy-done, bf16[2048,256]{1,0:T(8,128)(2,1)S(1)} %copy-done.1), custom_call_target="tpu_custom_call" | custom-call | tf_op jit(solution)/shard_map/pallas_call | solution.py:596
  115.9 0.2 copy.27
  116.1 0.4 reshape.188
  116.5 0.2 convolution_bitcast_fusion.1
  116.8 0.5 multiply_multiply_fusion.1
  117.2 0.7 convolution_bitcast_fusion
  117.9 0.1 convert_reduce_fusion
  118.0 0.7 fusion.4.x_ref
  118.7 17.9 %shard_map.66 = f32[273,128]{1,0:T(8,128)} custom-call(bf16[273,128]{1,0:T(8,128)(2,1)} %fusion.4.x_ref), custom_call_target="tpu_custom_call" | custom-call | tf_op jit(solution)/shard_map/pallas_call | solution.py:258
  136.7 0.0 copy-start.2
  136.7 0.1 fusion.5
  136.8 0.8 copy-done.2
  137.6 0.4 fusion.6
  138.1 0.5 multiply_multiply_fusion
  138.5 1.7 fusion.3
  140.3 1.1 iota_compare_fusion
  141.4 8.1 %multiply_reduce_fusion = (f32[4,896]{1,0:T(4,128)S(1)}, f32[4,896,1,128]{1,3,0,2:T(8,128)}) fusion(f32[4,128,896]{2,1,0:T(8,128)} %fusion.3, f32[4,128,896]{2,1,0:T(8,128)S(1)} %fusion.6, f32[4,128]{1,0:T(4,128)S(1)} %bitcast.87, bf16[4,896,128]{2,1,0:T(8,128)(2,1)S(1)} %bitcast.71, pred[896,896]{1,0:T(8,128)(4,1)} %iota_compare_fusion, ...), kind=kOutput, calls=%fused_computation.10 | convolution fusion | flops 949613056 | bytes 7471104 | tf_op jit(solution)/shard_map/bhts,bshe->bthe/dot_general | solution.py:651
  149.5 1.8 copy.35
  151.4 0.1 rsqrt.12
  151.4 0.8 dynamic_slice.3
  152.2 0.5 multiply_convert_fusion.x_ref
  152.8 54.2 %shard_map.67 = bf16[16,224,128]{2,1,0:T(8,128)(2,1)S(1)} custom-call(bf16[16,224,128]{2,1,0:T(8,128)(2,1)S(1)} %multiply_convert_fusion.x_ref, bf16[2048,2048]{1,0:T(8,128)(2,1)} %w_ref.3), custom_call_target="tpu_custom_call" | custom-call | tf_op jit(solution)/shard_map/pallas_call | solution.py:515
  206.9 0.9 copy.66
  (8 shorter events, 0.2 us)
Async XLA Ops:
  0.0 77.6 %copy-start = (bf16[2048,256]{1,0:T(8,128)(2,1)S(1)}, bf16[2048,256]{1,0:T(8,128)(2,1)}, u32[]{:S(2)}) copy-start(bf16[2048,256]{1,0:T(8,128)(2,1)} %wq_ref.1) | copy-start | bytes 3145732
  0.0 77.6 %copy-start.1 = (bf16[2048,256]{1,0:T(8,128)(2,1)S(1)}, bf16[2048,256]{1,0:T(8,128)(2,1)}, u32[]{:S(2)}) copy-start(bf16[2048,256]{1,0:T(8,128)(2,1)} %wk_ref.1) | copy-start | bytes 3145732
  136.7 0.9 copy-start.2

commit v21 on v20

--- a/solution.py
+++ b/solution.py
@@ -630,17 +630,18 @@
     own_zero = jnp.sum(value_f32, axis=1)[:, :, None, :]
     own_one = jnp.einsum("bthf,bthe->bhfe", key_linear, value_f32, precision=highest)
     own_two = jnp.einsum("bthf,bthe->bhfe", key_square, value_f32, precision=highest)
-    own = jnp.concatenate([own_zero, own_one, own_two], axis=2)
+    own = jnp.concatenate([own_two, own_one, own_zero], axis=2)
     slab_total = jnp.sum(own, axis=0)
     state_rows = slab_total.shape[0] * slab_total.shape[1]
     prefix = scan_seq(slab_total.astype(jnp.bfloat16).reshape(state_rows, HEAD_DIM), 7).reshape(slab_total.shape)
     earlier = jnp.concatenate([jnp.zeros_like(own[:1]), jnp.cumsum(own, axis=0)[:-1]], axis=0) + prefix[None]
     query_linear, query_square = feature_parts(query_blocks.astype(jnp.float32))
-    inter = earlier[:, :, 0][:, None] + jnp.einsum(
-        "bthf,bhfe->bthe", query_linear, earlier[:, :, 1 : 1 + FEAT], precision=highest
+    square_rows = FEAT * FEAT
+    inter = earlier[:, :, square_rows + FEAT][:, None] + jnp.einsum(
+        "bthf,bhfe->bthe", query_linear, earlier[:, :, square_rows : square_rows + FEAT], precision=highest
     )
     inter = inter + jnp.einsum(
-        "bthf,bhfe->bthe", query_square, earlier[:, :, 1 + FEAT :], precision=highest
+        "bthf,bhfe->bthe", query_square, earlier[:, :, :square_rows], precision=highest
     )
     scores = jnp.einsum(
         "bthf,bshf->bhts", query_blocks, key_blocks, preferred_element_type=jnp.float32

time: 208 us -> 208 us (level)
  no operation moved by 1% of the time
where the time goes in v21:
time: 208 us
  Pallas kernels  187 us (90%)
  matrix products  11.2 us (5%)
  local copies, waits for them, and re-layouts  6.21 us (3%)
  other arithmetic  3.52 us (2%)
    pallas_call x1, Pallas kernels, opening(): pl.pallas_call(opening_kernel, out_shape=(jax.ShapeDtypeStruct(x.shape, x...  76.3 us
    pallas_call x1, Pallas kernels, closing(): pl.pallas_call(closing_kernel, out_shape=jax.ShapeDtypeStruct(block, hidd...  54.2 us
    pallas_call x1, Pallas kernels, middle(): pl.pallas_call(middle_kernel, out_shape=(jax.ShapeDtypeStruct(qk_shape, r...  38.3 us
    pallas_call x1, Pallas kernels, scan_seq(): pl.pallas_call(functools.partial(scan_kernel, width), out_shape=jax.Shape...  17.9 us
    dot_general x1, matrix products, attend(): jnp.einsum('bhts,bshe->bthe', weights, value_blocks, preferred_element_ty...  8.11 us

profile of v21, /device:TPU:1, one launch (start us, length us, event | category | flops | bytes accessed | tf_op | source)
XLA Modules:
  0.0 207.8 jit_solution(17108571683662654109)
XLA Ops:
  0.0 0.0 copy-start
  0.0 0.0 copy-start.1
  0.0 76.3 %shard_map.64 = (bf16[16,224,128]{2,1,0:T(8,128)(2,1)}, bf16[16,2048,128]{2,1,0:T(8,128)(2,1)}) custom-call(bf16[16,224,128]{2,1,0:T(8,128)(2,1)} %bitcast.83, bf16[2048,128]{1,0:T(8,128)(2,1)} %w_ref.2), custom_call_target="tpu_custom_call" | custom-call | tf_op jit(solution)/shard_map/pallas_call | solution.py:422
  76.3 1.3 copy_bitcast_fusion.rows_ref
  77.6 0.0 copy-done
  77.6 0.0 copy-done.1
  77.6 38.3 %shard_map.65 = (bf16[16,32,224]{2,1,0:T(8,128)(2,1)S(1)}, bf16[16,224,128]{2,1,0:T(8,128)(2,1)S(1)}) custom-call(bf16[224,2048]{1,0:T(8,128)(2,1)S(1)} %copy_bitcast_fusion.rows_ref, bf16[16,2048,128]{2,1,0:T(8,128)(2,1)} %get-tuple-element.10.w_ref, bf16[2048,256]{1,0:T(8,128)(2,1)S(1)} %copy-done, bf16[2048,256]{1,0:T(8,128)(2,1)S(1)} %copy-done.1), custom_call_target="tpu_custom_call" | custom-call | tf_op jit(solution)/shard_map/pallas_call | solution.py:596
  115.9 0.2 copy.27
  116.1 0.4 reshape.188
  116.5 0.5 multiply_multiply_fusion.1
  117.0 0.7 convolution_bitcast_fusion
  117.6 0.2 convolution_bitcast_fusion.1
  117.9 0.1 convert_reduce_fusion
  118.0 0.7 fusion.4.x_ref
  118.7 17.9 %shard_map.66 = f32[273,128]{1,0:T(8,128)} custom-call(bf16[273,128]{1,0:T(8,128)(2,1)} %fusion.4.x_ref), custom_call_target="tpu_custom_call" | custom-call | tf_op jit(solution)/shard_map/pallas_call | solution.py:258
  136.6 0.0 copy-start.2
  136.7 0.8 copy-done.2
  137.6 0.4 fusion.6
  138.0 0.5 multiply_multiply_fusion
  138.5 1.7 fusion.3
  140.3 1.1 iota_compare_fusion
  141.4 8.1 %multiply_reduce_fusion = (f32[4,896]{1,0:T(4,128)S(1)}, f32[4,896,1,128]{1,3,0,2:T(8,128)}) fusion(f32[4,128,896]{2,1,0:T(8,128)} %fusion.3, f32[4,128,896]{2,1,0:T(8,128)S(1)} %fusion.6, f32[4,128]{1,0:T(4,128)S(1)} %bitcast.87, bf16[4,896,128]{2,1,0:T(8,128)(2,1)S(1)} %bitcast.71, pred[896,896]{1,0:T(8,128)(4,1)} %iota_compare_fusion, ...), kind=kOutput, calls=%fused_computation.10 | convolution fusion | flops 949613056 | bytes 7471104 | tf_op jit(solution)/shard_map/bhts,bshe->bthe/dot_general | solution.py:652
  149.5 1.8 copy.35
  151.3 0.1 rsqrt.12
  151.4 0.8 dynamic_slice.3
  152.2 0.5 multiply_convert_fusion.x_ref
  152.7 54.2 %shard_map.67 = bf16[16,224,128]{2,1,0:T(8,128)(2,1)S(1)} custom-call(bf16[16,224,128]{2,1,0:T(8,128)(2,1)S(1)} %multiply_convert_fusion.x_ref, bf16[2048,2048]{1,0:T(8,128)(2,1)} %w_ref.3), custom_call_target="tpu_custom_call" | custom-call | tf_op jit(solution)/shard_map/pallas_call | solution.py:515
  206.9 0.9 copy.66
  (9 shorter events, 0.2 us)
Async XLA Ops:
  0.0 77.6 %copy-start = (bf16[2048,256]{1,0:T(8,128)(2,1)S(1)}, bf16[2048,256]{1,0:T(8,128)(2,1)}, u32[]{:S(2)}) copy-start(bf16[2048,256]{1,0:T(8,128)(2,1)} %wq_ref.1) | copy-start | bytes 3145732
  0.0 77.6 %copy-start.1 = (bf16[2048,256]{1,0:T(8,128)(2,1)S(1)}, bf16[2048,256]{1,0:T(8,128)(2,1)}, u32[]{:S(2)}) copy-start(bf16[2048,256]{1,0:T(8,128)(2,1)} %wk_ref.1) | copy-start | bytes 3145732
  136.6 0.9 copy-start.2
